TPU v7x, 32 devices: a whole 2x2x4 slice. The times are simulated.
32 devices in a mesh: groups: 2 (over x), radius: 16 (over z, y, core).
Axes of the slice: x: 2, y: 2, z: 4, core: 2. Of those that a mesh axis runs over, the one named last changes fastest.
Arguments:
- states: float32 [8, 400, 2048], P('groups', None, 'radius'), parts along dimension 0, may hold values from -6 to 6
- dipole: float32 [400, 400], replicated, may hold values from -0.625 to 0.625
- pattern: int32 [25, 25], replicated, may hold values 0 or 1
- angular: int32 [400], replicated, may hold values from 0 to 11
- thresholds: float32 [400], replicated, may hold values from 0 to 2
- surface_profile: float32 [2, 2048], P(None, 'radius'), may hold values from 0.2 to 1.5
- pulse_field: float32 [4], P('groups'), parts along dimension 0, may hold values from -0.05 to 0.05
Outputs:
- final_states: float32 [8, 400, 2048], P('groups', None, 'radius'), parts along dimension 0
- gradient: float32 [4], P('groups'), parts along dimension 0
There are 2 independent parts, one for each index of `groups`. A program takes and returns all parts, laid end to end along the dimension named above; an argument that names none is the same for every part. Nothing has to cross between parts.
All inputs are finite; a program needn't handle non-finite values.
Results may differ from a plain program's by a relative error of at most 0.00019.
Values sent between devices are 32-bit elements; how exact they have to be, the bound alone decides.
No kernel may reach another device: no remote copies, remote signals or barrier semaphores. Data moves between devices by JAX's collectives and lax.ppermute only.
A program may use at most 64 MiB of HBM per device.

v0:
```python
import math

import jax
import jax.numpy as jnp
from jax import lax
from jax.sharding import PartitionSpec as P

STEPS = 2
ORDER = 4


inner_radius = 20.0
spacing = 0.08
time_step = 0.005


def spread(value, axis, root):
    mine = lax.axis_index(axis) == root
    return lax.psum(jnp.where(mine, value, jnp.zeros_like(value)), axis)


def padded(cells, sides, width):
    for axis, dim in sides:
        count = lax.axis_size(axis)
        ends = count - 1
        head = lax.slice_in_dim(cells, 0, width, axis=dim)
        tail = lax.slice_in_dim(cells, cells.shape[dim] - width, cells.shape[dim], axis=dim)
        cells = jnp.concatenate(
            [
                lax.ppermute(tail, axis, [(i, (i + 1) % count) for i in range(ends)]),
                cells,
                lax.ppermute(head, axis, [((i + 1) % count, i) for i in range(ends)]),
            ],
            axis=dim,
        )
    return cells


def coupling_matrix(dipole, pattern, angular):
    channels = dipole.shape[0]
    blocks = pattern.shape[0]
    block_size = channels // blocks
    joined = jnp.maximum(pattern, pattern.T)
    block_owner = jnp.arange(channels, dtype=jnp.int32) // block_size
    block_pick = (block_owner[:, None] == jnp.arange(blocks, dtype=jnp.int32)[None, :]).astype(
        jnp.int32
    )
    block_mask = jnp.dot(jnp.dot(block_pick, joined), block_pick.T)
    selection = jnp.abs(angular[:, None] - angular[None, :]) == 1
    allowed = (block_mask > 0) & selection
    return jnp.where(allowed, 0.5 * (dipole + dipole.T), jnp.zeros_like(dipole))


def surface_pair(points):
    value_row = (
        4.0 * points[:, :, 0] - 6.0 * points[:, :, 1] + 4.0 * points[:, :, 2] - points[:, :, 3]
    )
    slope_row = (
        -13.0 / 3.0 * points[:, :, 0]
        + 9.5 * points[:, :, 1]
        - 7.0 * points[:, :, 2]
        + 11.0 / 6.0 * points[:, :, 3]
    )
    return jnp.stack([value_row, slope_row])


def apply_hamiltonian(
    extended,
    positions,
    profile_rows,
    boundary,
    coupling,
    thresholds,
    centrifugal,
    strength,
    power,
    grid_points,
):
    center = extended[:, :, 2:-2]
    radial_values = inner_radius + (positions + 1).astype(jnp.float32) * spacing
    kinetic = (
        -0.5
        / (spacing * spacing)
        * (
            -1.0 / 12.0 * (extended[:, :, :-4] + extended[:, :, 4:])
            + 4.0 / 3.0 * (extended[:, :, 1:-3] + extended[:, :, 3:-1])
            - 2.5 * center
        )
    )
    potential = (
        thresholds[:, None] + centrifugal[:, None] / (radial_values * radial_values)[None, :]
    ) * center
    mixed_rows = jnp.einsum("cd,kdr->kcr", coupling, center, precision=lax.Precision.HIGHEST)
    driven = (strength * radial_values)[None, None, :] * mixed_rows
    boundary_term = (
        boundary[0][:, :, None] * profile_rows[0][None, None, :]
        + boundary[1][:, :, None] * profile_rows[1][None, None, :]
    )
    hamiltonian = kinetic + potential + driven + boundary_term
    advanced = (
        time_step
        / power
        * jnp.stack([hamiltonian[1], -hamiltonian[0], hamiltonian[3], -hamiltonian[2]])
    )
    inside = (positions >= 0) & (positions < grid_points)
    return (jnp.where(inside[None, None, :], advanced, jnp.zeros_like(advanced)), mixed_rows)


def boundary_data(points):
    return spread(surface_pair(points), "radius", 0)


def per_device(states, dipole, pattern, angular, thresholds, surface_profile, pulse_field):
    local_rows = states.shape[2]
    devices = lax.axis_size("radius")
    grid_points = local_rows * devices
    first_point = lax.axis_index("radius") * local_rows
    coupling = coupling_matrix(dipole, pattern, angular)
    centrifugal = 0.5 * (angular * (angular + 1)).astype(jnp.float32)
    local_positions = first_point + jnp.arange(local_rows, dtype=jnp.int32)
    radial_values = inner_radius + (local_positions + 1).astype(jnp.float32) * spacing
    normalizer = math.sqrt(states.shape[1] * grid_points) * (inner_radius + grid_points * spacing)
    partials = []
    for step_index in range(STEPS):
        strength = pulse_field[step_index]
        summed = states
        taylor_term = states
        for power in range(1, ORDER + 1):
            boundary = boundary_data(taylor_term[:, :, :4])
            extended = padded(taylor_term, (("radius", 2),), 2)
            taylor_term, mixed_rows = apply_hamiltonian(
                extended,
                local_positions,
                surface_profile,
                boundary,
                coupling,
                thresholds,
                centrifugal,
                strength,
                power,
                grid_points,
            )
            if power == 1:
                mixed_state = mixed_rows
            summed = summed + taylor_term
        intersection = jnp.sum(
            radial_values[None, :] * (states[2] * mixed_state[1] - states[3] * mixed_state[0])
        )
        intersection = lax.psum(intersection, "radius")
        partials.append(intersection)
        states = summed
    gathered = jnp.stack(partials)
    return (states, gathered / normalizer)


def solution(mesh):
    return jax.shard_map(
        per_device,
        mesh=mesh,
        in_specs=(P("groups", None, "radius"), P(), P(), P(), P(), P(None, "radius"), P("groups")),
        out_specs=(P("groups", None, "radius"), P("groups")),
        check_vma=False,
    )
```

profile of v0, /device:TPU:0, one launch (start us, length us, event | category | flops | bytes accessed | tf_op | source)
XLA Modules:
  0.0 623.6 jit_solution(16780126876502364732)
XLA Ops:
  7.4 63.8 %psum.70 = f32[2,4,400]{2,1,0:T(4,128)S(1)} all-reduce(f32[2,4,400]{2,1,0:T(4,128)S(1)} %maximum_select_fusion), channel_id=1, replica_groups=mesh['groups'=2,'radius'=16] {'radius'}, use_global_device_ids=true, to_apply=%region_0.1 | all-reduce | flops 3200 | bytes 25600 | tf_op jit(solution)/shard_map/psum | solution.py:19
  92.6 2.7 fusion.123
  95.3 57.6 %psum.71 = f32[2,4,400]{2,1,0:T(4,128)S(1)} all-reduce(f32[2,4,400]{2,1,0:T(4,128)S(1)} %maximum_select_fusion.1), channel_id=1, replica_groups=mesh['groups'=2,'radius'=16] {'radius'}, use_global_device_ids=true, to_apply=%region_1.2 | all-reduce | flops 3200 | bytes 25600 | tf_op jit(solution)/shard_map/psum | solution.py:19
  158.5 3.6 fusion.73
  164.2 2.7 fusion.121
  166.9 58.7 %psum.72 = f32[2,4,400]{2,1,0:T(4,128)S(1)} all-reduce(f32[2,4,400]{2,1,0:T(4,128)S(1)} %maximum_select_fusion.2), channel_id=1, replica_groups=mesh['groups'=2,'radius'=16] {'radius'}, use_global_device_ids=true, to_apply=%region_2.3 | all-reduce | flops 3200 | bytes 25600 | tf_op jit(solution)/shard_map/psum | solution.py:19
  230.7 3.6 fusion.63
  236.4 2.7 fusion.119
  239.1 58.7 %psum.73 = f32[2,4,400]{2,1,0:T(4,128)S(1)} all-reduce(f32[2,4,400]{2,1,0:T(4,128)S(1)} %maximum_select_fusion.3), channel_id=1, replica_groups=mesh['groups'=2,'radius'=16] {'radius'}, use_global_device_ids=true, to_apply=%region_3.4 | all-reduce | flops 3200 | bytes 25600 | tf_op jit(solution)/shard_map/psum | solution.py:19
  303.1 3.6 fusion.53
  308.3 5.1 fusion.105
  318.7 2.9 fusion.126
  323.4 58.7 %psum.74 = f32[2,4,400]{2,1,0:T(4,128)S(1)} all-reduce(f32[2,4,400]{2,1,0:T(4,128)S(1)} %maximum_select_fusion.4), channel_id=1, replica_groups=mesh['groups'=2,'radius'=16] {'radius'}, use_global_device_ids=true, to_apply=%region_4.5 | all-reduce | flops 3200 | bytes 25600 | tf_op jit(solution)/shard_map/psum | solution.py:19
  386.7 3.6 fusion.43
  392.4 2.7 fusion.115
  395.1 58.7 %psum.75 = f32[2,4,400]{2,1,0:T(4,128)S(1)} all-reduce(f32[2,4,400]{2,1,0:T(4,128)S(1)} %maximum_select_fusion.5), channel_id=1, replica_groups=mesh['groups'=2,'radius'=16] {'radius'}, use_global_device_ids=true, to_apply=%region_5.6 | all-reduce | flops 3200 | bytes 25600 | tf_op jit(solution)/shard_map/psum | solution.py:19
  459.0 3.6 fusion.33
  464.6 2.7 fusion.113
  467.3 58.7 %psum.76 = f32[2,4,400]{2,1,0:T(4,128)S(1)} all-reduce(f32[2,4,400]{2,1,0:T(4,128)S(1)} %maximum_select_fusion.6), channel_id=1, replica_groups=mesh['groups'=2,'radius'=16] {'radius'}, use_global_device_ids=true, to_apply=%region_6.7 | all-reduce | flops 3200 | bytes 25600 | tf_op jit(solution)/shard_map/psum | solution.py:19
  531.4 3.6 fusion.23
  537.1 2.7 fusion.111
  539.8 58.7 %all-reduce = (f32[2,4,400]{2,1,0:T(4,128)S(1)}, f32[1]{0:T(128)}, f32[1]{0:T(128)}) all-reduce(f32[2,4,400]{2,1,0:T(4,128)S(1)} %maximum_select_fusion.7, f32[1]{0:T(128)} %bitcast.50, f32[1]{0:T(128)} %bitcast.48), channel_id=1, replica_groups=mesh['groups'=2,'radius'=16] {'radius'}, use_global_device_ids=true, to_apply=%region_7.8 | all-reduce | flops 3202 | bytes 25616 | tf_op jit(solution)/shard_map/psum | solution.py:19
  605.6 3.7 fusion.13
  610.9 10.9 %fusion.110 = f32[4,400,128]{1,0,2:T(4,128)S(1)} fusion(f32[1,400,128]{1,0,2:T(1,128)S(1)} %get-tuple-element.14, f32[1,400,128]{1,0,2:T(1,128)S(1)} %get-tuple-element.15, f32[1,400,128]{1,0,2:T(1,128)S(1)} %get-tuple-element.16, f32[1,400,128]{1,0,2:T(1,128)S(1)} %get-tuple-element.13, pred[128]{0:T(512)(128)(4,1)S(1)} %compare_and_fusion, ...), kind=kLoop, calls=%fused_computation.166 | loop fusion | flops 9830400 | bytes 8192128 | tf_op jit(solution)/shard_map/add | solution.py:145
  (249 shorter events, 87.1 us)
Async XLA Ops:
  0.6 70.6 %copy-start.66 = (f32[2]{0:T(128)S(1)}, f32[2]{0:T(128)}, u32[]{:S(2)}) copy-start(f32[2]{0:T(128)} %param.13) | copy-start | bytes 28
  0.6 72.3 %copy-start.62 = (s32[400]{0:T(512)S(1)}, s32[400]{0:T(512)}, u32[]{:S(2)}) copy-start(s32[400]{0:T(512)} %param.10) | copy-start | bytes 4804
  0.7 72.3 %copy-start.34 = (f32[400,400]{1,0:T(8,128)S(1)}, f32[400,400]{1,0:T(8,128)}, u32[]{:S(2)}) copy-start(f32[400,400]{1,0:T(8,128)} %param.8) | copy-start | bytes 1920004
  2.4 85.6 %collective-permute-start = (f32[4,400,2]{1,0,2:T(4,128)S(1)}, f32[4,400,2]{1,0,2:T(4,128)S(1)}, u32[]{:S(2)}, u32[]{:S(2)}) collective-permute-start(f32[4,400,2]{1,0,2:T(4,128)S(1)} %get-tuple-element.75), channel_id=1, source_target_pairs={{0,1},{1,2},{2,3},{3,4},{4,5},{5,6},{6,7},{7,8},{8,9},{9,10},{10,1... | collective-permute-start | bytes 38408 | tf_op jit(solution)/shard_map/ppermute | solution.py:30
  4.8 83.3 %collective-permute-start.1 = (f32[4,400,2]{1,0,2:T(4,128)S(1)}, f32[4,400,2]{1,0,2:T(4,128)S(1)}, u32[]{:S(2)}, u32[]{:S(2)}) collective-permute-start(f32[4,400,2]{1,0,2:T(4,128)S(1)} %get-tuple-element.76), channel_id=1, source_target_pairs={{1,0},{2,1},{3,2},{4,3},{5,4},{6,5},{7,6},{8,7},{9,8},{10,9},{11,1... | collective-permute-start | bytes 38408 | tf_op jit(solution)/shard_map/ppermute | solution.py:32
  6.8 67.3 %copy-start.61 = (s32[25,25]{1,0:T(8,128)S(1)}, s32[25,25]{1,0:T(8,128)}, u32[]{:S(2)}) copy-start(s32[25,25]{1,0:T(8,128)} %param.9) | copy-start | bytes 7504
  152.9 5.6 collective-permute-start.2
  154.2 4.3 collective-permute-start.3
  225.6 5.2 collective-permute-start.4
  226.9 3.9 collective-permute-start.5
  297.8 5.3 collective-permute-start.6
  299.1 4.0 collective-permute-start.7
  307.7 5.7 copy-start.35
  307.7 5.7 copy-start.37
  318.7 66.2 %copy-start.68 = (f32[128]{0:T(128)S(1)}, f32[128]{0:T(128)}, u32[]{:S(2)}) copy-start(f32[128]{0:T(128)} %multiply_add_fusion) | copy-start | bytes 1540
  318.7 67.9 %copy-start.63 = (f32[128]{0:T(128)S(1)}, f32[128]{0:T(128)}, u32[]{:S(2)}) copy-start(f32[128]{0:T(128)} %broadcast_multiply_fusion) | copy-start | bytes 1540
  382.1 4.6 collective-permute-start.8
  383.4 3.3 collective-permute-start.9
  453.8 5.2 collective-permute-start.10
  455.1 3.9 collective-permute-start.11
  526.0 5.4 collective-permute-start.12
  527.3 4.1 collective-permute-start.13
  598.5 7.0 %collective-permute-start.14 = (f32[4,400,2]{1,0,2:T(4,128)S(1)}, f32[4,400,2]{1,0,2:T(4,128)S(1)}, u32[]{:S(2)}, u32[]{:S(2)}) collective-permute-start(f32[4,400,2]{1,0,2:T(4,128)S(1)} %get-tuple-element.19), channel_id=1, source_target_pairs={{0,1},{1,2},{2,3},{3,4},{4,5},{5,6},{6,7},{7,8},{8,9},{9,10},{10,1... | collective-permute-start | bytes 38408 | tf_op jit(solution)/shard_map/ppermute | solution.py:30
  599.8 5.7 collective-permute-start.15
  (61 other events, 148.9 us)
where the time goes:
time: 633 us; the launch traced here: 624 us
  blocking collectives  474 us (75%)
  other arithmetic  68.8 us (11%)
  local copies, waits for them, and re-layouts  31.9 us (5%)
  matrix products  24 us (4%)
  starting transfers between devices  22.7 us (4%)
    psum x8, blocking collectives, spread(): return lax.psum(jnp.where(mine, value, jnp.zeros_like(value)), axis)  474 us
    add x8, other arithmetic, apply_hamiltonian(): hamiltonian = kinetic + potential + driven + boundary_term  27.6 us
    dot_general x8, matrix products, apply_hamiltonian(): jnp.einsum('cd,kdr->kcr', coupling, center, precision=lax.Precision.HIGHEST)  21.4 us
    dot_general x8, local copies, waits for them, and re-layouts, apply_hamiltonian(): jnp.einsum('cd,kdr->kcr', coupling, center, precision=lax.Precision.HIGHEST)  19.5 us
    add x2, other arithmetic, per_device(): summed = summed + taylor_term  16 us
  transfers between devices with their start and end apart: 16, of which 0 were waited for; matrix products, arithmetic and copies ran while one was open for 6% of the time, Pallas kernels for 0%

commit v1 on v0

v1 whole, which is shorter than its diff:
```python
import functools
import math

import jax
import jax.numpy as jnp
from jax import lax
from jax.experimental import pallas as pl
from jax.experimental.pallas import tpu as pltpu
from jax.sharding import PartitionSpec as P

STEPS = 2
ORDER = 4

inner_radius = 20.0
spacing = 0.08
time_step = 0.005

HALO = 2 * ORDER * STEPS
INNER = 24
KIN = 1.0 / (24.0 * spacing * spacing)
VALUE = (4.0, -6.0, 4.0, -1.0)
SLOPE = (-13.0 / 3.0, 9.5, -7.0, 11.0 / 6.0)

F32 = jnp.float32
BF16 = jnp.bfloat16

OWN = {"a": 0, "c": 128, "b": 512, "d": 640}
EXTRA = {"a": 256, "c": 256, "b": 384, "d": 384}
PARTS = ("a", "b", "c", "d")


def iota(shape, dim):
    return lax.broadcasted_iota(jnp.int32, shape, dim)


def pack_kernel(states_ref, profile_ref, right_ref, left_ref, inner_ref):
    channels = states_ref.shape[1]
    half = channels // 2
    local = states_ref.shape[2]

    def gather(rows_ref, rows, moves, lanes):
        out = None
        for part, source, target, width in moves:
            moved = rows_ref[part, rows, :]
            shift = (target - source) % local
            if shift:
                moved = pltpu.roll(moved, shift, 1)
            if out is None:
                out = moved
            else:
                inside = (lanes >= target) & (lanes < target + width)
                out = jnp.where(inside, moved, out)
        return out

    order = {0: 0, 2: 64, 1: 16, 3: 80}
    lanes = iota((half, local), 1)
    right = None
    for out_ref, source in ((right_ref, local - HALO), (left_ref, 0)):
        packed = None
        for h in range(2):
            moves = [(k, source, order[k] + 32 * h, HALO) for k in range(4)]
            got = gather(states_ref, pl.ds(half * h, half), moves, lanes)
            if packed is None:
                packed = got
            else:
                packed = jnp.where((lanes & 32) != 0, got, packed)
        out_ref[:half, :] = packed
        prof = profile_ref[...]
        shift = (-source) % local
        if shift:
            prof = pltpu.roll(prof, shift, 1)
        out_ref[half : half + 2, :] = prof
        out_ref[half + 2 :, :] = jnp.zeros((out_ref.shape[0] - half - 2, local), F32)

    lanes = iota((channels, local), 1)
    moves = []
    for k, first in ((0, 32), (2, 96), (1, 0), (3, 64)):
        moves.append((k, 0, first, INNER))
        moves.append((k, 0, first + INNER, 8))
    inner_ref[:channels, :] = gather(states_ref, pl.ds(0, channels), moves, lanes)
    prof = profile_ref[...]
    lanes2 = iota((2, local), 1)
    shifted = pltpu.roll(prof, 32, 1)
    inner_ref[channels : channels + 2, :] = jnp.where(
        (lanes2 & 63) >= 32 + INNER, pltpu.roll(prof, 32 + INNER, 1), shifted
    )
    inner_ref[channels + 2 :, :] = jnp.zeros((inner_ref.shape[0] - channels - 2, local), F32)


def lane_points(lanes, first, local):
    e = (lanes - local) & 63
    own = lanes < local
    point = jnp.where(
        own,
        first + lanes,
        jnp.where(
            e < 16,
            first - 16 + e,
            jnp.where(
                e < 32,
                first + local + e - 16,
                jnp.where(e < 32 + INNER, e - 32, e - 32 - INNER),
            ),
        ),
    )
    segment = jnp.where(own, 0, jnp.where(e < 32, 0, jnp.where(e < 32 + INNER, 1, 2)))
    return point, segment


def table_kernel(
    first_ref, dipole_ref, pattern_ref, angular_ref, thr_ref, coupling_ref, kinetic_ref, pot_ref, *, grid_points
):
    channels = dipole_ref.shape[0]
    blocks = pattern_ref.shape[0]
    size = channels // blocks
    local = 128
    first = first_ref[0]
    pattern = pattern_ref[...].astype(F32)
    joined = jnp.maximum(pattern, pattern.T).astype(BF16)
    tall = (iota((channels, blocks), 0) // size == iota((channels, blocks), 1)).astype(F32).astype(BF16)
    wide = (iota((blocks, channels), 1) // size == iota((blocks, channels), 0)).astype(F32).astype(BF16)
    rows = jnp.dot(tall, joined, preferred_element_type=F32).astype(BF16)
    mask = jnp.dot(rows, wide, preferred_element_type=F32)
    ang = jnp.broadcast_to(angular_ref[...].astype(F32), (channels, channels))
    angt = ang.T
    allowed = (mask > 0.5) & (jnp.abs(ang - angt) == 1.0)
    dip = dipole_ref[...]
    coupling = jnp.where(allowed, 0.5 * (dip + dip.T), 0.0)
    high = coupling.astype(BF16)
    low = (coupling - high.astype(F32)).astype(BF16)
    coupling_ref[...] = jnp.concatenate([high, high, low], axis=1)
    lanes = iota((8, 2 * local), 1)
    point, _ = lane_points(lanes, first, local)
    radii = inner_radius + (point + 1).astype(F32) * spacing
    inverse = (1.0 / (radii * radii))[:1]
    centrifugal = 0.5 * angt[:, :local] * (angt[:, :local] + 1.0)
    thr = jnp.broadcast_to(thr_ref[...], (local, channels)).T
    pot_ref[:, :local] = thr + centrifugal * inverse[:, :local]
    pot_ref[:, local:] = thr + centrifugal * inverse[:, local:]
    shape = (2 * local, 2 * local)
    src, dst = iota(shape, 0), iota(shape, 1)
    sp, ss = lane_points(src, first, local)
    dp, ds = lane_points(dst, first, local)
    gap = jnp.abs(sp - dp)
    coef = jnp.where(gap == 0, 30.0, jnp.where(gap == 1, -16.0, jnp.where(gap == 2, 1.0, 0.0)))
    same = (ss < 2) & (ss == jnp.minimum(ds, 1))
    valid = (dp >= 0) & (dp < grid_points) & ((dst < local) | (((dst - local) & 63) < 60))
    coef = jnp.where(same & valid, coef, 0.0)
    for which in range(2):
        mine = (src < local) | ((src - local) // 64 == which)
        mine = mine & ((dst < local) | ((dst - local) // 64 == which))
        kinetic_ref[which] = jnp.where(mine, coef, 0.0)


def split_store(stack_ref, at, value):
    channels = value.shape[0]
    width = value.shape[1]
    high = value.astype(BF16)
    low = (value - high.astype(F32)).astype(BF16)
    stack_ref[:channels, at : at + width] = high
    stack_ref[channels : 2 * channels, at : at + width] = low
    stack_ref[2 * channels :, at : at + width] = high


def lane_radii(first, local):
    lanes = iota((8, 2 * local), 1)
    point, _ = lane_points(lanes, first, local)
    return (inner_radius + (point + 1).astype(F32) * spacing)[:1]


def mix(coupling_ref, stack_ref, mixed_ref):
    for n in range(3):
        cut = slice(256 * n, 256 * n + 256)
        mixed_ref[:, cut] = jnp.dot(coupling_ref[...], stack_ref[:, cut], preferred_element_type=F32)


def stencil(stack_ref, matrix_ref, moved_ref):
    channels = stack_ref.shape[0] // 3
    for k, part in enumerate(PARTS):
        own, extra = OWN[part], EXTRA[part]
        weights = matrix_ref[0 if part in "ab" else 1]
        total = None
        for rows in (slice(0, channels), slice(channels, 2 * channels)):
            left = jnp.concatenate([stack_ref[rows, own : own + 128], stack_ref[rows, extra : extra + 128]], axis=1)
            got = jnp.dot(left, weights, preferred_element_type=F32)
            total = got if total is None else total + got
        moved_ref[k] = total


def advance(v_ref, total_ref, stack_ref, mixed_ref, moved_ref, pot_ref, drive, scale, chunk=80):
    channels = v_ref.shape[0]
    local = 128
    for c0 in range(0, channels, chunk):
        rows = slice(c0, c0 + chunk)
        pot_own, pot_extra = pot_ref[rows, :local], pot_ref[rows, local:]
        drive_own, drive_extra = drive[:, :local], drive[:, local:]

        def hamiltonian(at, moved, pot, force):
            cut = slice(at, at + local)
            return KIN * moved + pot * v_ref[rows, cut] + force * mixed_ref[rows, cut]

        new = {}
        for source, target, sign in ((1, "a", 1.0), (0, "b", -1.0), (3, "c", 1.0), (2, "d", -1.0)):
            part = PARTS[source]
            new[OWN[target]] = (sign * scale) * hamiltonian(
                OWN[part], moved_ref[source, rows, :local], pot_own, drive_own
            )
        for source, target, sign in (("b", "a", 1.0), ("a", "b", -1.0)):
            k = PARTS.index(source)
            moved = moved_ref[k, rows, local:] + moved_ref[k + 2, rows, local:]
            new[EXTRA[target]] = (sign * scale) * hamiltonian(EXTRA[source], moved, pot_extra, drive_extra)
        for at, value in new.items():
            cut = slice(at, at + local)
            v_ref[rows, cut] = value
            total_ref[rows, cut] = total_ref[rows, cut] + value
            high = value.astype(BF16)
            low = (value - high.astype(F32)).astype(BF16)
            stack_ref[c0 : c0 + chunk, cut] = high
            stack_ref[channels + c0 : channels + c0 + chunk, cut] = low
            stack_ref[2 * channels + c0 : 2 * channels + c0 + chunk, cut] = high


def intersect(state_ref, mixed_ref, radii):
    def at(ref, part):
        return ref[:, OWN[part] : OWN[part] + 128]

    both = at(state_ref, "c") * at(mixed_ref, "b") - at(state_ref, "d") * at(mixed_ref, "a")
    return jnp.sum(both * radii[:, :128], axis=0, keepdims=True)


def first_kernel(
    first_ref,
    field_ref,
    states_ref,
    left_ref,
    right_ref,
    inner_ref,
    profile_ref,
    coupling_ref,
    kinetic_ref,
    pot_ref,
    state_ref,
    mixed_ref,
    matrix_ref,
    part_ref,
    v_ref,
    stack_ref,
    moved_ref,
    work_ref,
):
    channels = states_ref.shape[1]
    half = channels // 2
    local = 128
    first = first_ref[0]
    for k, part in enumerate(PARTS):
        v_ref[:, OWN[part] : OWN[part] + local] = states_ref[k]
    lanes = iota((half, local), 1) & 63
    for pair, at in ((0, 256), (1, 384)):
        for h in range(2):
            rows = slice(half * h, half * h + half)
            back = 16 * pair + 32 * h
            lo = left_ref[:half, :]
            ro = right_ref[:half, :]
            if back:
                lo = pltpu.roll(lo, local - back, 1)
            if back != 16:
                ro = pltpu.roll(ro, (16 - back) % local, 1)
            io = inner_ref[rows, :]
            if pair:
                io = pltpu.roll(io, 32, 1)
            v_ref[rows, at : at + local] = jnp.where(lanes < 16, lo, jnp.where(lanes < 32, ro, io))
    state_ref[...] = v_ref[...]
    split_store(stack_ref, 0, v_ref[...])
    p_own = profile_ref[...]
    lanes2 = iota((2, local), 1)
    p_extra = jnp.where(
        lanes2 < 16,
        left_ref[half : half + 2, :],
        jnp.where(lanes2 < 32, pltpu.roll(right_ref[half : half + 2, :], 16, 1), inner_ref[channels : channels + 2, :]),
    )
    p_extra = jnp.where((lanes2 & 63) < 60, p_extra, 0.0)
    p_extra = jnp.where(lanes2 < 64, p_extra, pltpu.roll(p_extra, 64, 1))
    profile = jnp.concatenate([p_own, p_extra], axis=1)
    cols = iota((1, 2 * local), 1)
    work_ref[...] = kinetic_ref[...]
    for which in range(2):
        mine = (cols < local) | ((cols - local) // 64 == which)
        for i in range(4):
            row = (VALUE[i] / KIN) * profile[0:1] + (SLOPE[i] / KIN) * profile[1:2]
            at = local + 64 * which + 32 + i
            row = jnp.where(mine, row, 0.0) + work_ref[which, at : at + 1, :]
            high = row.astype(BF16).astype(F32)
            work_ref[which, at : at + 1, :] = high
            at = local + 64 * which + 32 + INNER + i
            work_ref[which, at : at + 1, :] = row - high
    matrix_ref[...] = work_ref[...].astype(BF16)
    radii = lane_radii(first, local)
    drive = field_ref[0] * radii
    for power in range(1, ORDER + 1):
        mix(coupling_ref, stack_ref, mixed_ref)
        stencil(stack_ref, matrix_ref, moved_ref)
        if power == 1:
            part_ref[0:1, :] = intersect(state_ref, mixed_ref, radii)
        advance(v_ref, state_ref, stack_ref, mixed_ref, moved_ref, pot_ref, drive, time_step / power)
    split_store(stack_ref, 0, state_ref[...])
    mix(coupling_ref, stack_ref, mixed_ref)
    part_ref[1:2, :] = intersect(state_ref, mixed_ref, radii)
    part_ref[2:, :] = jnp.zeros((part_ref.shape[0] - 2, local), F32)


def second_kernel(
    first_ref, field_ref, state_in_ref, mixed_in_ref, matrix_ref, coupling_ref, pot_ref, out_ref, v_ref, total_ref, stack_ref, mixed_ref, moved_ref
):
    local = 128
    radii = lane_radii(first_ref[0], local)
    drive = field_ref[1] * radii
    v_ref[...] = state_in_ref[...]
    total_ref[...] = state_in_ref[...]
    split_store(stack_ref, 0, state_in_ref[...])
    for power in range(1, ORDER + 1):
        if power > 1:
            mix(coupling_ref, stack_ref, mixed_ref)
        stencil(stack_ref, matrix_ref, moved_ref)
        advance(
            v_ref,
            total_ref,
            stack_ref,
            mixed_in_ref if power == 1 else mixed_ref,
            moved_ref,
            pot_ref,
            drive,
            time_step / power,
        )
    for k, part in enumerate(PARTS):
        out_ref[k] = total_ref[:, OWN[part] : OWN[part] + local]


def tree(count):
    if count == 16:
        return [[2], [4, 8, 12], [1]]
    return [[1 << k] for k in range((count - 1).bit_length())]


def broadcast(value, axis, count):
    here = lax.axis_index(axis)
    have = [0]
    for offsets in tree(count):
        fresh, chosen = [], value
        for offset in offsets:
            pairs = [(h, h + offset) for h in have if h + offset < count]
            got = lax.ppermute(value, axis, pairs)
            to = [p[1] for p in pairs]
            hit = functools.reduce(jnp.logical_or, [here == t for t in to])
            chosen = jnp.where(hit, got, chosen)
            fresh += to
        value = chosen
        have += fresh
    return value


def vmem(count):
    return [pl.BlockSpec(memory_space=pltpu.VMEM)] * count


def smem(count):
    return [pl.BlockSpec(memory_space=pltpu.SMEM)] * count


def params():
    return pltpu.CompilerParams(vmem_limit_bytes=48 * 1024 * 1024)


def per_device(states, dipole, pattern, angular, thresholds, surface_profile, pulse_field, *, count):
    channels, local = states.shape[1:]
    grid_points = local * count
    half = channels // 2
    axis = "radius"
    first = (lax.axis_index(axis) * local).reshape(1).astype(jnp.int32)
    shape = jax.ShapeDtypeStruct

    to_right, to_left, inner = pl.pallas_call(
        pack_kernel,
        out_shape=(shape((half + 8, local), F32), shape((half + 8, local), F32), shape((channels + 8, local), F32)),
        in_specs=vmem(2),
        out_specs=tuple(vmem(3)),
        compiler_params=params(),
        name="pack",
    )(states, surface_profile)
    left = lax.ppermute(to_right, axis, [(i, i + 1) for i in range(count - 1)])
    right = lax.ppermute(to_left, axis, [(i + 1, i) for i in range(count - 1)])
    inner = broadcast(inner, axis, count)

    coupling, kinetic, pot = pl.pallas_call(
        functools.partial(table_kernel, grid_points=grid_points),
        out_shape=(
            shape((channels, 3 * channels), BF16),
            shape((2, 2 * local, 2 * local), F32),
            shape((channels, 2 * local), F32),
        ),
        in_specs=smem(1) + vmem(4),
        out_specs=tuple(vmem(3)),
        compiler_params=params(),
        name="tables",
    )(first, dipole, pattern, angular.reshape(1, channels), thresholds.reshape(1, channels))

    width = 6 * local
    state, mixed, matrix, part = pl.pallas_call(
        first_kernel,
        out_shape=(
            shape((channels, width), F32),
            shape((channels, width), F32),
            shape((2, 2 * local, 2 * local), BF16),
            shape((8, local), F32),
        ),
        in_specs=smem(2) + vmem(8),
        out_specs=tuple(vmem(4)),
        scratch_shapes=[
            pltpu.VMEM((channels, width), F32),
            pltpu.VMEM((3 * channels, width), BF16),
            pltpu.VMEM((4, channels, 2 * local), F32),
            pltpu.VMEM((2, 2 * local, 2 * local), F32),
        ],
        compiler_params=params(),
        name="first",
    )(first, pulse_field, states, left, right, inner, surface_profile, coupling, kinetic, pot)

    final = pl.pallas_call(
        second_kernel,
        out_shape=shape(states.shape, F32),
        in_specs=smem(2) + vmem(5),
        out_specs=vmem(1)[0],
        scratch_shapes=[
            pltpu.VMEM((channels, width), F32),
            pltpu.VMEM((channels, width), F32),
            pltpu.VMEM((3 * channels, width), BF16),
            pltpu.VMEM((channels, width), F32),
            pltpu.VMEM((4, channels, 2 * local), F32),
        ],
        compiler_params=params(),
        name="second",
    )(first, pulse_field, state, mixed, matrix, coupling, pot)

    bit = 1
    while bit < count:
        part = part + lax.ppermute(part, axis, [(i, i ^ bit) for i in range(count)])
        bit *= 2
    normalizer = math.sqrt(channels * grid_points) * (inner_radius + grid_points * spacing)
    gradient = jnp.sum(part[:STEPS], axis=1) / normalizer
    return final, gradient


def solution(mesh):
    return jax.shard_map(
        functools.partial(per_device, count=mesh.shape["radius"]),
        mesh=mesh,
        in_specs=(P("groups", None, "radius"), P(), P(), P(), P(), P(None, "radius"), P("groups")),
        out_specs=(P("groups", None, "radius"), P("groups")),
        check_vma=False,
    )
```

time: 633 us -> 61.7 us (0.10); the launches traced: 624 us -> 61.4 us
  blocking collectives: 474 us -> 0 us
  other arithmetic: 68.8 us -> 0.78 us
  local copies, waits for them, and re-layouts: 31.9 us -> 1.85 us
  matrix products: 24 us -> 0 us
  waiting for transfers between devices: 0.04 us -> 19.9 us
  Pallas kernels: 0 us -> 19 us
    psum x8 -> x0, blocking collectives: 474 us -> none  [spread(): return lax.psum(jnp.where(mine, value, jnp.zeros_like(value)), axis)]
    add x12 -> x4, other arithmetic: 44.2 us -> 0.01 us  [per_device(): part = part + lax.ppermute(part, axis, [(i, i ^ bit) for i in range(count)])]
    dot_general x9 -> x0, matrix products: 24 us -> none  [the longest x8 21.4 us: apply_hamiltonian(): jnp.einsum('cd,kdr->kcr', coupling, center, precision=lax.Precision.HIGHEST)]
    ppermute x16 -> x11, waiting for transfers between devices: 0.04 us -> 19.9 us  [the longest x5 8.38 us: broadcast(): got = lax.ppermute(value, axis, pairs)]
    dot_general x8 -> x0, local copies, waits for them, and re-layouts: 19.5 us -> none  [apply_hamiltonian(): jnp.einsum('cd,kdr->kcr', coupling, center, precision=lax.Precision.HIGHEST)]
    pallas_call x0 -> x4, Pallas kernels: none -> 19 us  [the longest x1 9.47 us: per_device(): pl.pallas_call(first_kernel, out_shape=(shape((channels, width), F32), sh...]
    select_n x15 -> x3, other arithmetic: 7.07 us -> 0.14 us  [broadcast(): chosen = jnp.where(hit, got, chosen)]
    slice x8 -> x0, other arithmetic: 6.49 us -> none  [apply_hamiltonian(): hamiltonian[1]]
  transfers between devices with their start and end apart: 16 -> 11, of which waited for: 0 -> 8; matrix products, arithmetic and copies ran while one was open for 6% -> 0% of each run, Pallas kernels for 0% -> 14%
where the time goes in v1:
time: 61.7 us; the launch traced here: 61.4 us
  waiting for transfers between devices  19.9 us (32%)
  Pallas kernels  19 us (31%)
  starting transfers between devices  19 us (31%)
  local copies, waits for them, and re-layouts  1.85 us (3%)
  between operations  0.86 us (1%)
  other arithmetic  0.78 us (1%)
    ppermute x5, starting transfers between devices, broadcast(): got = lax.ppermute(value, axis, pairs)  10.1 us
    pallas_call x1, Pallas kernels, per_device(): pl.pallas_call(first_kernel, out_shape=(shape((channels, width), F32), sh...  9.47 us
    ppermute x5, waiting for transfers between devices, broadcast(): got = lax.ppermute(value, axis, pairs)  8.38 us
    ppermute x4, waiting for transfers between devices, per_device(): part = part + lax.ppermute(part, axis, [(i, i ^ bit) for i in range(count)])  7.91 us
    pallas_call x1, Pallas kernels, per_device(): pl.pallas_call(second_kernel, out_shape=shape(states.shape, F32), in_spec...  7.86 us
    ppermute x4, starting transfers between devices, per_device(): part = part + lax.ppermute(part, axis, [(i, i ^ bit) for i in range(count)])  6.33 us
    ppermute x1, waiting for transfers between devices, per_device(): right = lax.ppermute(to_left, axis, [(i + 1, i) for i in range(count - 1)])  3.65 us
    unnamed x18, local copies, waits for them, and re-layouts  1.85 us
  transfers between devices with their start and end apart: 11, of which 8 were waited for; matrix products, arithmetic and copies ran while one was open for 0% of the time, Pallas kernels for 14%

profile of v1, /device:TPU:0, one launch (start us, length us, event | category | flops | bytes accessed | tf_op | source)
XLA Modules:
  0.0 61.4 jit_solution(1408573952209938315)
XLA Ops:
  0.6 1.1 %copy-done = f32[4,400,128]{2,1,0:T(8,128)S(1)} copy-done((f32[4,400,128]{2,1,0:T(8,128)S(1)}, f32[4,400,128]{2,1,0:T(8,128)}, u32[]{:S(2)}) %copy-start) | copy-done | bytes 819224
  1.8 0.7 %copy-done.4 = f32[2,128]{1,0:T(2,128)S(1)} copy-done((f32[2,128]{1,0:T(2,128)S(1)}, f32[2,128]{1,0:T(2,128)}, u32[]{:S(2)}) %copy-start.4) | copy-done | bytes 1048
  2.5 0.8 %pack.1 = (f32[208,128]{1,0:T(8,128)S(1)}, f32[208,128]{1,0:T(8,128)S(1)}, f32[408,128]{1,0:T(8,128)S(1)}) custom-call(f32[4,400,128]{2,1,0:T(8,128)S(1)} %copy-done, f32[2,128]{1,0:T(2,128)S(1)} %copy-done.4), custom_call_target="tpu_custom_call" | custom-call | tf_op jit(solution)/shard_map/pack/pallas_call | solution.py:381
  3.3 4.9 %collective-permute-start.2 = (f32[408,128]{1,0:T(8,128)S(1)}, f32[408,128]{1,0:T(8,128)S(1)}, u32[]{:S(2)}, u32[]{:S(2)}) collective-permute-start(f32[408,128]{1,0:T(8,128)S(1)} %get-tuple-element.14), channel_id=1, source_target_pairs={{0,2},{16,18}} | collective-permute-start | bytes 626696 | tf_op jit(solution)/shard_map/ppermute | solution.py:351
  8.2 3.3 %collective-permute-done.2 = f32[408,128]{1,0:T(8,128)S(1)} collective-permute-done((f32[408,128]{1,0:T(8,128)S(1)}, f32[408,128]{1,0:T(8,128)S(1)}, u32[]{:S(2)}, u32[]{:S(2)}) %collective-permute-start.2) | collective-permute-done | bytes 208928 | tf_op jit(solution)/shard_map/ppermute | solution.py:351
  11.5 1.3 %collective-permute-start.5 = (f32[408,128]{1,0:T(8,128)S(1)}, f32[408,128]{1,0:T(8,128)S(1)}, u32[]{:S(2)}, u32[]{:S(2)}) collective-permute-start(f32[408,128]{1,0:T(8,128)S(1)} %broadcast_select_fusion), channel_id=1, source_target_pairs={{0,4},{2,6},{16,20},{18,22}} | collective-permute-start | bytes 626696 | tf_op jit(solution)/shard_map/ppermute | solution.py:351
  12.8 1.3 %collective-permute-start.4 = (f32[408,128]{1,0:T(8,128)S(1)}, f32[408,128]{1,0:T(8,128)S(1)}, u32[]{:S(2)}, u32[]{:S(2)}) collective-permute-start(f32[408,128]{1,0:T(8,128)S(1)} %broadcast_select_fusion), channel_id=1, source_target_pairs={{0,8},{2,10},{16,24},{18,26}} | collective-permute-start | bytes 626696 | tf_op jit(solution)/shard_map/ppermute | solution.py:351
  14.1 1.3 %collective-permute-start.3 = (f32[408,128]{1,0:T(8,128)S(1)}, f32[408,128]{1,0:T(8,128)S(1)}, u32[]{:S(2)}, u32[]{:S(2)}) collective-permute-start(f32[408,128]{1,0:T(8,128)S(1)} %broadcast_select_fusion), channel_id=1, source_target_pairs={{0,12},{2,14},{16,28},{18,30}} | collective-permute-start | bytes 626696 | tf_op jit(solution)/shard_map/ppermute | solution.py:351
  15.5 0.6 %collective-permute-done.5 = f32[408,128]{1,0:T(8,128)S(1)} collective-permute-done((f32[408,128]{1,0:T(8,128)S(1)}, f32[408,128]{1,0:T(8,128)S(1)}, u32[]{:S(2)}, u32[]{:S(2)}) %collective-permute-start.5) | collective-permute-done | bytes 208928 | tf_op jit(solution)/shard_map/ppermute | solution.py:351
  16.1 2.2 %collective-permute-done.4 = f32[408,128]{1,0:T(8,128)S(1)} collective-permute-done((f32[408,128]{1,0:T(8,128)S(1)}, f32[408,128]{1,0:T(8,128)S(1)}, u32[]{:S(2)}, u32[]{:S(2)}) %collective-permute-start.4) | collective-permute-done | bytes 208928 | tf_op jit(solution)/shard_map/ppermute | solution.py:351
  18.3 2.2 %collective-permute-done.3 = f32[408,128]{1,0:T(8,128)S(1)} collective-permute-done((f32[408,128]{1,0:T(8,128)S(1)}, f32[408,128]{1,0:T(8,128)S(1)}, u32[]{:S(2)}, u32[]{:S(2)}) %collective-permute-start.3) | collective-permute-done | bytes 208928 | tf_op jit(solution)/shard_map/ppermute | solution.py:351
  20.6 1.3 %collective-permute-start.6 = (f32[408,128]{1,0:T(8,128)S(1)}, f32[408,128]{1,0:T(8,128)S(1)}, u32[]{:S(2)}, u32[]{:S(2)}) collective-permute-start(f32[408,128]{1,0:T(8,128)S(1)} %select_select_fusion), channel_id=1, source_target_pairs={{0,1},{2,3},{4,5},{6,7},{8,9},{10,11},{12,13},{14,15},{16,17},{18,... | collective-permute-start | bytes 626696 | tf_op jit(solution)/shard_map/ppermute | solution.py:351
  22.0 1.3 %collective-permute-start = (f32[208,128]{1,0:T(8,128)S(1)}, f32[208,128]{1,0:T(8,128)S(1)}, u32[]{:S(2)}, u32[]{:S(2)}) collective-permute-start(f32[208,128]{1,0:T(8,128)S(1)} %get-tuple-element.12), channel_id=1, source_target_pairs={{0,1},{1,2},{2,3},{3,4},{4,5},{5,6},{6,7},{7,8},{8,9},{9,10},{10,1... | collective-permute-start | bytes 319496 | tf_op jit(solution)/shard_map/ppermute | solution.py:389
  23.3 1.3 %collective-permute-start.1 = (f32[208,128]{1,0:T(8,128)S(1)}, f32[208,128]{1,0:T(8,128)S(1)}, u32[]{:S(2)}, u32[]{:S(2)}) collective-permute-start(f32[208,128]{1,0:T(8,128)S(1)} %get-tuple-element.13), channel_id=1, source_target_pairs={{1,0},{2,1},{3,2},{4,3},{5,4},{6,5},{7,6},{8,7},{9,8},{10,9},{11,1... | collective-permute-start | bytes 319496 | tf_op jit(solution)/shard_map/ppermute | solution.py:390
  24.6 0.8 %tables.1 = (bf16[400,1200]{1,0:T(8,128)(2,1)S(1)}, f32[2,256,256]{2,1,0:T(8,128)S(1)}, f32[400,256]{1,0:T(8,128)S(1)}) custom-call(s32[1]{0:T(128)} %bitcast.first_ref, f32[400,400]{1,0:T(8,128)S(1)} %copy-done.2, s32[25,25]{1,0:T(8,128)S(1)} %copy-done.3, s32[1,400]{1,0:T(1,128)S(1)} %bitcast.3, f32[1,400]{1,0:T(1,128)S(1)} %bitcast.4), custom_call_target="tpu_custom_call" | custom-call | tf_op jit(solution)/shard_map/tables/pallas_call | solution.py:393
  25.5 3.6 %collective-permute-done.1.right_ref = f32[208,128]{1,0:T(8,128)S(1)} collective-permute-done((f32[208,128]{1,0:T(8,128)S(1)}, f32[208,128]{1,0:T(8,128)S(1)}, u32[]{:S(2)}, u32[]{:S(2)}) %collective-permute-start.1) | collective-permute-done | bytes 106528 | tf_op jit(solution)/shard_map/ppermute | solution.py:390
  29.2 9.5 %first.1 = (f32[400,768]{1,0:T(8,128)S(1)}, f32[400,768]{1,0:T(8,128)S(1)}, bf16[2,256,256]{2,1,0:T(8,128)(2,1)S(1)}, f32[8,128]{1,0:T(8,128)S(1)}) custom-call(s32[1]{0:T(128)} %bitcast.first_ref, f32[2]{0:T(128)S(1)} %copy-done.8, f32[4,400,128]{2,1,0:T(8,128)S(1)} %copy-done.1, f32[208,128]{1,0:T(8,128)S(1)} %collective-permute-done.left_ref, ...), custom_call_target="tpu_custom_call" | custom-call | tf_op jit(solution)/shard_map/first/pallas_call | solution.py:407
  38.7 3.4 %collective-permute-start.7 = (f32[8,128]{1,0:T(8,128)S(1)}, f32[8,128]{1,0:T(8,128)S(1)}, u32[]{:S(2)}, u32[]{:S(2)}) collective-permute-start(f32[8,128]{1,0:T(8,128)S(1)} %get-tuple-element.21), channel_id=1, source_target_pairs={{0,1},{1,0},{2,3},{3,2},{4,5},{5,4},{6,7},{7,6},{8,9},{9,8},{10,11... | collective-permute-start | bytes 12296 | tf_op jit(solution)/shard_map/ppermute | solution.py:445
  42.0 0.8 %collective-permute-done.7 = f32[8,128]{1,0:T(8,128)S(1)} collective-permute-done((f32[8,128]{1,0:T(8,128)S(1)}, f32[8,128]{1,0:T(8,128)S(1)}, u32[]{:S(2)}, u32[]{:S(2)}) %collective-permute-start.7) | collective-permute-done | bytes 4128 | tf_op jit(solution)/shard_map/ppermute | solution.py:445
  43.0 3.5 %collective-permute-done.8 = f32[8,128]{1,0:T(8,128)S(1)} collective-permute-done((f32[8,128]{1,0:T(8,128)S(1)}, f32[8,128]{1,0:T(8,128)S(1)}, u32[]{:S(2)}, u32[]{:S(2)}) %collective-permute-start.8) | collective-permute-done | bytes 4128 | tf_op jit(solution)/shard_map/ppermute | solution.py:445
  46.5 3.6 %collective-permute-done.9 = f32[8,128]{1,0:T(8,128)S(1)} collective-permute-done((f32[8,128]{1,0:T(8,128)S(1)}, f32[8,128]{1,0:T(8,128)S(1)}, u32[]{:S(2)}, u32[]{:S(2)}) %collective-permute-start.9) | collective-permute-done | bytes 4128 | tf_op jit(solution)/shard_map/ppermute | solution.py:445
  50.1 2.8 %collective-permute-start.10 = (f32[8,128]{1,0:T(8,128)S(1)}, f32[8,128]{1,0:T(8,128)S(1)}, u32[]{:S(2)}, u32[]{:S(2)}) collective-permute-start(f32[8,128]{1,0:T(8,128)S(1)} %add.14), channel_id=1, source_target_pairs={{0,8},{1,9},{2,10},{3,11},{4,12},{5,13},{6,14},{7,15},{8,0},{9,1},... | collective-permute-start | bytes 12296 | tf_op jit(solution)/shard_map/ppermute | solution.py:445
  52.9 7.9 %second.1 = f32[4,400,128]{2,1,0:T(8,128)} custom-call(s32[1]{0:T(128)} %bitcast.first_ref, f32[2]{0:T(128)S(1)} %copy-done.8, f32[400,768]{1,0:T(8,128)S(1)} %get-tuple-element.18.state_in_ref, f32[400,768]{1,0:T(8,128)S(1)} %get-tuple-element.19.mixed_in_ref, bf16[2,256,256]{2,1,0:T(8,128)(2,1)S(1)} %get-tuple-element.20.matrix_ref, ...), custom_call_target="tpu_custom_call" | custom-call | tf_op jit(solution)/shard_map/second/pallas_call | solution.py:427
  60.9 0.5 broadcast_multiply_fusion
  (29 shorter events, 0.4 us)
Async XLA Ops:
  0.6 1.1 %copy-start = (f32[4,400,128]{2,1,0:T(8,128)S(1)}, f32[4,400,128]{2,1,0:T(8,128)}, u32[]{:S(2)}) copy-start(f32[4,400,128]{2,1,0:T(8,128)} %states_ref.3) | copy-start | bytes 2457604
  1.8 0.7 %copy-start.4 = (f32[2,128]{1,0:T(2,128)S(1)}, f32[2,128]{1,0:T(2,128)}, u32[]{:S(2)}) copy-start(f32[2,128]{1,0:T(2,128)} %profile_ref.3) | copy-start | bytes 3076
  2.5 22.1 %copy-start.2 = (f32[400,400]{1,0:T(8,128)S(1)}, f32[400,400]{1,0:T(8,128)}, u32[]{:S(2)}) copy-start(f32[400,400]{1,0:T(8,128)} %dipole_ref.1) | copy-start | bytes 1920004
  2.5 22.1 %copy-start.3 = (s32[25,25]{1,0:T(8,128)S(1)}, s32[25,25]{1,0:T(8,128)}, u32[]{:S(2)}) copy-start(s32[25,25]{1,0:T(8,128)} %pattern_ref.1) | copy-start | bytes 7504
  2.5 22.1 %copy-start.6 = (s32[400]{0:T(512)S(1)}, s32[400]{0:T(512)}, u32[]{:S(2)}) copy-start(s32[400]{0:T(512)} %param.10) | copy-start | bytes 4804
  2.5 22.2 %copy-start.7 = (f32[400]{0:T(512)S(1)}, f32[400]{0:T(512)}, u32[]{:S(2)}) copy-start(f32[400]{0:T(512)} %param.11) | copy-start | bytes 4804
  3.3 8.2 %collective-permute-start.2 = (f32[408,128]{1,0:T(8,128)S(1)}, f32[408,128]{1,0:T(8,128)S(1)}, u32[]{:S(2)}, u32[]{:S(2)}) collective-permute-start(f32[408,128]{1,0:T(8,128)S(1)} %get-tuple-element.14), channel_id=1, source_target_pairs={{0,2},{16,18}} | collective-permute-start | bytes 626696 | tf_op jit(solution)/shard_map/ppermute | solution.py:351
  11.5 4.6 %collective-permute-start.5 = (f32[408,128]{1,0:T(8,128)S(1)}, f32[408,128]{1,0:T(8,128)S(1)}, u32[]{:S(2)}, u32[]{:S(2)}) collective-permute-start(f32[408,128]{1,0:T(8,128)S(1)} %broadcast_select_fusion), channel_id=1, source_target_pairs={{0,4},{2,6},{16,20},{18,22}} | collective-permute-start | bytes 626696 | tf_op jit(solution)/shard_map/ppermute | solution.py:351
  12.8 5.5 %collective-permute-start.4 = (f32[408,128]{1,0:T(8,128)S(1)}, f32[408,128]{1,0:T(8,128)S(1)}, u32[]{:S(2)}, u32[]{:S(2)}) collective-permute-start(f32[408,128]{1,0:T(8,128)S(1)} %broadcast_select_fusion), channel_id=1, source_target_pairs={{0,8},{2,10},{16,24},{18,26}} | collective-permute-start | bytes 626696 | tf_op jit(solution)/shard_map/ppermute | solution.py:351
  14.1 6.5 %collective-permute-start.3 = (f32[408,128]{1,0:T(8,128)S(1)}, f32[408,128]{1,0:T(8,128)S(1)}, u32[]{:S(2)}, u32[]{:S(2)}) collective-permute-start(f32[408,128]{1,0:T(8,128)S(1)} %broadcast_select_fusion), channel_id=1, source_target_pairs={{0,12},{2,14},{16,28},{18,30}} | collective-permute-start | bytes 626696 | tf_op jit(solution)/shard_map/ppermute | solution.py:351
  15.4 13.7 %copy-start.1 = (f32[4,400,128]{2,1,0:T(8,128)S(1)}, f32[4,400,128]{2,1,0:T(8,128)}, u32[]{:S(2)}) copy-start(f32[4,400,128]{2,1,0:T(8,128)} %states_ref.3) | copy-start | bytes 2457604
  15.5 13.7 %copy-start.5 = (f32[2,128]{1,0:T(2,128)S(1)}, f32[2,128]{1,0:T(2,128)}, u32[]{:S(2)}) copy-start(f32[2,128]{1,0:T(2,128)} %profile_ref.3) | copy-start | bytes 3076
  15.5 13.7 %copy-start.8 = (f32[2]{0:T(128)S(1)}, f32[2]{0:T(128)}, u32[]{:S(2)}) copy-start(f32[2]{0:T(128)} %field_ref.3) | copy-start | bytes 28
  20.6 4.8 %collective-permute-start.6 = (f32[408,128]{1,0:T(8,128)S(1)}, f32[408,128]{1,0:T(8,128)S(1)}, u32[]{:S(2)}, u32[]{:S(2)}) collective-permute-start(f32[408,128]{1,0:T(8,128)S(1)} %select_select_fusion), channel_id=1, source_target_pairs={{0,1},{2,3},{4,5},{6,7},{8,9},{10,11},{12,13},{14,15},{16,17},{18,... | collective-permute-start | bytes 626696 | tf_op jit(solution)/shard_map/ppermute | solution.py:351
  22.0 3.6 %collective-permute-start = (f32[208,128]{1,0:T(8,128)S(1)}, f32[208,128]{1,0:T(8,128)S(1)}, u32[]{:S(2)}, u32[]{:S(2)}) collective-permute-start(f32[208,128]{1,0:T(8,128)S(1)} %get-tuple-element.12), channel_id=1, source_target_pairs={{0,1},{1,2},{2,3},{3,4},{4,5},{5,6},{6,7},{7,8},{8,9},{9,10},{10,1... | collective-permute-start | bytes 319496 | tf_op jit(solution)/shard_map/ppermute | solution.py:389
  23.3 5.9 %collective-permute-start.1 = (f32[208,128]{1,0:T(8,128)S(1)}, f32[208,128]{1,0:T(8,128)S(1)}, u32[]{:S(2)}, u32[]{:S(2)}) collective-permute-start(f32[208,128]{1,0:T(8,128)S(1)} %get-tuple-element.13), channel_id=1, source_target_pairs={{1,0},{2,1},{3,2},{4,3},{5,4},{6,5},{7,6},{8,7},{9,8},{10,9},{11,1... | collective-permute-start | bytes 319496 | tf_op jit(solution)/shard_map/ppermute | solution.py:390
  38.7 4.2 %collective-permute-start.7 = (f32[8,128]{1,0:T(8,128)S(1)}, f32[8,128]{1,0:T(8,128)S(1)}, u32[]{:S(2)}, u32[]{:S(2)}) collective-permute-start(f32[8,128]{1,0:T(8,128)S(1)} %get-tuple-element.21), channel_id=1, source_target_pairs={{0,1},{1,0},{2,3},{3,2},{4,5},{5,4},{6,7},{7,6},{8,9},{9,8},{10,11... | collective-permute-start | bytes 12296 | tf_op jit(solution)/shard_map/ppermute | solution.py:445
  42.9 3.6 %collective-permute-start.8 = (f32[8,128]{1,0:T(8,128)S(1)}, f32[8,128]{1,0:T(8,128)S(1)}, u32[]{:S(2)}, u32[]{:S(2)}) collective-permute-start(f32[8,128]{1,0:T(8,128)S(1)} %add.12), channel_id=1, source_target_pairs={{0,2},{1,3},{2,0},{3,1},{4,6},{5,7},{6,4},{7,5},{8,10},{9,11},{10,... | collective-permute-start | bytes 12296 | tf_op jit(solution)/shard_map/ppermute | solution.py:445
  46.5 3.6 %collective-permute-start.9 = (f32[8,128]{1,0:T(8,128)S(1)}, f32[8,128]{1,0:T(8,128)S(1)}, u32[]{:S(2)}, u32[]{:S(2)}) collective-permute-start(f32[8,128]{1,0:T(8,128)S(1)} %add.13), channel_id=1, source_target_pairs={{0,4},{1,5},{2,6},{3,7},{4,0},{5,1},{6,2},{7,3},{8,12},{9,13},{10,... | collective-permute-start | bytes 12296 | tf_op jit(solution)/shard_map/ppermute | solution.py:445
  50.1 10.7 %collective-permute-start.10 = (f32[8,128]{1,0:T(8,128)S(1)}, f32[8,128]{1,0:T(8,128)S(1)}, u32[]{:S(2)}, u32[]{:S(2)}) collective-permute-start(f32[8,128]{1,0:T(8,128)S(1)} %add.14), channel_id=1, source_target_pairs={{0,8},{1,9},{2,10},{3,11},{4,12},{5,13},{6,14},{7,15},{8,0},{9,1},... | collective-permute-start | bytes 12296 | tf_op jit(solution)/shard_map/ppermute | solution.py:445

commit v2 on v1

v2 whole, which is shorter than its diff:
```python
import functools
import math

import jax
import jax.numpy as jnp
from jax import lax
from jax.experimental import pallas as pl
from jax.experimental.pallas import tpu as pltpu
from jax.sharding import PartitionSpec as P

STEPS = 2
ORDER = 4

inner_radius = 20.0
spacing = 0.08
time_step = 0.005

HALO = 2 * ORDER * STEPS
INNER = 2 * ORDER * STEPS + 2
KIN = 1.0 / (24.0 * spacing * spacing)
VALUE = (4.0, -6.0, 4.0, -1.0)
SLOPE = (-13.0 / 3.0, 9.5, -7.0, 11.0 / 6.0)

F32 = jnp.float32
BF16 = jnp.bfloat16

OWN = {"a": 0, "c": 128, "b": 512, "d": 640}
EXTRA = {"a": 256, "c": 256, "b": 384, "d": 384}
PARTS = ("a", "b", "c", "d")


def iota(shape, dim):
    return lax.broadcasted_iota(jnp.int32, shape, dim)


def is_odd(first, local):
    return lax.rem(lax.div(first, local), 2) == 1


def pack_kernel(first_ref, states_any, profile_any, near_ref, far_ref, inner_ref, states_ref, profile_ref, sems):
    channels = states_ref.shape[1]
    half = channels // 2
    local = states_ref.shape[2]
    copies = [pltpu.make_async_copy(states_any.at[k], states_ref.at[k], sems.at[k]) for k in range(4)]
    copies.append(pltpu.make_async_copy(profile_any, profile_ref, sems.at[4]))
    for copy in copies:
        copy.start()
    copies[4].wait()
    odd = is_odd(first_ref[0], local)
    zeros = jnp.zeros((6, local), F32)
    prof = profile_ref[...]
    turned = pltpu.roll(prof, HALO, 1)
    for ref, value in (
        (near_ref, jnp.where(odd, prof, turned)),
        (far_ref, jnp.where(odd, turned, prof)),
        (inner_ref, prof),
    ):
        ref[half : half + 2, :] = value
        ref[half + 2 : half + 8, :] = zeros
    group = iota((half, local), 1) // 16
    pair = (iota((channels, local), 1) & 63) // 2
    right = left = more = None
    for k, first in ((0, 0), (2, 64), (1, 16), (3, 80)):
        copies[k].wait()
        for h in range(2):
            rows = states_ref[k, half * h : half * h + half, :]
            at = first + 32 * h
            hit = group == at // 16
            shift = (at + HALO) % local
            moved = pltpu.roll(rows, shift, 1) if shift else rows
            right = moved if right is None else jnp.where(hit, moved, right)
            moved = pltpu.roll(rows, at, 1) if at else rows
            left = moved if left is None else jnp.where(hit, moved, left)
        at = 64 * (k // 2) + 2 * (k % 2)
        moved = pltpu.roll(states_ref[k], (at - 16) % local, 1)
        more = moved if more is None else jnp.where(pair == k % 2, jnp.where(iota((channels, local), 1) // 64 == k // 2, moved, more), more)
    near_ref[:half, :] = jnp.where(odd, left, right)
    far_ref[:half, :] = jnp.where(odd, right, left)
    inner_ref[:half, :] = left
    rest = None
    quad = (iota((32, local), 1) & 63) // 4
    for i in range((channels + 31) // 32):
        rows = more[32 * i : min(32 * i + 32, channels)]
        if rows.shape[0] < 32:
            rows = jnp.concatenate([rows, jnp.zeros((32 - rows.shape[0], local), F32)], axis=0)
        moved = pltpu.roll(rows, 4 * i, 1) if i else rows
        rest = moved if rest is None else jnp.where(quad == i, moved, rest)
    inner_ref[half + 8 :, :] = rest


def lane_points(lanes, first, local):
    e = (lanes - local) & 63
    own = lanes < local
    point = jnp.where(
        own,
        first + lanes,
        jnp.where(
            e < 16,
            first - 16 + e,
            jnp.where(
                e < 32,
                first + local + e - 16,
                jnp.where(e < 32 + INNER, e - 32, e - 32 - INNER),
            ),
        ),
    )
    segment = jnp.where(
        own, 0, jnp.where(e < 32, 0, jnp.where(e < 32 + INNER, 1, jnp.where(e < 36 + INNER, 2, 3)))
    )
    return point, segment


def lane_radii(first, local):
    lanes = iota((8, 2 * local), 1)
    point, _ = lane_points(lanes, first, local)
    return (inner_radius + (point + 1).astype(F32) * spacing)[:1]


def table_kernel(
    first_ref,
    dipole_ref,
    pattern_ref,
    angular_ref,
    thr_ref,
    states_ref,
    coupling_ref,
    kinetic_ref,
    pot_ref,
    v_ref,
    stack_ref,
    mixed_ref,
    part_ref,
    *,
    grid_points,
):
    channels = dipole_ref.shape[0]
    blocks = pattern_ref.shape[0]
    size = channels // blocks
    local = 128
    first = first_ref[0]
    pattern = pattern_ref[...].astype(F32)
    joined = jnp.maximum(pattern, pattern.T).astype(BF16)
    tall = (iota((channels, blocks), 0) // size == iota((channels, blocks), 1)).astype(F32).astype(BF16)
    wide = (iota((blocks, channels), 1) // size == iota((blocks, channels), 0)).astype(F32).astype(BF16)
    rows = jnp.dot(tall, joined, preferred_element_type=F32).astype(BF16)
    mask = jnp.dot(rows, wide, preferred_element_type=F32)
    ang = jnp.broadcast_to(angular_ref[...].astype(F32), (channels, channels))
    angt = ang.T
    allowed = (mask > 0.5) & (jnp.abs(ang - angt) == 1.0)
    dip = dipole_ref[...]
    coupling = jnp.where(allowed, 0.5 * (dip + dip.T), 0.0)
    high = coupling.astype(BF16)
    low = (coupling - high.astype(F32)).astype(BF16)
    coupling_ref[...] = jnp.concatenate([high, high, low], axis=1)
    radii = lane_radii(first, local)
    inverse = 1.0 / (radii * radii)
    centrifugal = 0.5 * angt[:, :local] * (angt[:, :local] + 1.0)
    thr = jnp.broadcast_to(thr_ref[...], (local, channels)).T
    pot_ref[:, :local] = thr + centrifugal * inverse[:, :local]
    pot_ref[:, local:] = thr + centrifugal * inverse[:, local:]
    shape = (2 * local, 2 * local)
    src, dst = iota(shape, 0), iota(shape, 1)
    sp, ss = lane_points(src, first, local)
    dp, ds = lane_points(dst, first, local)
    gap = jnp.abs(sp - dp)
    coef = jnp.where(gap == 0, 30.0, jnp.where(gap == 1, -16.0, jnp.where(gap == 2, 1.0, 0.0)))
    same = (ss < 2) & (ss == jnp.minimum(ds, 1))
    valid = (dp >= 0) & (dp < grid_points) & (ds < 3)
    coef = jnp.where(same & valid, coef, 0.0)
    for which in range(2):
        mine = (src < local) | ((src - local) // 64 == which)
        mine = mine & ((dst < local) | ((dst - local) // 64 == which))
        kinetic_ref[which] = jnp.where(mine, coef, 0.0)
    for k, part in enumerate(PARTS):
        at = OWN[part]
        v_ref[:, at : at + local] = states_ref[k]
        split_store(stack_ref, at, states_ref[k])
    mix(coupling_ref, stack_ref, mixed_ref, (0, 2))
    part_ref[0:1, :] = intersect(v_ref, mixed_ref, radii)
    part_ref[1:, :] = jnp.zeros((part_ref.shape[0] - 1, local), F32)


def split_store(stack_ref, at, value):
    channels = value.shape[0]
    width = value.shape[1]
    high = value.astype(BF16)
    low = (value - high.astype(F32)).astype(BF16)
    stack_ref[:channels, at : at + width] = high
    stack_ref[channels : 2 * channels, at : at + width] = low
    stack_ref[2 * channels :, at : at + width] = high


def mix(coupling_ref, stack_ref, mixed_ref, tiles):
    for n in tiles:
        cut = slice(256 * n, 256 * n + 256)
        mixed_ref[:, cut] = jnp.dot(coupling_ref[...], stack_ref[:, cut], preferred_element_type=F32)


def stencil(stack_ref, matrix_ref, moved_ref):
    channels = stack_ref.shape[0] // 3
    for k, part in enumerate(PARTS):
        own, extra = OWN[part], EXTRA[part]
        weights = matrix_ref[0 if part in "ab" else 1]
        total = None
        for rows in (slice(0, channels), slice(channels, 2 * channels)):
            left = jnp.concatenate([stack_ref[rows, own : own + 128], stack_ref[rows, extra : extra + 128]], axis=1)
            got = jnp.dot(left, weights, preferred_element_type=F32)
            total = got if total is None else total + got
        moved_ref[k] = total


def advance(v_ref, total_ref, stack_ref, mixed_ref, moved_ref, pot_ref, drive, scale, own_only=False, chunk=80):
    channels = v_ref.shape[0]
    local = 128
    for c0 in range(0, channels, chunk):
        rows = slice(c0, c0 + chunk)
        pot_own, pot_extra = pot_ref[rows, :local], pot_ref[rows, local:]
        drive_own, drive_extra = drive[:, :local], drive[:, local:]

        def hamiltonian(at, moved, pot, force):
            cut = slice(at, at + local)
            return KIN * moved + pot * v_ref[rows, cut] + force * mixed_ref[rows, cut]

        new = {}
        for source, target, sign in ((1, "a", 1.0), (0, "b", -1.0), (3, "c", 1.0), (2, "d", -1.0)):
            part = PARTS[source]
            new[OWN[target]] = (sign * scale) * hamiltonian(
                OWN[part], moved_ref[source, rows, :local], pot_own, drive_own
            )
        if not own_only:
            for source, target, sign in (("b", "a", 1.0), ("a", "b", -1.0)):
                k = PARTS.index(source)
                moved = moved_ref[k, rows, local:] + moved_ref[k + 2, rows, local:]
                new[EXTRA[target]] = (sign * scale) * hamiltonian(EXTRA[source], moved, pot_extra, drive_extra)
        for at, value in new.items():
            cut = slice(at, at + local)
            total_ref[rows, cut] = total_ref[rows, cut] + value
            if own_only:
                continue
            v_ref[rows, cut] = value
            high = value.astype(BF16)
            low = (value - high.astype(F32)).astype(BF16)
            stack_ref[c0 : c0 + chunk, cut] = high
            stack_ref[channels + c0 : channels + c0 + chunk, cut] = low
            stack_ref[2 * channels + c0 : 2 * channels + c0 + chunk, cut] = high


def intersect(state_ref, mixed_ref, radii):
    def at(ref, part):
        return ref[:, OWN[part] : OWN[part] + 128]

    both = at(state_ref, "c") * at(mixed_ref, "b") - at(state_ref, "d") * at(mixed_ref, "a")
    return jnp.sum(both * radii[:, :128], axis=0, keepdims=True)


def first_kernel(
    first_ref,
    field_ref,
    far_ref,
    got_ref,
    sent_ref,
    profile_ref,
    coupling_ref,
    kinetic_ref,
    pot_ref,
    part_in_ref,
    v_in_ref,
    stack_in_ref,
    mixed_in_ref,
    v_ref,
    stack_ref,
    mixed_ref,
    state_ref,
    matrix_ref,
    part_ref,
    moved_ref,
    work_ref,
    *,
    scaling,
):
    del v_in_ref, stack_in_ref, mixed_in_ref
    channels = v_ref.shape[0]
    half = channels // 2
    local = 128
    first = first_ref[0]
    odd = is_odd(first, local)
    split = half + 40
    inner = jnp.where(odd, got_ref[:split, :], sent_ref[:split, :])
    left = jnp.where(odd, got_ref[split:, :], far_ref[...])
    right = jnp.where(odd, far_ref[...], got_ref[split:, :])
    lanes = iota((half, local), 1) & 63
    for pair, at in ((0, 256), (1, 384)):
        for h in range(2):
            back = 16 * pair + 32 * h

            def rolled(value, to):
                shift = (to - back) % local
                return pltpu.roll(value, shift, 1) if shift else value

            value = jnp.where(
                lanes < 16,
                rolled(left[:half, :], 0),
                jnp.where(
                    lanes < 32,
                    rolled(right[:half, :], 16),
                    jnp.where(
                        lanes < 48,
                        rolled(inner[:half, :], 32),
                        jnp.where(
                            (lanes >= 50) & (lanes < 54), rolled(inner[:half, :], 50), jnp.zeros((half, local), F32)
                        ),
                    ),
                ),
            )
            v_ref[half * h : half * h + half, at : at + local] = value
        narrow = iota((32, local), 1) & 63
        for i in range((channels + 31) // 32):
            rows = slice(32 * i, min(32 * i + 32, channels))
            count = rows.stop - rows.start
            value = pltpu.roll(inner[half + 8 : half + 8 + count, :], (48 - 4 * i - 2 * pair) % local, 1)
            hit = (narrow[:count] >= 48) & (narrow[:count] < 50)
            v_ref[rows, at : at + local] = jnp.where(hit, value, v_ref[rows, at : at + local])
    state_ref[...] = v_ref[...]
    split_store(stack_ref, 256, v_ref[:, 256:512])
    p_own = profile_ref[...]
    lanes2 = iota((2, local), 1)
    inner_profile = inner[half : half + 2, :]
    p_extra = jnp.where(
        lanes2 < 16,
        left[half : half + 2, :],
        jnp.where(
            lanes2 < 32,
            pltpu.roll(right[half : half + 2, :], 16, 1),
            jnp.where(
                lanes2 < 32 + INNER,
                pltpu.roll(inner_profile, 32, 1),
                jnp.where(lanes2 < 36 + INNER, pltpu.roll(inner_profile, 32 + INNER, 1), 0.0),
            ),
        ),
    )
    p_extra = jnp.where(lanes2 < 64, p_extra, pltpu.roll(p_extra, 64, 1))
    profile = jnp.concatenate([p_own, p_extra], axis=1)
    cols = iota((1, 2 * local), 1)
    work_ref[...] = kinetic_ref[...]
    for which in range(2):
        mine = (cols < local) | ((cols - local) // 64 == which)
        for i in range(4):
            row = (VALUE[i] / KIN) * profile[0:1] + (SLOPE[i] / KIN) * profile[1:2]
            at = local + 64 * which + 32 + i
            row = jnp.where(mine, row, 0.0) + work_ref[which, at : at + 1, :]
            high = row.astype(BF16).astype(F32)
            work_ref[which, at : at + 1, :] = high
            at = local + 64 * which + 32 + INNER + i
            work_ref[which, at : at + 1, :] = row - high
    matrix_ref[...] = work_ref[...].astype(BF16)
    radii = lane_radii(first, local)
    drive = field_ref[0] * radii
    for power in range(1, ORDER + 1):
        mix(coupling_ref, stack_ref, mixed_ref, (1,) if power == 1 else (0, 1, 2))
        stencil(stack_ref, matrix_ref, moved_ref)
        advance(v_ref, state_ref, stack_ref, mixed_ref, moved_ref, pot_ref, drive, time_step / power)
    split_store(stack_ref, 0, state_ref[...])
    mix(coupling_ref, stack_ref, mixed_ref, (0, 1, 2))
    part_ref[...] = jnp.zeros(part_ref.shape, F32)
    for n, value in ((0, part_in_ref[0:1, :]), (1, intersect(state_ref, mixed_ref, radii))):
        whole = jnp.sum(value, axis=1, keepdims=True) * scaling
        part_ref[n : n + 1, :] = jnp.broadcast_to(whole, (1, local))
    v_ref[...] = state_ref[...]


def later_kernel(
    first_ref,
    field_ref,
    after_ref,
    matrix_ref,
    coupling_ref,
    pot_ref,
    v_in_ref,
    stack_in_ref,
    mixed_in_ref,
    total_in_ref,
    v_ref,
    stack_ref,
    mixed_ref,
    total_ref,
    kept_ref,
    moved_ref,
    *,
    power,
):
    del v_in_ref, stack_in_ref, mixed_in_ref, total_in_ref
    kept_ref[...] = after_ref[...]
    radii = lane_radii(first_ref[0], 128)
    drive = field_ref[1] * radii
    stencil(stack_ref, matrix_ref, moved_ref)
    advance(v_ref, total_ref, stack_ref, mixed_ref, moved_ref, pot_ref, drive, time_step / power)
    mix(coupling_ref, stack_ref, mixed_ref, (0, 1, 2) if power + 1 < ORDER else (0, 2))


def last_kernel(
    first_ref,
    field_ref,
    after_ref,
    matrix_ref,
    pot_ref,
    v_ref,
    stack_ref,
    mixed_ref,
    total_ref,
    out_ref,
    moved_ref,
):
    del after_ref
    local = 128
    radii = lane_radii(first_ref[0], local)
    drive = field_ref[1] * radii
    stencil(stack_ref, matrix_ref, moved_ref)
    channels = v_ref.shape[0]
    scale = time_step / ORDER
    for c0 in range(0, channels, 80):
        rows = slice(c0, c0 + 80)
        for source, target, sign in ((1, 0, 1.0), (0, 1, -1.0), (3, 2, 1.0), (2, 3, -1.0)):
            cut = slice(OWN[PARTS[source]], OWN[PARTS[source]] + local)
            into = slice(OWN[PARTS[target]], OWN[PARTS[target]] + local)
            value = (
                KIN * moved_ref[source, rows, :local]
                + pot_ref[rows, :local] * v_ref[rows, cut]
                + drive[:, :local] * mixed_ref[rows, cut]
            )
            out_ref[target, rows, :] = total_ref[rows, into] + (sign * scale) * value


def tree(count):
    if count == 16:
        return [[2], [4, 8, 12]]
    return [[1 << k] for k in range(1, (count - 1).bit_length())]


def swaps(start, count):
    return [(start + i, 1 - 2 * (i % 2)) for i in range(count)]


def vmem(count):
    return [pl.BlockSpec(memory_space=pltpu.VMEM)] * count


def smem(count):
    return [pl.BlockSpec(memory_space=pltpu.SMEM)] * count


def params():
    return pltpu.CompilerParams(vmem_limit_bytes=32 * 1024 * 1024)


def per_device(states, dipole, pattern, angular, thresholds, surface_profile, pulse_field, *, count):
    channels, local = states.shape[1:]
    grid_points = local * count
    half = channels // 2
    axis = "radius"
    here = lax.axis_index(axis)
    first = (here * local).reshape(1).astype(jnp.int32)
    shape = jax.ShapeDtypeStruct
    width = 6 * local
    scaling = 1.0 / (math.sqrt(channels * grid_points) * (inner_radius + grid_points * spacing))

    near, far, inner = pl.pallas_call(
        pack_kernel,
        out_shape=(
            shape((half + 8, local), F32),
            shape((half + 8, local), F32),
            shape((half + 40, local), F32),
        ),
        in_specs=smem(1) + [pl.BlockSpec(memory_space=pltpu.HBM)] * 2,
        out_specs=tuple(vmem(3)),
        scratch_shapes=[
            pltpu.VMEM(states.shape, F32),
            pltpu.VMEM(surface_profile.shape, F32),
            pltpu.SemaphoreType.DMA((5,)),
        ],
        compiler_params=params(),
        name="pack",
    )(
        first,
        pltpu.with_memory_space_constraint(states, pltpu.HBM),
        pltpu.with_memory_space_constraint(surface_profile, pltpu.HBM),
    )

    coupling, kinetic, pot, v, stack, mixed, part = pl.pallas_call(
        functools.partial(table_kernel, grid_points=grid_points),
        out_shape=(
            shape((channels, 3 * channels), BF16),
            shape((2, 2 * local, 2 * local), F32),
            shape((channels, 2 * local), F32),
            shape((channels, width), F32),
            shape((3 * channels, width), BF16),
            shape((channels, width), F32),
            shape((8, local), F32),
        ),
        in_specs=smem(1) + vmem(5),
        out_specs=tuple(vmem(7)),
        compiler_params=params(),
        name="tables",
    )(first, dipole, pattern, angular.reshape(1, channels), thresholds.reshape(1, channels), states)

    far = lax.ppermute(far, axis, [(i, i + d) for i, d in swaps(1, count - 2)])
    have = [0]
    for offsets in tree(count):
        fresh, chosen = [], inner
        for offset in offsets:
            pairs = [(h, h + offset) for h in have if h + offset < count]
            got = lax.ppermute(inner, axis, pairs)
            to = [p[1] for p in pairs]
            hit = functools.reduce(jnp.logical_or, [here == t for t in to])
            chosen = jnp.where(hit, got, chosen)
            fresh += to
        if len(have) == 1:
            chosen, far = lax.optimization_barrier((chosen, far))
        inner = chosen
        have += fresh
    sent = jnp.concatenate([inner, near])
    got = lax.ppermute(sent, axis, [(i, i + d) for i, d in swaps(0, count)])

    moved = pltpu.VMEM((4, channels, 2 * local), F32)
    evolved = (
        shape((channels, width), F32),
        shape((3 * channels, width), BF16),
        shape((channels, width), F32),
        shape((channels, width), F32),
    )
    v, stack, mixed, total, matrix, part = pl.pallas_call(
        functools.partial(first_kernel, scaling=scaling),
        out_shape=evolved + (shape((2, 2 * local, 2 * local), BF16), shape((8, local), F32)),
        in_specs=smem(2) + vmem(11),
        out_specs=tuple(vmem(6)),
        scratch_shapes=[moved, pltpu.VMEM((2, 2 * local, 2 * local), F32)],
        input_output_aliases={10: 0, 11: 1, 12: 2},
        compiler_params=params(),
        name="first",
    )(first, pulse_field, far, got, sent, surface_profile, coupling, kinetic, pot, part, v, stack, mixed)

    rounds = (count - 1).bit_length()
    for power in range(1, ORDER + 1):
        low, high = rounds * (power - 1) // ORDER, rounds * power // ORDER
        before = part
        for bit in range(low, high - 1):
            before = before + lax.ppermute(before, axis, [(i, i ^ (1 << bit)) for i in range(count)])
        got = lax.ppermute(before, axis, [(i, i ^ (1 << (high - 1))) for i in range(count)])
        if power < ORDER:
            v, stack, mixed, total, kept = pl.pallas_call(
                functools.partial(later_kernel, power=power),
                out_shape=evolved + (shape(part.shape, F32),),
                in_specs=smem(2) + vmem(8),
                out_specs=tuple(vmem(5)),
                scratch_shapes=[moved],
                input_output_aliases={6: 0, 7: 1, 8: 2, 9: 3},
                compiler_params=params(),
                name="later",
            )(first, pulse_field, before, matrix, coupling, pot, v, stack, mixed, total)
            part = kept + got
        else:
            final = pl.pallas_call(
                last_kernel,
                out_shape=shape(states.shape, F32),
                in_specs=smem(2) + vmem(7),
                out_specs=vmem(1)[0],
                scratch_shapes=[moved],
                compiler_params=params(),
                name="last",
            )(first, pulse_field, before, matrix, pot, v, stack, mixed, total)
            part = before + got
    return final, part[:STEPS, 0]


def solution(mesh):
    return jax.shard_map(
        functools.partial(per_device, count=mesh.shape["radius"]),
        mesh=mesh,
        in_specs=(P("groups", None, "radius"), P(), P(), P(), P(), P(None, "radius"), P("groups")),
        out_specs=(P("groups", None, "radius"), P("groups")),
        check_vma=False,
    )
```

time: 61.7 us -> 49.9 us (0.81)
  waiting for transfers between devices: 19.9 us -> 7.26 us
  Pallas kernels: 19 us -> 22.8 us
  local copies, waits for them, and re-layouts: 1.85 us -> 0.66 us
  starting transfers between devices: 19 us -> 17.9 us
  other arithmetic: 0.78 us -> 0.08 us
    ppermute x11 -> x10, waiting for transfers between devices: 19.9 us -> 7.26 us  [the longest x4 5.83 us: per_device(): got = lax.ppermute(inner, axis, pairs)]
    unnamed x18 -> x14, local copies, waits for them, and re-layouts: 1.85 us -> 0.03 us
    pallas_call x2 -> x5, Pallas kernels: 17.3 us -> 19.1 us  [the longest x1 9.13 us: per_device(): pl.pallas_call(functools.partial(first_kernel, scaling=scaling), out_shap...]
    pallas_call x1, Pallas kernels: 0.81 us -> 2.18 us  [per_device(): pl.pallas_call(pack_kernel, out_shape=(shape((half + 8, local), F32), sha...]
    ppermute x11 -> x10, starting transfers between devices: 19 us -> 17.9 us  [the longest x4 11.8 us: per_device(): got = lax.ppermute(inner, axis, pairs)]
    pallas_call x1, Pallas kernels: 0.84 us -> 1.49 us  [per_device(): pl.pallas_call(functools.partial(table_kernel, grid_points=grid_points),...]
    slice x0 -> x1, local copies, waits for them, and re-layouts: none -> 0.63 us  [per_device(): return (final, part[:STEPS, 0])]
  transfers between devices with their start and end apart: 11 -> 10, of which waited for: 8 -> 4; matrix products, arithmetic and copies ran while one was open for 0% -> 0% of each run, Pallas kernels for 14% -> 23%
where the time goes in v2:
time: 49.9 us; the launch traced here: 49.6 us
  Pallas kernels  22.8 us (46%)
  starting transfers between devices  17.9 us (36%)
  waiting for transfers between devices  7.26 us (15%)
  between operations  0.93 us (2%)
  local copies, waits for them, and re-layouts  0.66 us (1%)
    ppermute x4, starting transfers between devices, per_device(): got = lax.ppermute(inner, axis, pairs)  11.8 us
    pallas_call x1, Pallas kernels, per_device(): pl.pallas_call(functools.partial(first_kernel, scaling=scaling), out_shap...  9.13 us
    pallas_call x3, Pallas kernels, per_device(): pl.pallas_call(functools.partial(later_kernel, power=power), out_shape=ev...  7.92 us
    ppermute x4, waiting for transfers between devices, per_device(): got = lax.ppermute(inner, axis, pairs)  5.83 us
    ppermute x4, starting transfers between devices, per_device(): lax.ppermute(before, axis, [(i, i ^ 1 << high - 1) for i in range(count)])  5.33 us
    pallas_call x1, Pallas kernels, per_device(): pl.pallas_call(pack_kernel, out_shape=(shape((half + 8, local), F32), sha...  2.18 us
    pallas_call x1, Pallas kernels, per_device(): pl.pallas_call(last_kernel, out_shape=shape(states.shape, F32), in_specs=...  2.07 us
    pallas_call x1, Pallas kernels, per_device(): pl.pallas_call(functools.partial(table_kernel, grid_points=grid_points),...  1.49 us
  transfers between devices with their start and end apart: 10, of which 4 were waited for; matrix products, arithmetic and copies ran while one was open for 0% of the time, Pallas kernels for 23%

profile of v2, /device:TPU:0, one launch (start us, length us, event | category | flops | bytes accessed | tf_op | source)
XLA Modules:
  0.0 49.6 jit_solution(13278287149040085008)
XLA Ops:
  0.7 2.2 %pack.1 = (f32[208,128]{1,0:T(8,128)S(1)}, f32[208,128]{1,0:T(8,128)S(1)}, f32[240,128]{1,0:T(8,128)S(1)}) custom-call(s32[1]{0:T(128)} %bitcast.first_ref, f32[4,400,128]{2,1,0:T(8,128)} %states_ref.1, f32[2,128]{1,0:T(2,128)} %profile_ref.1), custom_call_target="tpu_custom_call" | custom-call | tf_op jit(solution)/shard_map/pack/pallas_call | solution.py:466
  2.9 4.9 %collective-permute-start = (f32[240,128]{1,0:T(8,128)S(1)}, f32[240,128]{1,0:T(8,128)S(1)}, u32[]{:S(2)}, u32[]{:S(2)}) collective-permute-start(f32[240,128]{1,0:T(8,128)S(1)} %get-tuple-element.35), channel_id=1, source_target_pairs={{0,2},{16,18}} | collective-permute-start | bytes 368648 | tf_op jit(solution)/shard_map/ppermute | solution.py:511
  7.8 0.7 %collective-permute-start.1 = (f32[208,128]{1,0:T(8,128)S(1)}, f32[208,128]{1,0:T(8,128)S(1)}, u32[]{:S(2)}, u32[]{:S(2)}) collective-permute-start(f32[208,128]{1,0:T(8,128)S(1)} %get-tuple-element.36), channel_id=1, source_target_pairs={{1,2},{2,1},{3,4},{4,3},{5,6},{6,5},{7,8},{8,7},{9,10},{10,9},{11,... | collective-permute-start | bytes 319496 | tf_op jit(solution)/shard_map/ppermute | solution.py:505
  8.4 3.5 %collective-permute-done = f32[240,128]{1,0:T(8,128)S(1)} collective-permute-done((f32[240,128]{1,0:T(8,128)S(1)}, f32[240,128]{1,0:T(8,128)S(1)}, u32[]{:S(2)}, u32[]{:S(2)}) %collective-permute-start) | collective-permute-done | bytes 122912 | tf_op jit(solution)/shard_map/ppermute | solution.py:511
  11.9 3.6 %collective-permute-start.4 = (f32[240,128]{1,0:T(8,128)S(1)}, f32[240,128]{1,0:T(8,128)S(1)}, u32[]{:S(2)}, u32[]{:S(2)}) collective-permute-start(f32[240,128]{1,0:T(8,128)S(1)} %broadcast_select_fusion), channel_id=1, source_target_pairs={{0,4},{2,6},{16,20},{18,22}} | collective-permute-start | bytes 368648 | tf_op jit(solution)/shard_map/ppermute | solution.py:511
  15.5 1.7 %collective-permute-start.3 = (f32[240,128]{1,0:T(8,128)S(1)}, f32[240,128]{1,0:T(8,128)S(1)}, u32[]{:S(2)}, u32[]{:S(2)}) collective-permute-start(f32[240,128]{1,0:T(8,128)S(1)} %broadcast_select_fusion), channel_id=1, source_target_pairs={{0,8},{2,10},{16,24},{18,26}} | collective-permute-start | bytes 368648 | tf_op jit(solution)/shard_map/ppermute | solution.py:511
  17.2 1.7 %collective-permute-start.2 = (f32[240,128]{1,0:T(8,128)S(1)}, f32[240,128]{1,0:T(8,128)S(1)}, u32[]{:S(2)}, u32[]{:S(2)}) collective-permute-start(f32[240,128]{1,0:T(8,128)S(1)} %broadcast_select_fusion), channel_id=1, source_target_pairs={{0,12},{2,14},{16,28},{18,30}} | collective-permute-start | bytes 368648 | tf_op jit(solution)/shard_map/ppermute | solution.py:511
  18.9 0.0 copy-start.3
  18.9 0.0 copy-start.4
  18.9 0.7 %collective-permute-done.3 = f32[240,128]{1,0:T(8,128)S(1)} collective-permute-done((f32[240,128]{1,0:T(8,128)S(1)}, f32[240,128]{1,0:T(8,128)S(1)}, u32[]{:S(2)}, u32[]{:S(2)}) %collective-permute-start.3) | collective-permute-done | bytes 122912 | tf_op jit(solution)/shard_map/ppermute | solution.py:511
  19.6 1.7 %collective-permute-done.2 = f32[240,128]{1,0:T(8,128)S(1)} collective-permute-done((f32[240,128]{1,0:T(8,128)S(1)}, f32[240,128]{1,0:T(8,128)S(1)}, u32[]{:S(2)}, u32[]{:S(2)}) %collective-permute-start.2) | collective-permute-done | bytes 122912 | tf_op jit(solution)/shard_map/ppermute | solution.py:511
  21.4 0.1 collective-permute-start.5
  21.5 1.5 %tables.1 = (bf16[400,1200]{1,0:T(8,128)(2,1)S(1)}, f32[2,256,256]{2,1,0:T(8,128)S(1)}, f32[400,256]{1,0:T(8,128)S(1)}, f32[400,768]{1,0:T(8,128)S(1)}, bf16[120...) custom-call(s32[1]{0:T(128)} %bitcast.first_ref, f32[400,400]{1,0:T(8,128)S(1)} %copy-done.1, ...), custom_call_target="tpu_custom_call" | custom-call | tf_op jit(solution)/shard_map/tables/pallas_call | solution.py:488
  23.0 9.1 %first.1 = (f32[400,768]{1,0:T(8,128)S(1)}, bf16[1200,768]{1,0:T(8,128)(2,1)S(1)}, f32[400,768]{1,0:T(8,128)S(1)}, f32[400,768]{1,0:T(8,128)S(1)}, bf16[2,256,25...) custom-call(s32[1]{0:T(128)} %bitcast.first_ref, ...), custom_call_target="tpu_custom_call", output_to_operand_aliasing={{0}: (10, {}), {1}: (11, {}), {2}: (12, {})} | custom-call | tf_op jit(solution)/shard_map/first/pallas_call | solution.py:530
  32.2 0.5 collective-permute-start.6
  32.6 2.9 %later.3 = (f32[400,768]{1,0:T(8,128)S(1)}, bf16[1200,768]{1,0:T(8,128)(2,1)S(1)}, f32[400,768]{1,0:T(8,128)S(1)}, f32[400,768]{1,0:T(8,128)S(1)}, f32[8,128]{1,0:T(8,128)S(1)}) custom-call(s32[1]{0:T(128)} %bitcast.first_ref, f32[2]{0:T(128)S(1)} %copy-done.3, ...), custom_call_target="tpu_custom_call", output_to_operand_aliasing={{0}: (6, {}), {1}: (7, {}), {2}: (8, {}), {3}: (9, {})} | custom-call | tf_op jit(solution)/shard_map/later/pallas_call | solution.py:549
  35.5 1.3 %collective-permute-start.7 = (f32[8,128]{1,0:T(8,128)S(1)}, f32[8,128]{1,0:T(8,128)S(1)}, u32[]{:S(2)}, u32[]{:S(2)}) collective-permute-start(f32[8,128]{1,0:T(8,128)S(1)} %add.12.after_ref), channel_id=1, source_target_pairs={{0,2},{1,3},{2,0},{3,1},{4,6},{5,7},{6,4},{7,5},{8,10},{9,11},{10,... | collective-permute-start | bytes 12296 | tf_op jit(solution)/shard_map/ppermute | solution.py:547
  36.9 2.9 %later.4 = (f32[400,768]{1,0:T(8,128)S(1)}, bf16[1200,768]{1,0:T(8,128)(2,1)S(1)}, f32[400,768]{1,0:T(8,128)S(1)}, f32[400,768]{1,0:T(8,128)S(1)}, f32[8,128]{1,0:T(8,128)S(1)}) custom-call(s32[1]{0:T(128)} %bitcast.first_ref, f32[2]{0:T(128)S(1)} %copy-done.3, ...), custom_call_target="tpu_custom_call", output_to_operand_aliasing={{0}: (6, {}), {1}: (7, {}), {2}: (8, {}), {3}: (9, {})} | custom-call | tf_op jit(solution)/shard_map/later/pallas_call | solution.py:549
  39.8 0.1 collective-permute-start.8
  39.8 2.2 %later.5 = (f32[400,768]{1,0:T(8,128)S(1)}, bf16[1200,768]{1,0:T(8,128)(2,1)S(1)}, f32[400,768]{1,0:T(8,128)S(1)}, f32[400,768]{1,0:T(8,128)S(1)}, f32[8,128]{1,0:T(8,128)S(1)}) custom-call(s32[1]{0:T(128)} %bitcast.first_ref, f32[2]{0:T(128)S(1)} %copy-done.3, ...), custom_call_target="tpu_custom_call", output_to_operand_aliasing={{0}: (6, {}), {1}: (7, {}), {2}: (8, {}), {3}: (9, {})} | custom-call | tf_op jit(solution)/shard_map/later/pallas_call | solution.py:549
  42.0 1.4 %collective-permute-done.8 = f32[8,128]{1,0:T(8,128)S(1)} collective-permute-done((f32[8,128]{1,0:T(8,128)S(1)}, f32[8,128]{1,0:T(8,128)S(1)}, u32[]{:S(2)}, u32[]{:S(2)}) %collective-permute-start.8) | collective-permute-done | bytes 4128 | tf_op jit(solution)/shard_map/ppermute | solution.py:547
  43.4 3.5 %collective-permute-start.9 = (f32[8,128]{1,0:T(8,128)S(1)}, f32[8,128]{1,0:T(8,128)S(1)}, u32[]{:S(2)}, u32[]{:S(2)}) collective-permute-start(f32[8,128]{1,0:T(8,128)S(1)} %add.14.after_ref), channel_id=1, source_target_pairs={{0,8},{1,9},{2,10},{3,11},{4,12},{5,13},{6,14},{7,15},{8,0},{9,1},... | collective-permute-start | bytes 12296 | tf_op jit(solution)/shard_map/ppermute | solution.py:547
  46.9 2.1 %last.1 = f32[4,400,128]{2,1,0:T(8,128)} custom-call(s32[1]{0:T(128)} %bitcast.first_ref, f32[2]{0:T(128)S(1)} %copy-done.3, f32[8,128]{1,0:T(8,128)S(1)} %add.14.after_ref, bf16[2,256,256]{2,1,0:T(8,128)(2,1)S(1)} %get-tuple-element.48.matrix_ref, f32[400,256]{1,0:T(8,128)S(1)} %get-tuple-element.42.pot_ref, f32[400,768]{1,0:T(8,128)S(1)} %get-tuple-element.64.v_ref, ...), custom_call_target="tpu_custom_call" | custom-call | tf_op jit(solution)/shard_map/last/pallas_call | solution.py:561
  49.0 0.6 %slice_reduce_fusion = f32[2]{0:T(128)} fusion(f32[8,128]{1,0:T(8,128)S(1)} %add.15), kind=kLoop, calls=%fused_computation.3 | loop fusion | bytes 16 | tf_op jit(solution)/shard_map/slice | solution.py:571
  (25 shorter events, 0.1 us)
Async XLA Ops:
  0.6 20.8 %copy-start = (f32[4,400,128]{2,1,0:T(8,128)S(1)}, f32[4,400,128]{2,1,0:T(8,128)}, u32[]{:S(2)}) copy-start(f32[4,400,128]{2,1,0:T(8,128)} %states_ref.1) | copy-start | bytes 2457604
  0.6 20.8 %copy-start.6 = (f32[400]{0:T(512)S(1)}, f32[400]{0:T(512)}, u32[]{:S(2)}) copy-start(f32[400]{0:T(512)} %param.11) | copy-start | bytes 4804
  0.7 20.8 %copy-start.5 = (s32[400]{0:T(512)S(1)}, s32[400]{0:T(512)}, u32[]{:S(2)}) copy-start(s32[400]{0:T(512)} %param.10) | copy-start | bytes 4804
  0.7 20.8 %copy-start.2 = (s32[25,25]{1,0:T(8,128)S(1)}, s32[25,25]{1,0:T(8,128)}, u32[]{:S(2)}) copy-start(s32[25,25]{1,0:T(8,128)} %pattern_ref.1) | copy-start | bytes 7504
  0.7 20.8 %copy-start.1 = (f32[400,400]{1,0:T(8,128)S(1)}, f32[400,400]{1,0:T(8,128)}, u32[]{:S(2)}) copy-start(f32[400,400]{1,0:T(8,128)} %dipole_ref.1) | copy-start | bytes 1920004
  2.9 9.0 %collective-permute-start = (f32[240,128]{1,0:T(8,128)S(1)}, f32[240,128]{1,0:T(8,128)S(1)}, u32[]{:S(2)}, u32[]{:S(2)}) collective-permute-start(f32[240,128]{1,0:T(8,128)S(1)} %get-tuple-element.35), channel_id=1, source_target_pairs={{0,2},{16,18}} | collective-permute-start | bytes 368648 | tf_op jit(solution)/shard_map/ppermute | solution.py:511
  7.8 4.2 %collective-permute-start.1 = (f32[208,128]{1,0:T(8,128)S(1)}, f32[208,128]{1,0:T(8,128)S(1)}, u32[]{:S(2)}, u32[]{:S(2)}) collective-permute-start(f32[208,128]{1,0:T(8,128)S(1)} %get-tuple-element.36), channel_id=1, source_target_pairs={{1,2},{2,1},{3,4},{4,3},{5,6},{6,5},{7,8},{8,7},{9,10},{10,9},{11,... | collective-permute-start | bytes 319496 | tf_op jit(solution)/shard_map/ppermute | solution.py:505
  11.9 7.0 %collective-permute-start.4 = (f32[240,128]{1,0:T(8,128)S(1)}, f32[240,128]{1,0:T(8,128)S(1)}, u32[]{:S(2)}, u32[]{:S(2)}) collective-permute-start(f32[240,128]{1,0:T(8,128)S(1)} %broadcast_select_fusion), channel_id=1, source_target_pairs={{0,4},{2,6},{16,20},{18,22}} | collective-permute-start | bytes 368648 | tf_op jit(solution)/shard_map/ppermute | solution.py:511
  15.5 4.1 %collective-permute-start.3 = (f32[240,128]{1,0:T(8,128)S(1)}, f32[240,128]{1,0:T(8,128)S(1)}, u32[]{:S(2)}, u32[]{:S(2)}) collective-permute-start(f32[240,128]{1,0:T(8,128)S(1)} %broadcast_select_fusion), channel_id=1, source_target_pairs={{0,8},{2,10},{16,24},{18,26}} | collective-permute-start | bytes 368648 | tf_op jit(solution)/shard_map/ppermute | solution.py:511
  17.2 4.1 %collective-permute-start.2 = (f32[240,128]{1,0:T(8,128)S(1)}, f32[240,128]{1,0:T(8,128)S(1)}, u32[]{:S(2)}, u32[]{:S(2)}) collective-permute-start(f32[240,128]{1,0:T(8,128)S(1)} %broadcast_select_fusion), channel_id=1, source_target_pairs={{0,12},{2,14},{16,28},{18,30}} | collective-permute-start | bytes 368648 | tf_op jit(solution)/shard_map/ppermute | solution.py:511
  18.9 4.1 %copy-start.3 = (f32[2]{0:T(128)S(1)}, f32[2]{0:T(128)}, u32[]{:S(2)}) copy-start(f32[2]{0:T(128)} %field_ref.9) | copy-start | bytes 28
  18.9 4.1 %copy-start.4 = (f32[2,128]{1,0:T(2,128)S(1)}, f32[2,128]{1,0:T(2,128)}, u32[]{:S(2)}) copy-start(f32[2,128]{1,0:T(2,128)} %profile_ref.1) | copy-start | bytes 3076
  21.4 1.6 %collective-permute-start.5 = (f32[448,128]{1,0:T(8,128)S(1)}, f32[448,128]{1,0:T(8,128)S(1)}, u32[]{:S(2)}, u32[]{:S(2)}) collective-permute-start(f32[448,128]{1,0:T(8,128)S(1)} %pad_maximum_fusion.sent_ref), channel_id=1, source_target_pairs={{0,1},{1,0},{2,3},{3,2},{4,5},{5,4},{6,7},{7,6},{8,9},{9,8},{10,11... | collective-permute-start | bytes 688136 | tf_op jit(solution)/shard_map/ppermute | solution.py:521
  32.2 3.4 %collective-permute-start.6 = (f32[8,128]{1,0:T(8,128)S(1)}, f32[8,128]{1,0:T(8,128)S(1)}, u32[]{:S(2)}, u32[]{:S(2)}) collective-permute-start(f32[8,128]{1,0:T(8,128)S(1)} %get-tuple-element.47.after_ref), channel_id=1, source_target_pairs={{0,1},{1,0},{2,3},{3,2},{4,5},{5,4},{6,7},{7,6},{8,9},{9,8},{10,11... | collective-permute-start | bytes 12296 | tf_op jit(solution)/shard_map/ppermute | solution.py:547
  35.5 4.2 %collective-permute-start.7 = (f32[8,128]{1,0:T(8,128)S(1)}, f32[8,128]{1,0:T(8,128)S(1)}, u32[]{:S(2)}, u32[]{:S(2)}) collective-permute-start(f32[8,128]{1,0:T(8,128)S(1)} %add.12.after_ref), channel_id=1, source_target_pairs={{0,2},{1,3},{2,0},{3,1},{4,6},{5,7},{6,4},{7,5},{8,10},{9,11},{10,... | collective-permute-start | bytes 12296 | tf_op jit(solution)/shard_map/ppermute | solution.py:547
  39.8 3.7 %collective-permute-start.8 = (f32[8,128]{1,0:T(8,128)S(1)}, f32[8,128]{1,0:T(8,128)S(1)}, u32[]{:S(2)}, u32[]{:S(2)}) collective-permute-start(f32[8,128]{1,0:T(8,128)S(1)} %add.13.after_ref), channel_id=1, source_target_pairs={{0,4},{1,5},{2,6},{3,7},{4,0},{5,1},{6,2},{7,3},{8,12},{9,13},{10,... | collective-permute-start | bytes 12296 | tf_op jit(solution)/shard_map/ppermute | solution.py:547
  43.4 5.5 %collective-permute-start.9 = (f32[8,128]{1,0:T(8,128)S(1)}, f32[8,128]{1,0:T(8,128)S(1)}, u32[]{:S(2)}, u32[]{:S(2)}) collective-permute-start(f32[8,128]{1,0:T(8,128)S(1)} %add.14.after_ref), channel_id=1, source_target_pairs={{0,8},{1,9},{2,10},{3,11},{4,12},{5,13},{6,14},{7,15},{8,0},{9,1},... | collective-permute-start | bytes 12296 | tf_op jit(solution)/shard_map/ppermute | solution.py:547

commit v3 on v2

--- a/solution.py
+++ b/solution.py
@@ -24,7 +24,7 @@
 F32 = jnp.float32
 BF16 = jnp.bfloat16
 
-OWN = {"a": 0, "c": 128, "b": 512, "d": 640}
+OWN = {"a": 0, "b": 128, "c": 512, "d": 640}
 EXTRA = {"a": 256, "c": 256, "b": 384, "d": 384}
 PARTS = ("a", "b", "c", "d")
 
@@ -126,7 +126,6 @@
     coupling_ref,
     kinetic_ref,
     pot_ref,
-    v_ref,
     stack_ref,
     mixed_ref,
     part_ref,
@@ -172,11 +171,9 @@
         mine = mine & ((dst < local) | ((dst - local) // 64 == which))
         kinetic_ref[which] = jnp.where(mine, coef, 0.0)
     for k, part in enumerate(PARTS):
-        at = OWN[part]
-        v_ref[:, at : at + local] = states_ref[k]
-        split_store(stack_ref, at, states_ref[k])
+        split_store(stack_ref, OWN[part], states_ref[k])
     mix(coupling_ref, stack_ref, mixed_ref, (0, 2))
-    part_ref[0:1, :] = intersect(v_ref, mixed_ref, radii)
+    part_ref[0:1, :] = intersect(states_ref[2], states_ref[3], mixed_ref, radii)
     part_ref[1:, :] = jnp.zeros((part_ref.shape[0] - 1, local), F32)
 
 
@@ -196,9 +193,9 @@
         mixed_ref[:, cut] = jnp.dot(coupling_ref[...], stack_ref[:, cut], preferred_element_type=F32)
 
 
-def stencil(stack_ref, matrix_ref, moved_ref):
+def stencil(stack_ref, matrix_ref, moved_ref, parts):
     channels = stack_ref.shape[0] // 3
-    for k, part in enumerate(PARTS):
+    for part in parts:
         own, extra = OWN[part], EXTRA[part]
         weights = matrix_ref[0 if part in "ab" else 1]
         total = None
@@ -206,50 +203,48 @@
             left = jnp.concatenate([stack_ref[rows, own : own + 128], stack_ref[rows, extra : extra + 128]], axis=1)
             got = jnp.dot(left, weights, preferred_element_type=F32)
             total = got if total is None else total + got
-        moved_ref[k] = total
-
-
-def advance(v_ref, total_ref, stack_ref, mixed_ref, moved_ref, pot_ref, drive, scale, own_only=False, chunk=80):
-    channels = v_ref.shape[0]
-    local = 128
+        moved_ref[PARTS.index(part)] = total
+
+
+def advance(targets, old, keep, mixed_ref, moved_ref, pot_ref, drive, scale, chunk=80):
+    channels, local = pot_ref.shape[0], 128
+    own, extra = slice(0, local), slice(local, 2 * local)
     for c0 in range(0, channels, chunk):
         rows = slice(c0, c0 + chunk)
-        pot_own, pot_extra = pot_ref[rows, :local], pot_ref[rows, local:]
-        drive_own, drive_extra = drive[:, :local], drive[:, local:]
-
-        def hamiltonian(at, moved, pot, force):
-            cut = slice(at, at + local)
-            return KIN * moved + pot * v_ref[rows, cut] + force * mixed_ref[rows, cut]
-
-        new = {}
-        for source, target, sign in ((1, "a", 1.0), (0, "b", -1.0), (3, "c", 1.0), (2, "d", -1.0)):
-            part = PARTS[source]
-            new[OWN[target]] = (sign * scale) * hamiltonian(
-                OWN[part], moved_ref[source, rows, :local], pot_own, drive_own
+        for target in targets:
+            sign = 1.0 if target in ("a", "c", "ac") else -1.0
+            if len(target) == 1:
+                source = {"a": "b", "b": "a", "c": "d", "d": "c"}[target]
+                to, at, lanes = OWN[target], OWN[source], own
+                moved = moved_ref[PARTS.index(source), rows, own]
+            else:
+                k, m = (1, 3) if target == "ac" else (0, 2)
+                to, at, lanes = EXTRA[target[0]], EXTRA[PARTS[k]], extra
+                moved = moved_ref[k, rows, extra] + moved_ref[m, rows, extra]
+            factor = sign * scale
+            value = (
+                (factor * KIN) * moved
+                + (factor * pot_ref[rows, lanes]) * old(at, rows)
+                + (factor * drive[:, lanes]) * mixed_ref[rows, at : at + local]
             )
-        if not own_only:
-            for source, target, sign in (("b", "a", 1.0), ("a", "b", -1.0)):
-                k = PARTS.index(source)
-                moved = moved_ref[k, rows, local:] + moved_ref[k + 2, rows, local:]
-                new[EXTRA[target]] = (sign * scale) * hamiltonian(EXTRA[source], moved, pot_extra, drive_extra)
-        for at, value in new.items():
-            cut = slice(at, at + local)
-            total_ref[rows, cut] = total_ref[rows, cut] + value
-            if own_only:
-                continue
-            v_ref[rows, cut] = value
-            high = value.astype(BF16)
-            low = (value - high.astype(F32)).astype(BF16)
-            stack_ref[c0 : c0 + chunk, cut] = high
-            stack_ref[channels + c0 : channels + c0 + chunk, cut] = low
-            stack_ref[2 * channels + c0 : 2 * channels + c0 + chunk, cut] = high
-
-
-def intersect(state_ref, mixed_ref, radii):
-    def at(ref, part):
-        return ref[:, OWN[part] : OWN[part] + 128]
-
-    both = at(state_ref, "c") * at(mixed_ref, "b") - at(state_ref, "d") * at(mixed_ref, "a")
+            keep(to, rows, value)
+
+
+def split_rows(stack_ref, at, rows, value):
+    channels = stack_ref.shape[0] // 3
+    high = value.astype(BF16)
+    low = (value - high.astype(F32)).astype(BF16)
+    cut = slice(at, at + value.shape[1])
+    stack_ref[rows, cut] = high
+    stack_ref[channels + rows.start : channels + rows.stop, cut] = low
+    stack_ref[2 * channels + rows.start : 2 * channels + rows.stop, cut] = high
+
+
+def intersect(third, fourth, mixed_ref, radii):
+    def mixed(part):
+        return mixed_ref[:, OWN[part] : OWN[part] + 128]
+
+    both = third * mixed("b") - fourth * mixed("a")
     return jnp.sum(both * radii[:, :128], axis=0, keepdims=True)
 
 
@@ -260,25 +255,27 @@
     got_ref,
     sent_ref,
     profile_ref,
+    states_ref,
     coupling_ref,
     kinetic_ref,
     pot_ref,
     part_in_ref,
-    v_in_ref,
     stack_in_ref,
     mixed_in_ref,
-    v_ref,
     stack_ref,
     mixed_ref,
     state_ref,
     matrix_ref,
     part_ref,
+    v_ref,
+    other_v_ref,
+    other_stack_ref,
     moved_ref,
     work_ref,
     *,
     scaling,
 ):
-    del v_in_ref, stack_in_ref, mixed_in_ref
+    del stack_in_ref, mixed_in_ref
     channels = v_ref.shape[0]
     half = channels // 2
     local = 128
@@ -320,7 +317,6 @@
             value = pltpu.roll(inner[half + 8 : half + 8 + count, :], (48 - 4 * i - 2 * pair) % local, 1)
             hit = (narrow[:count] >= 48) & (narrow[:count] < 50)
             v_ref[rows, at : at + local] = jnp.where(hit, value, v_ref[rows, at : at + local])
-    state_ref[...] = v_ref[...]
     split_store(stack_ref, 256, v_ref[:, 256:512])
     p_own = profile_ref[...]
     lanes2 = iota((2, local), 1)
@@ -355,17 +351,40 @@
     matrix_ref[...] = work_ref[...].astype(BF16)
     radii = lane_radii(first, local)
     drive = field_ref[0] * radii
+    own_at = {OWN[part]: k for k, part in enumerate(PARTS)}
+    vs, stacks = (v_ref, other_v_ref), (stack_ref, other_stack_ref)
     for power in range(1, ORDER + 1):
-        mix(coupling_ref, stack_ref, mixed_ref, (1,) if power == 1 else (0, 1, 2))
-        stencil(stack_ref, matrix_ref, moved_ref)
-        advance(v_ref, state_ref, stack_ref, mixed_ref, moved_ref, pot_ref, drive, time_step / power)
-    split_store(stack_ref, 0, state_ref[...])
-    mix(coupling_ref, stack_ref, mixed_ref, (0, 1, 2))
+        v, stack = vs[1 - power % 2], stacks[1 - power % 2]
+        next_v, next_stack = vs[power % 2], stacks[power % 2]
+
+        def old(at, rows):
+            if power == 1 and at in own_at:
+                return states_ref[own_at[at], rows, :]
+            return v[rows, at : at + local]
+
+        def keep(at, rows, value):
+            cut = slice(at, at + local)
+            before = old(at, rows) if power == 1 else state_ref[rows, cut]
+            state_ref[rows, cut] = before + value
+            if power < ORDER:
+                next_v[rows, cut] = value
+                split_rows(next_stack, at, rows, value)
+            else:
+                split_rows(next_stack, at, rows, before + value)
+
+        scale = time_step / power
+        mix(coupling_ref, stack, mixed_ref, (1,) if power == 1 else (0, 2, 1))
+        stencil(stack, matrix_ref, moved_ref, "ab")
+        advance("ab", old, keep, mixed_ref, moved_ref, pot_ref, drive, scale)
+        stencil(stack, matrix_ref, moved_ref, "cd")
+        advance("cd", old, keep, mixed_ref, moved_ref, pot_ref, drive, scale)
+        advance(("ac", "bd"), old, keep, mixed_ref, moved_ref, pot_ref, drive, scale)
+    mix(coupling_ref, stack_ref, mixed_ref, (0,))
     part_ref[...] = jnp.zeros(part_ref.shape, F32)
-    for n, value in ((0, part_in_ref[0:1, :]), (1, intersect(state_ref, mixed_ref, radii))):
+    state = [state_ref[:, OWN[part] : OWN[part] + local] for part in "cd"]
+    for n, value in ((0, part_in_ref[0:1, :]), (1, intersect(state[0], state[1], mixed_ref, radii))):
         whole = jnp.sum(value, axis=1, keepdims=True) * scaling
         part_ref[n : n + 1, :] = jnp.broadcast_to(whole, (1, local))
-    v_ref[...] = state_ref[...]
 
 
 def later_kernel(
@@ -385,49 +404,97 @@
     total_ref,
     kept_ref,
     moved_ref,
+    now_ref,
     *,
     power,
 ):
-    del v_in_ref, stack_in_ref, mixed_in_ref, total_in_ref
     kept_ref[...] = after_ref[...]
-    radii = lane_radii(first_ref[0], 128)
+    local = 128
+    radii = lane_radii(first_ref[0], local)
     drive = field_ref[1] * radii
-    stencil(stack_ref, matrix_ref, moved_ref)
-    advance(v_ref, total_ref, stack_ref, mixed_ref, moved_ref, pot_ref, drive, time_step / power)
-    mix(coupling_ref, stack_ref, mixed_ref, (0, 1, 2) if power + 1 < ORDER else (0, 2))
-
-
-def last_kernel(
+
+    def old(at, rows):
+        return v_in_ref[rows, at : at + local]
+
+    def keep(at, rows, value):
+        cut = slice(at, at + local)
+        v_ref[rows, cut] = value
+        split_rows(stack_ref, at, rows, value)
+        if at in OWN.values():
+            total_ref[rows, cut] = total_in_ref[rows, cut] + value
+
+    scale = time_step / power
+    mix(coupling_ref, stack_in_ref, now_ref, (2, 1))
+    stencil(stack_in_ref, matrix_ref, moved_ref, "ab")
+    advance("ab", old, keep, mixed_in_ref, moved_ref, pot_ref, drive, scale)
+    stencil(stack_in_ref, matrix_ref, moved_ref, "cd")
+    advance("cd", old, keep, now_ref, moved_ref, pot_ref, drive, scale)
+    advance(("ac", "bd"), old, keep, now_ref, moved_ref, pot_ref, drive, scale)
+    mix(coupling_ref, stack_ref, mixed_ref, (0, 2, 1))
+
+
+def rest_kernel(
     first_ref,
     field_ref,
     after_ref,
     matrix_ref,
+    coupling_ref,
     pot_ref,
+    v_in_ref,
+    stack_in_ref,
+    mixed_in_ref,
+    total_in_ref,
+    out_any,
     v_ref,
+    other_v_ref,
     stack_ref,
+    other_stack_ref,
     mixed_ref,
     total_ref,
-    out_ref,
     moved_ref,
+    sems,
 ):
     del after_ref
     local = 128
     radii = lane_radii(first_ref[0], local)
     drive = field_ref[1] * radii
-    stencil(stack_ref, matrix_ref, moved_ref)
-    channels = v_ref.shape[0]
-    scale = time_step / ORDER
-    for c0 in range(0, channels, 80):
-        rows = slice(c0, c0 + 80)
-        for source, target, sign in ((1, 0, 1.0), (0, 1, -1.0), (3, 2, 1.0), (2, 3, -1.0)):
-            cut = slice(OWN[PARTS[source]], OWN[PARTS[source]] + local)
-            into = slice(OWN[PARTS[target]], OWN[PARTS[target]] + local)
-            value = (
-                KIN * moved_ref[source, rows, :local]
-                + pot_ref[rows, :local] * v_ref[rows, cut]
-                + drive[:, :local] * mixed_ref[rows, cut]
-            )
-            out_ref[target, rows, :] = total_ref[rows, into] + (sign * scale) * value
+    own_at = {OWN[part]: k for k, part in enumerate(PARTS)}
+    vs, stacks = (v_ref, other_v_ref), (stack_ref, other_stack_ref)
+    copies = [pltpu.make_async_copy(total_ref.at[k], out_any.at[k], sems.at[k]) for k in range(4)]
+    for power in range(2, ORDER + 1):
+        v, stack = vs[power % 2], stacks[power % 2]
+        next_v, next_stack = vs[1 - power % 2], stacks[1 - power % 2]
+        if power == 2:
+            v, stack = v_in_ref, stack_in_ref
+        mixed = mixed_in_ref if power == 2 else mixed_ref
+        final = power == ORDER
+
+        def old(at, rows):
+            return v[rows, at : at + local]
+
+        def keep(at, rows, value):
+            cut = slice(at, at + local)
+            if not final:
+                next_v[rows, cut] = value
+                split_rows(next_stack, at, rows, value)
+            if at in own_at:
+                k = own_at[at]
+                before = total_in_ref[rows, cut] if power == 2 else total_ref[k, rows, :]
+                total_ref[k, rows, :] = before + value
+
+        scale = time_step / power
+        if power > 2:
+            mix(coupling_ref, stack, mixed_ref, (0, 2) if final else (0, 2, 1))
+        for pair in ("ab", "cd"):
+            stencil(stack, matrix_ref, moved_ref, pair)
+            advance(pair, old, keep, mixed, moved_ref, pot_ref, drive, scale)
+            if final:
+                for part in pair:
+                    copies[PARTS.index(part)].start()
+        if not final:
+            advance(("ac", "bd"), old, keep, mixed, moved_ref, pot_ref, drive, scale)
+    for copy in copies:
+        copy.wait()
 
 
 def tree(count):
@@ -438,6 +505,13 @@
 
 def swaps(start, count):
     return [(start + i, 1 - 2 * (i % 2)) for i in range(count)]
+
+
+def full_cycle(pairs, count):
+    to = {i: i ^ 1 for i in range(count)}
+    for a, b in pairs:
+        to[a], to[b], to[b ^ 1], to[a ^ 1] = b, b ^ 1, a ^ 1, a
+    return sorted(to.items())
 
 
 def vmem(count):
@@ -485,36 +559,36 @@
         pltpu.with_memory_space_constraint(surface_profile, pltpu.HBM),
     )
 
-    coupling, kinetic, pot, v, stack, mixed, part = pl.pallas_call(
+    coupling, kinetic, pot, stack, mixed, part = pl.pallas_call(
         functools.partial(table_kernel, grid_points=grid_points),
         out_shape=(
             shape((channels, 3 * channels), BF16),
             shape((2, 2 * local, 2 * local), F32),
             shape((channels, 2 * local), F32),
-            shape((channels, width), F32),
             shape((3 * channels, width), BF16),
             shape((channels, width), F32),
             shape((8, local), F32),
         ),
         in_specs=smem(1) + vmem(5),
-        out_specs=tuple(vmem(7)),
+        out_specs=tuple(vmem(6)),
         compiler_params=params(),
         name="tables",
     )(first, dipole, pattern, angular.reshape(1, channels), thresholds.reshape(1, channels), states)
 
     far = lax.ppermute(far, axis, [(i, i + d) for i, d in swaps(1, count - 2)])
-    have = [0]
+    have, far_waits = [0], True
     for offsets in tree(count):
         fresh, chosen = [], inner
         for offset in offsets:
             pairs = [(h, h + offset) for h in have if h + offset < count]
-            got = lax.ppermute(inner, axis, pairs)
+            got = lax.ppermute(inner, axis, full_cycle(pairs, count))
             to = [p[1] for p in pairs]
             hit = functools.reduce(jnp.logical_or, [here == t for t in to])
             chosen = jnp.where(hit, got, chosen)
             fresh += to
-        if len(have) == 1:
+        if len(have) > 1 and far_waits:
             chosen, far = lax.optimization_barrier((chosen, far))
+            far_waits = False
         inner = chosen
         have += fresh
     sent = jnp.concatenate([inner, near])
@@ -527,47 +601,71 @@
         shape((channels, width), F32),
         shape((channels, width), F32),
     )
-    v, stack, mixed, total, matrix, part = pl.pallas_call(
+    stack, mixed, total, matrix, part = pl.pallas_call(
         functools.partial(first_kernel, scaling=scaling),
-        out_shape=evolved + (shape((2, 2 * local, 2 * local), BF16), shape((8, local), F32)),
+        out_shape=evolved[1:] + (shape((2, 2 * local, 2 * local), BF16), shape((8, local), F32)),
         in_specs=smem(2) + vmem(11),
-        out_specs=tuple(vmem(6)),
-        scratch_shapes=[moved, pltpu.VMEM((2, 2 * local, 2 * local), F32)],
-        input_output_aliases={10: 0, 11: 1, 12: 2},
+        out_specs=tuple(vmem(5)),
+        scratch_shapes=[
+            pltpu.VMEM((channels, width), F32),
+            pltpu.VMEM((channels, width), F32),
+            pltpu.VMEM((3 * channels, width), BF16),
+            moved,
+            pltpu.VMEM((2, 2 * local, 2 * local), F32),
+        ],
+        input_output_aliases={11: 0, 12: 1},
         compiler_params=params(),
         name="first",
-    )(first, pulse_field, far, got, sent, surface_profile, coupling, kinetic, pot, part, v, stack, mixed)
-
-    rounds = (count - 1).bit_length()
-    for power in range(1, ORDER + 1):
-        low, high = rounds * (power - 1) // ORDER, rounds * power // ORDER
-        before = part
-        for bit in range(low, high - 1):
-            before = before + lax.ppermute(before, axis, [(i, i ^ (1 << bit)) for i in range(count)])
-        got = lax.ppermute(before, axis, [(i, i ^ (1 << (high - 1))) for i in range(count)])
-        if power < ORDER:
-            v, stack, mixed, total, kept = pl.pallas_call(
-                functools.partial(later_kernel, power=power),
-                out_shape=evolved + (shape(part.shape, F32),),
-                in_specs=smem(2) + vmem(8),
-                out_specs=tuple(vmem(5)),
-                scratch_shapes=[moved],
-                input_output_aliases={6: 0, 7: 1, 8: 2, 9: 3},
-                compiler_params=params(),
-                name="later",
-            )(first, pulse_field, before, matrix, coupling, pot, v, stack, mixed, total)
-            part = kept + got
-        else:
-            final = pl.pallas_call(
-                last_kernel,
-                out_shape=shape(states.shape, F32),
-                in_specs=smem(2) + vmem(7),
-                out_specs=vmem(1)[0],
-                scratch_shapes=[moved],
-                compiler_params=params(),
-                name="last",
-            )(first, pulse_field, before, matrix, pot, v, stack, mixed, total)
-            part = before + got
+    )(first, pulse_field, far, got, sent, surface_profile, states, coupling, kinetic, pot, part, stack, mixed)
+
+    bits = (count - 1).bit_length()
+    groups = [range(low, min(low + 2, bits)) for low in range(0, bits, 2)]
+
+    def send(value, group):
+        low = group[0]
+        return [
+            lax.ppermute(value, axis, [(i, i ^ (pattern << low)) for i in range(count)])
+            for pattern in range(1, 1 << len(group))
+        ]
+
+    def add(value, got):
+        if len(got) == 1:
+            return value + got[0]
+        return (value + got[0]) + (got[1] + got[2])
+
+    got = send(part, groups[0])
+    v, stack, mixed, total, part = pl.pallas_call(
+        functools.partial(later_kernel, power=1),
+        out_shape=evolved + (shape(part.shape, F32),),
+        in_specs=smem(2) + vmem(8),
+        out_specs=tuple(vmem(5)),
+        scratch_shapes=[moved, pltpu.VMEM((channels, width), F32)],
+        compiler_params=params(),
+        name="later",
+    )(first, pulse_field, part, matrix, coupling, pot, total, stack, mixed, total)
+    part = add(part, got)
+    for group in groups[1:-1]:
+        part = add(part, send(part, group))
+    got = send(part, groups[-1])
+    final = pl.pallas_call(
+        rest_kernel,
+        out_shape=shape(states.shape, F32),
+        in_specs=smem(2) + vmem(8),
+        out_specs=pl.BlockSpec(memory_space=pltpu.HBM),
+        scratch_shapes=[
+            pltpu.VMEM((channels, width), F32),
+            pltpu.VMEM((channels, width), F32),
+            pltpu.VMEM((3 * channels, width), BF16),
+            pltpu.VMEM((3 * channels, width), BF16),
+            pltpu.VMEM((channels, width), F32),
+            pltpu.VMEM(states.shape, F32),
+            moved,
+            pltpu.SemaphoreType.DMA((4,)),
+        ],
+        compiler_params=params(),
+        name="rest",
+    )(first, pulse_field, part, matrix, coupling, pot, v, stack, mixed, total)
+    part = add(part, got)
     return final, part[:STEPS, 0]
 
 

time: 49.9 us -> 41.1 us (0.82)
  starting transfers between devices: 17.9 us -> 13 us
  Pallas kernels: 22.8 us -> 19.5 us
    ppermute x8 -> x10, starting transfers between devices: 17.1 us -> 10.7 us  [the longest x6 6.63 us: send(): lax.ppermute(value, axis, [(i, i ^ pattern << low) for i in range(count)])]
    pallas_call x4 -> x2, Pallas kernels: 9.99 us -> 8.04 us  [the longest x1 4.93 us: per_device(): pl.pallas_call(rest_kernel, out_shape=shape(states.shape, F32), in_specs=...]
    ppermute x1, starting transfers between devices: 0.07 us -> 1.69 us  [per_device(): got = lax.ppermute(sent, axis, [(i, i + d) for i, d in swaps(0, count)])]
    pallas_call x1, Pallas kernels: 9.13 us -> 7.87 us  [per_device(): pl.pallas_call(functools.partial(first_kernel, scaling=scaling), out_shap...]
    ppermute x8 -> x10, waiting for transfers between devices: 7.25 us -> 6.78 us  [the longest x4 6.76 us: per_device(): got = lax.ppermute(inner, axis, full_cycle(pairs, count))]
  transfers between devices with their start and end apart: 10 -> 12, of which waited for: 4 -> 4; matrix products, arithmetic and copies ran while one was open for 0% -> 0% of each run, Pallas kernels for 23% -> 23%
where the time goes in v3:
time: 41.1 us; the launch traced here: 40.9 us
  Pallas kernels  19.5 us (47%)
  starting transfers between devices  13 us (32%)
  waiting for transfers between devices  6.78 us (16%)
  between operations  0.87 us (2%)
  local copies, waits for them, and re-layouts  0.68 us (2%)
    pallas_call x1, Pallas kernels, per_device(): pl.pallas_call(functools.partial(first_kernel, scaling=scaling), out_shap...  7.87 us
    ppermute x4, waiting for transfers between devices, per_device(): got = lax.ppermute(inner, axis, full_cycle(pairs, count))  6.76 us
    ppermute x6, starting transfers between devices, send(): lax.ppermute(value, axis, [(i, i ^ pattern << low) for i in range(count)])  6.63 us
    pallas_call x1, Pallas kernels, per_device(): pl.pallas_call(rest_kernel, out_shape=shape(states.shape, F32), in_specs=...  4.93 us
    ppermute x4, starting transfers between devices, per_device(): got = lax.ppermute(inner, axis, full_cycle(pairs, count))  4.04 us
    pallas_call x1, Pallas kernels, per_device(): pl.pallas_call(functools.partial(later_kernel, power=1), out_shape=evolve...  3.11 us
    pallas_call x1, Pallas kernels, per_device(): pl.pallas_call(pack_kernel, out_shape=(shape((half + 8, local), F32), sha...  2.18 us
    ppermute x1, starting transfers between devices, per_device(): got = lax.ppermute(sent, axis, [(i, i + d) for i, d in swaps(0, count)])  1.69 us
  transfers between devices with their start and end apart: 12, of which 4 were waited for; matrix products, arithmetic and copies ran while one was open for 0% of the time, Pallas kernels for 23%

profile of v3, /device:TPU:0, one launch (start us, length us, event | category | flops | bytes accessed | tf_op | source)
XLA Modules:
  0.0 40.9 jit_solution(4666206354441815997)
XLA Ops:
  0.7 2.2 %pack.1 = (f32[208,128]{1,0:T(8,128)S(1)}, f32[208,128]{1,0:T(8,128)S(1)}, f32[240,128]{1,0:T(8,128)S(1)}) custom-call(s32[1]{0:T(128)} %bitcast.first_ref, f32[4,400,128]{2,1,0:T(8,128)} %states_ref.3, f32[2,128]{1,0:T(2,128)} %profile_ref.1), custom_call_target="tpu_custom_call" | custom-call | tf_op jit(solution)/shard_map/pack/pallas_call | solution.py:540
  2.9 3.0 %collective-permute-start = (f32[240,128]{1,0:T(8,128)S(1)}, f32[240,128]{1,0:T(8,128)S(1)}, u32[]{:S(2)}, u32[]{:S(2)}) collective-permute-start(f32[240,128]{1,0:T(8,128)S(1)} %get-tuple-element.23), channel_id=1, source_target_pairs={{0,2},{1,0},{2,3},{3,1},{4,5},{5,4},{6,7},{7,6},{8,9},{9,8},{10,11... | collective-permute-start | bytes 368648 | tf_op jit(solution)/shard_map/ppermute | solution.py:584
  5.9 2.4 %collective-permute-done = f32[240,128]{1,0:T(8,128)S(1)} collective-permute-done((f32[240,128]{1,0:T(8,128)S(1)}, f32[240,128]{1,0:T(8,128)S(1)}, u32[]{:S(2)}, u32[]{:S(2)}) %collective-permute-start) | collective-permute-done | bytes 122912 | tf_op jit(solution)/shard_map/ppermute | solution.py:584
  8.4 1.0 %collective-permute-start.1 = (f32[240,128]{1,0:T(8,128)S(1)}, f32[240,128]{1,0:T(8,128)S(1)}, u32[]{:S(2)}, u32[]{:S(2)}) collective-permute-start(f32[240,128]{1,0:T(8,128)S(1)} %broadcast_select_fusion), channel_id=1, source_target_pairs={{0,12},{1,0},{2,14},{3,2},{4,5},{5,4},{6,7},{7,6},{8,9},{9,8},{10,... | collective-permute-start | bytes 368648 | tf_op jit(solution)/shard_map/ppermute | solution.py:584
  9.4 0.0 collective-permute-start.2
  9.4 0.7 %collective-permute-start.4 = (f32[208,128]{1,0:T(8,128)S(1)}, f32[208,128]{1,0:T(8,128)S(1)}, u32[]{:S(2)}, u32[]{:S(2)}) collective-permute-start(f32[208,128]{1,0:T(8,128)S(1)} %get-tuple-element.24), channel_id=1, source_target_pairs={{1,2},{2,1},{3,4},{4,3},{5,6},{6,5},{7,8},{8,7},{9,10},{10,9},{11,... | collective-permute-start | bytes 319496 | tf_op jit(solution)/shard_map/ppermute | solution.py:578
  10.1 0.0 copy-start.3
  10.1 0.0 copy-start.4
  10.1 1.7 %collective-permute-done.1 = f32[240,128]{1,0:T(8,128)S(1)} collective-permute-done((f32[240,128]{1,0:T(8,128)S(1)}, f32[240,128]{1,0:T(8,128)S(1)}, u32[]{:S(2)}, u32[]{:S(2)}) %collective-permute-start.1) | collective-permute-done | bytes 122912 | tf_op jit(solution)/shard_map/ppermute | solution.py:584
  11.8 1.3 %collective-permute-done.2 = f32[240,128]{1,0:T(8,128)S(1)} collective-permute-done((f32[240,128]{1,0:T(8,128)S(1)}, f32[240,128]{1,0:T(8,128)S(1)}, u32[]{:S(2)}, u32[]{:S(2)}) %collective-permute-start.2) | collective-permute-done | bytes 122912 | tf_op jit(solution)/shard_map/ppermute | solution.py:584
  13.1 1.3 %collective-permute-done.3 = f32[240,128]{1,0:T(8,128)S(1)} collective-permute-done((f32[240,128]{1,0:T(8,128)S(1)}, f32[240,128]{1,0:T(8,128)S(1)}, u32[]{:S(2)}, u32[]{:S(2)}) %collective-permute-start.3) | collective-permute-done | bytes 122912 | tf_op jit(solution)/shard_map/ppermute | solution.py:584
  14.5 1.7 %collective-permute-start.5 = (f32[448,128]{1,0:T(8,128)S(1)}, f32[448,128]{1,0:T(8,128)S(1)}, u32[]{:S(2)}, u32[]{:S(2)}) collective-permute-start(f32[448,128]{1,0:T(8,128)S(1)} %constant_dynamic-update-slice_fusion.sent_ref), channel_id=1, source_target_pairs={{0,1},{1,0},{2,3},{3,2},{4,5},{5,4},{6,7},{7,6},{8,9},{9,8},{10,11... | collective-permute-start | bytes 688136 | tf_op jit(solution)/shard_map/ppermute | solution.py:595
  16.2 1.4 %tables.1 = (bf16[400,1200]{1,0:T(8,128)(2,1)S(1)}, f32[2,256,256]{2,1,0:T(8,128)S(1)}, f32[400,256]{1,0:T(8,128)S(1)}, bf16[1200,768]{1,0:T(8,128)(2,1)S(1)}, f...) custom-call(s32[1]{0:T(128)} %bitcast.first_ref, f32[400,400]{1,0:T(8,128)S(1)} %copy-done.1, s32[25,25]{1,0:T(8,128)S(1)} %copy-done.2, ...), custom_call_target="tpu_custom_call" | custom-call | tf_op jit(solution)/shard_map/tables/pallas_call | solution.py:562
  17.6 0.0 collective-permute-done.5.got_ref
  17.7 7.9 %first.1 = (bf16[1200,768]{1,0:T(8,128)(2,1)S(1)}, f32[400,768]{1,0:T(8,128)S(1)}, f32[400,768]{1,0:T(8,128)S(1)}, bf16[2,256,256]{2,1,0:T(8,128)(2,1)S(1)}, f32[8,128]{1,0:T(8,128)S(1)}) custom-call(s32[1]{0:T(128)} %bitcast.first_ref, f32[2]{0:T(128)S(1)} %copy-done.3, ...), custom_call_target="tpu_custom_call", output_to_operand_aliasing={{0}: (11, {}), {1}: (12, {})} | custom-call | tf_op jit(solution)/shard_map/first/pallas_call | solution.py:604
  25.5 0.0 collective-permute-start.6
  25.6 2.5 %collective-permute-start.7 = (f32[8,128]{1,0:T(8,128)S(1)}, f32[8,128]{1,0:T(8,128)S(1)}, u32[]{:S(2)}, u32[]{:S(2)}) collective-permute-start(f32[8,128]{1,0:T(8,128)S(1)} %get-tuple-element.34.after_ref), channel_id=1, source_target_pairs={{0,2},{1,3},{2,0},{3,1},{4,6},{5,7},{6,4},{7,5},{8,10},{9,11},{10,... | collective-permute-start | bytes 12296 | tf_op jit(solution)/shard_map/ppermute | solution.py:627
  28.1 0.1 collective-permute-start.8
  28.2 3.1 %later.1 = (f32[400,768]{1,0:T(8,128)S(1)}, bf16[1200,768]{1,0:T(8,128)(2,1)S(1)}, f32[400,768]{1,0:T(8,128)S(1)}, f32[400,768]{1,0:T(8,128)S(1)}, f32[8,128]{1,0:T(8,128)S(1)}) custom-call(s32[1]{0:T(128)} %bitcast.first_ref, f32[2]{0:T(128)S(1)} %copy-done.3, f32[8,128]{1,0:T(8,128)S(1)} %get-tuple-element.34.after_ref, ...), custom_call_target="tpu_custom_call" | custom-call | tf_op jit(solution)/shard_map/later/pallas_call | solution.py:637
  31.3 0.0 collective-permute-done.7
  31.4 2.7 %collective-permute-start.10 = (f32[8,128]{1,0:T(8,128)S(1)}, f32[8,128]{1,0:T(8,128)S(1)}, u32[]{:S(2)}, u32[]{:S(2)}) collective-permute-start(f32[8,128]{1,0:T(8,128)S(1)} %add_add_fusion.1.after_ref), channel_id=1, source_target_pairs={{0,8},{1,9},{2,10},{3,11},{4,12},{5,13},{6,14},{7,15},{8,0},{9,1},... | collective-permute-start | bytes 12296 | tf_op jit(solution)/shard_map/ppermute | solution.py:627
  34.1 1.3 %collective-permute-start.11 = (f32[8,128]{1,0:T(8,128)S(1)}, f32[8,128]{1,0:T(8,128)S(1)}, u32[]{:S(2)}, u32[]{:S(2)}) collective-permute-start(f32[8,128]{1,0:T(8,128)S(1)} %add_add_fusion.1.after_ref), channel_id=1, source_target_pairs={{0,12},{1,13},{2,14},{3,15},{4,8},{5,9},{6,10},{7,11},{8,4},{9,5},... | collective-permute-start | bytes 12296 | tf_op jit(solution)/shard_map/ppermute | solution.py:627
  35.3 4.9 %rest.1 = f32[4,400,128]{2,1,0:T(8,128)} custom-call(s32[1]{0:T(128)} %bitcast.first_ref, f32[2]{0:T(128)S(1)} %copy-done.3, f32[8,128]{1,0:T(8,128)S(1)} %add_add_fusion.1.after_ref, bf16[2,256,256]{2,1,0:T(8,128)(2,1)S(1)} %get-tuple-element.35.matrix_ref, bf16[400,1200]{1,0:T(8,128)(2,1)S(1)} %get-tuple-element.28.coupling_ref, ...), custom_call_target="tpu_custom_call" | custom-call | tf_op jit(solution)/shard_map/rest/pallas_call | solution.py:650
  40.3 0.6 %slice_reduce_fusion = f32[2]{0:T(128)} fusion(f32[8,128]{1,0:T(8,128)S(1)} %add_add_fusion), kind=kLoop, calls=%fused_computation.6 | loop fusion | bytes 16 | tf_op jit(solution)/shard_map/slice | solution.py:669
  (26 shorter events, 0.1 us)
Async XLA Ops:
  0.6 15.6 %copy-start = (f32[4,400,128]{2,1,0:T(8,128)S(1)}, f32[4,400,128]{2,1,0:T(8,128)}, u32[]{:S(2)}) copy-start(f32[4,400,128]{2,1,0:T(8,128)} %states_ref.3) | copy-start | bytes 2457604
  0.6 15.5 %copy-start.5 = (s32[400]{0:T(512)S(1)}, s32[400]{0:T(512)}, u32[]{:S(2)}) copy-start(s32[400]{0:T(512)} %param.10) | copy-start | bytes 4804
  0.7 15.5 %copy-start.6 = (f32[400]{0:T(512)S(1)}, f32[400]{0:T(512)}, u32[]{:S(2)}) copy-start(f32[400]{0:T(512)} %param.11) | copy-start | bytes 4804
  0.7 15.5 %copy-start.1 = (f32[400,400]{1,0:T(8,128)S(1)}, f32[400,400]{1,0:T(8,128)}, u32[]{:S(2)}) copy-start(f32[400,400]{1,0:T(8,128)} %dipole_ref.1) | copy-start | bytes 1920004
  0.7 15.5 %copy-start.2 = (s32[25,25]{1,0:T(8,128)S(1)}, s32[25,25]{1,0:T(8,128)}, u32[]{:S(2)}) copy-start(s32[25,25]{1,0:T(8,128)} %pattern_ref.1) | copy-start | bytes 7504
  2.9 5.5 %collective-permute-start = (f32[240,128]{1,0:T(8,128)S(1)}, f32[240,128]{1,0:T(8,128)S(1)}, u32[]{:S(2)}, u32[]{:S(2)}) collective-permute-start(f32[240,128]{1,0:T(8,128)S(1)} %get-tuple-element.23), channel_id=1, source_target_pairs={{0,2},{1,0},{2,3},{3,1},{4,5},{5,4},{6,7},{7,6},{8,9},{9,8},{10,11... | collective-permute-start | bytes 368648 | tf_op jit(solution)/shard_map/ppermute | solution.py:584
  8.4 3.4 %collective-permute-start.1 = (f32[240,128]{1,0:T(8,128)S(1)}, f32[240,128]{1,0:T(8,128)S(1)}, u32[]{:S(2)}, u32[]{:S(2)}) collective-permute-start(f32[240,128]{1,0:T(8,128)S(1)} %broadcast_select_fusion), channel_id=1, source_target_pairs={{0,12},{1,0},{2,14},{3,2},{4,5},{5,4},{6,7},{7,6},{8,9},{9,8},{10,... | collective-permute-start | bytes 368648 | tf_op jit(solution)/shard_map/ppermute | solution.py:584
  9.4 3.7 %collective-permute-start.2 = (f32[240,128]{1,0:T(8,128)S(1)}, f32[240,128]{1,0:T(8,128)S(1)}, u32[]{:S(2)}, u32[]{:S(2)}) collective-permute-start(f32[240,128]{1,0:T(8,128)S(1)} %broadcast_select_fusion), channel_id=1, source_target_pairs={{0,8},{1,0},{2,10},{3,2},{4,5},{5,4},{6,7},{7,6},{8,9},{9,1},{10,1... | collective-permute-start | bytes 368648 | tf_op jit(solution)/shard_map/ppermute | solution.py:584
  9.4 5.0 %collective-permute-start.3 = (f32[240,128]{1,0:T(8,128)S(1)}, f32[240,128]{1,0:T(8,128)S(1)}, u32[]{:S(2)}, u32[]{:S(2)}) collective-permute-start(f32[240,128]{1,0:T(8,128)S(1)} %broadcast_select_fusion), channel_id=1, source_target_pairs={{0,4},{1,0},{2,6},{3,2},{4,5},{5,1},{6,7},{7,3},{8,9},{9,8},{10,11... | collective-permute-start | bytes 368648 | tf_op jit(solution)/shard_map/ppermute | solution.py:584
  9.4 5.1 %collective-permute-start.4 = (f32[208,128]{1,0:T(8,128)S(1)}, f32[208,128]{1,0:T(8,128)S(1)}, u32[]{:S(2)}, u32[]{:S(2)}) collective-permute-start(f32[208,128]{1,0:T(8,128)S(1)} %get-tuple-element.24), channel_id=1, source_target_pairs={{1,2},{2,1},{3,4},{4,3},{5,6},{6,5},{7,8},{8,7},{9,10},{10,9},{11,... | collective-permute-start | bytes 319496 | tf_op jit(solution)/shard_map/ppermute | solution.py:578
  10.1 7.6 %copy-start.3 = (f32[2]{0:T(128)S(1)}, f32[2]{0:T(128)}, u32[]{:S(2)}) copy-start(f32[2]{0:T(128)} %field_ref.5) | copy-start | bytes 28
  10.1 7.6 %copy-start.4 = (f32[2,128]{1,0:T(2,128)S(1)}, f32[2,128]{1,0:T(2,128)}, u32[]{:S(2)}) copy-start(f32[2,128]{1,0:T(2,128)} %profile_ref.1) | copy-start | bytes 3076
  14.5 3.1 %collective-permute-start.5 = (f32[448,128]{1,0:T(8,128)S(1)}, f32[448,128]{1,0:T(8,128)S(1)}, u32[]{:S(2)}, u32[]{:S(2)}) collective-permute-start(f32[448,128]{1,0:T(8,128)S(1)} %constant_dynamic-update-slice_fusion.sent_ref), channel_id=1, source_target_pairs={{0,1},{1,0},{2,3},{3,2},{4,5},{5,4},{6,7},{7,6},{8,9},{9,8},{10,11... | collective-permute-start | bytes 688136 | tf_op jit(solution)/shard_map/ppermute | solution.py:595
  25.5 5.8 %collective-permute-start.6 = (f32[8,128]{1,0:T(8,128)S(1)}, f32[8,128]{1,0:T(8,128)S(1)}, u32[]{:S(2)}, u32[]{:S(2)}) collective-permute-start(f32[8,128]{1,0:T(8,128)S(1)} %get-tuple-element.34.after_ref), channel_id=1, source_target_pairs={{0,1},{1,0},{2,3},{3,2},{4,5},{5,4},{6,7},{7,6},{8,9},{9,8},{10,11... | collective-permute-start | bytes 12296 | tf_op jit(solution)/shard_map/ppermute | solution.py:627
  25.6 5.7 %collective-permute-start.7 = (f32[8,128]{1,0:T(8,128)S(1)}, f32[8,128]{1,0:T(8,128)S(1)}, u32[]{:S(2)}, u32[]{:S(2)}) collective-permute-start(f32[8,128]{1,0:T(8,128)S(1)} %get-tuple-element.34.after_ref), channel_id=1, source_target_pairs={{0,2},{1,3},{2,0},{3,1},{4,6},{5,7},{6,4},{7,5},{8,10},{9,11},{10,... | collective-permute-start | bytes 12296 | tf_op jit(solution)/shard_map/ppermute | solution.py:627
  28.1 3.2 %collective-permute-start.8 = (f32[8,128]{1,0:T(8,128)S(1)}, f32[8,128]{1,0:T(8,128)S(1)}, u32[]{:S(2)}, u32[]{:S(2)}) collective-permute-start(f32[8,128]{1,0:T(8,128)S(1)} %get-tuple-element.34.after_ref), channel_id=1, source_target_pairs={{0,3},{1,2},{2,1},{3,0},{4,7},{5,6},{6,5},{7,4},{8,11},{9,10},{10,... | collective-permute-start | bytes 12296 | tf_op jit(solution)/shard_map/ppermute | solution.py:627
  31.4 8.9 %collective-permute-start.10 = (f32[8,128]{1,0:T(8,128)S(1)}, f32[8,128]{1,0:T(8,128)S(1)}, u32[]{:S(2)}, u32[]{:S(2)}) collective-permute-start(f32[8,128]{1,0:T(8,128)S(1)} %add_add_fusion.1.after_ref), channel_id=1, source_target_pairs={{0,8},{1,9},{2,10},{3,11},{4,12},{5,13},{6,14},{7,15},{8,0},{9,1},... | collective-permute-start | bytes 12296 | tf_op jit(solution)/shard_map/ppermute | solution.py:627
  34.1 6.2 %collective-permute-start.11 = (f32[8,128]{1,0:T(8,128)S(1)}, f32[8,128]{1,0:T(8,128)S(1)}, u32[]{:S(2)}, u32[]{:S(2)}) collective-permute-start(f32[8,128]{1,0:T(8,128)S(1)} %add_add_fusion.1.after_ref), channel_id=1, source_target_pairs={{0,12},{1,13},{2,14},{3,15},{4,8},{5,9},{6,10},{7,11},{8,4},{9,5},... | collective-permute-start | bytes 12296 | tf_op jit(solution)/shard_map/ppermute | solution.py:627
  35.3 5.0 %collective-permute-start.9 = (f32[8,128]{1,0:T(8,128)S(1)}, f32[8,128]{1,0:T(8,128)S(1)}, u32[]{:S(2)}, u32[]{:S(2)}) collective-permute-start(f32[8,128]{1,0:T(8,128)S(1)} %add_add_fusion.1.after_ref), channel_id=1, source_target_pairs={{0,4},{1,5},{2,6},{3,7},{4,0},{5,1},{6,2},{7,3},{8,12},{9,13},{10,... | collective-permute-start | bytes 12296 | tf_op jit(solution)/shard_map/ppermute | solution.py:627

commit v4 on v3

--- a/solution.py
+++ b/solution.py
@@ -57,35 +57,36 @@
     ):
         ref[half : half + 2, :] = value
         ref[half + 2 : half + 8, :] = zeros
-    group = iota((half, local), 1) // 16
-    pair = (iota((channels, local), 1) & 63) // 2
-    right = left = more = None
+    group = iota((half, local), 1) // HALO
+    groups = local // HALO
+    right = left = None
+    rest = [None, None]
     for k, first in ((0, 0), (2, 64), (1, 16), (3, 80)):
         copies[k].wait()
         for h in range(2):
-            rows = states_ref[k, half * h : half * h + half, :]
             at = first + 32 * h
-            hit = group == at // 16
-            shift = (at + HALO) % local
-            moved = pltpu.roll(rows, shift, 1) if shift else rows
-            right = moved if right is None else jnp.where(hit, moved, right)
-            moved = pltpu.roll(rows, at, 1) if at else rows
-            left = moved if left is None else jnp.where(hit, moved, left)
-        at = 64 * (k // 2) + 2 * (k % 2)
-        moved = pltpu.roll(states_ref[k], (at - 16) % local, 1)
-        more = moved if more is None else jnp.where(pair == k % 2, jnp.where(iota((channels, local), 1) // 64 == k // 2, moved, more), more)
+            moved = pltpu.roll(states_ref[k, half * h : half * h + half, :], (at + HALO) % local, 1)
+
+            def put(old, to):
+                return moved if old is None else jnp.where(group == to // HALO % groups, moved, old)
+
+            right = put(right, at)
+            left = put(left, at + HALO)
+            rest[h] = put(rest[h], at + 2 * HALO)
     near_ref[:half, :] = jnp.where(odd, left, right)
     far_ref[:half, :] = jnp.where(odd, right, left)
     inner_ref[:half, :] = left
-    rest = None
-    quad = (iota((32, local), 1) & 63) // 4
-    for i in range((channels + 31) // 32):
-        rows = more[32 * i : min(32 * i + 32, channels)]
-        if rows.shape[0] < 32:
-            rows = jnp.concatenate([rows, jnp.zeros((32 - rows.shape[0], local), F32)], axis=0)
-        moved = pltpu.roll(rows, 4 * i, 1) if i else rows
-        rest = moved if rest is None else jnp.where(quad == i, moved, rest)
-    inner_ref[half + 8 :, :] = rest
+    lanes = iota((32, local), 1)
+    more = None
+    for h in range(2):
+        for i in range((half + 31) // 32):
+            rows = rest[h][32 * i : min(32 * i + 32, half)]
+            if rows.shape[0] < 32:
+                rows = jnp.concatenate([rows, jnp.zeros((32 - rows.shape[0], local), F32)], axis=0)
+            moved = pltpu.roll(rows, 2 * i, 1) if i else rows
+            hit = ((lanes & 15) // 2 == i) & ((lanes & 32) == 32 * (1 - h))
+            more = moved if more is None else jnp.where(hit, moved, more)
+    inner_ref[half + 8 :, :] = more
 
 
 def lane_points(lanes, first, local):
@@ -294,29 +295,24 @@
                 shift = (to - back) % local
                 return pltpu.roll(value, shift, 1) if shift else value
 
+            halo = jnp.where(((lanes - back) & 63) < 16, left[:half, :], right[:half, :])
             value = jnp.where(
-                lanes < 16,
-                rolled(left[:half, :], 0),
+                lanes < 32,
+                rolled(halo, 0),
                 jnp.where(
-                    lanes < 32,
-                    rolled(right[:half, :], 16),
-                    jnp.where(
-                        lanes < 48,
-                        rolled(inner[:half, :], 32),
-                        jnp.where(
-                            (lanes >= 50) & (lanes < 54), rolled(inner[:half, :], 50), jnp.zeros((half, local), F32)
-                        ),
-                    ),
+                    lanes < 48,
+                    rolled(inner[:half, :], 16),
+                    jnp.where((lanes >= 50) & (lanes < 54), rolled(inner[:half, :], 34), 0.0),
                 ),
             )
             v_ref[half * h : half * h + half, at : at + local] = value
-        narrow = iota((32, local), 1) & 63
-        for i in range((channels + 31) // 32):
-            rows = slice(32 * i, min(32 * i + 32, channels))
-            count = rows.stop - rows.start
-            value = pltpu.roll(inner[half + 8 : half + 8 + count, :], (48 - 4 * i - 2 * pair) % local, 1)
-            hit = (narrow[:count] >= 48) & (narrow[:count] < 50)
-            v_ref[rows, at : at + local] = jnp.where(hit, value, v_ref[rows, at : at + local])
+            narrow = iota((32, local), 1) & 63
+            for i in range((half + 31) // 32):
+                rows = slice(half * h + 32 * i, half * h + min(32 * i + 32, half))
+                count = rows.stop - rows.start
+                value = rolled(inner[half + 8 : half + 8 + count, :], 16 - 2 * i)
+                hit = (narrow[:count] >= 48) & (narrow[:count] < 50)
+                v_ref[rows, at : at + local] = jnp.where(hit, value, v_ref[rows, at : at + local])
     split_store(stack_ref, 256, v_ref[:, 256:512])
     p_own = profile_ref[...]
     lanes2 = iota((2, local), 1)
@@ -373,18 +369,20 @@
                 split_rows(next_stack, at, rows, before + value)
 
         scale = time_step / power
-        mix(coupling_ref, stack, mixed_ref, (1,) if power == 1 else (0, 2, 1))
-        stencil(stack, matrix_ref, moved_ref, "ab")
-        advance("ab", old, keep, mixed_ref, moved_ref, pot_ref, drive, scale)
-        stencil(stack, matrix_ref, moved_ref, "cd")
-        advance("cd", old, keep, mixed_ref, moved_ref, pot_ref, drive, scale)
+        for pair, tile in (("ab", 0), ("cd", 2)):
+            if power > 1:
+                mix(coupling_ref, stack, mixed_ref, (tile,))
+            stencil(stack, matrix_ref, moved_ref, pair)
+            advance(pair, old, keep, mixed_ref, moved_ref, pot_ref, drive, scale)
+        mix(coupling_ref, stack, mixed_ref, (1,))
         advance(("ac", "bd"), old, keep, mixed_ref, moved_ref, pot_ref, drive, scale)
     mix(coupling_ref, stack_ref, mixed_ref, (0,))
     part_ref[...] = jnp.zeros(part_ref.shape, F32)
     state = [state_ref[:, OWN[part] : OWN[part] + local] for part in "cd"]
     for n, value in ((0, part_in_ref[0:1, :]), (1, intersect(state[0], state[1], mixed_ref, radii))):
         whole = jnp.sum(value, axis=1, keepdims=True) * scaling
-        part_ref[n : n + 1, :] = jnp.broadcast_to(whole, (1, local))
+        here = (iota(part_ref.shape, 0) == 0) & (iota(part_ref.shape, 1) == n)
+        part_ref[...] = jnp.where(here, whole, part_ref[...])
 
 
 def later_kernel(
@@ -424,13 +422,15 @@
             total_ref[rows, cut] = total_in_ref[rows, cut] + value
 
     scale = time_step / power
-    mix(coupling_ref, stack_in_ref, now_ref, (2, 1))
     stencil(stack_in_ref, matrix_ref, moved_ref, "ab")
     advance("ab", old, keep, mixed_in_ref, moved_ref, pot_ref, drive, scale)
+    mix(coupling_ref, stack_in_ref, now_ref, (2,))
     stencil(stack_in_ref, matrix_ref, moved_ref, "cd")
+    mix(coupling_ref, stack_ref, mixed_ref, (0,))
     advance("cd", old, keep, now_ref, moved_ref, pot_ref, drive, scale)
+    mix(coupling_ref, stack_in_ref, now_ref, (1,))
     advance(("ac", "bd"), old, keep, now_ref, moved_ref, pot_ref, drive, scale)
-    mix(coupling_ref, stack_ref, mixed_ref, (0, 2, 1))
+    mix(coupling_ref, stack_ref, mixed_ref, (2, 1))
 
 
 def rest_kernel(
@@ -483,15 +483,17 @@
                 total_ref[k, rows, :] = before + value
 
         scale = time_step / power
-        if power > 2:
-            mix(coupling_ref, stack, mixed_ref, (0, 2) if final else (0, 2, 1))
-        for pair in ("ab", "cd"):
+        for pair, tile in (("ab", 0), ("cd", 2)):
+            if power > 2:
+                mix(coupling_ref, stack, mixed_ref, (tile,))
             stencil(stack, matrix_ref, moved_ref, pair)
             advance(pair, old, keep, mixed, moved_ref, pot_ref, drive, scale)
             if final:
                 for part in pair:
                     copies[PARTS.index(part)].start()
         if not final:
+            if power > 2:
+                mix(coupling_ref, stack, mixed_ref, (1,))
             advance(("ac", "bd"), old, keep, mixed, moved_ref, pot_ref, drive, scale)
     for copy in copies:
         copy.wait()
@@ -666,7 +668,7 @@
         name="rest",
     )(first, pulse_field, part, matrix, coupling, pot, v, stack, mixed, total)
     part = add(part, got)
-    return final, part[:STEPS, 0]
+    return final, part[0, :STEPS]
 
 
 def solution(mesh):

time: 41.1 us -> 39.6 us (0.964)
  Pallas kernels: 19.5 us -> 18.2 us
    slice x1 -> x0, local copies, waits for them, and re-layouts: 0.63 us -> none  [per_device(): return (final, part[:STEPS, 0])]
    pallas_call x1, Pallas kernels: 7.87 us -> 7.26 us  [per_device(): pl.pallas_call(functools.partial(first_kernel, scaling=scaling), out_shap...]
    squeeze x0 -> x1, local copies, waits for them, and re-layouts: none -> 0.51 us  [per_device(): return (final, part[0, :STEPS])]
  transfers between devices with their start and end apart: 12 -> 12, of which waited for: 4 -> 5; matrix products, arithmetic and copies ran while one was open for 0% -> 0% of each run, Pallas kernels for 23% -> 23%
where the time goes in v4:
time: 39.6 us; the launch traced here: 39.5 us
  Pallas kernels  18.2 us (46%)
  starting transfers between devices  13 us (33%)
  waiting for transfers between devices  6.86 us (17%)
  between operations  0.86 us (2%)
  local copies, waits for them, and re-layouts  0.57 us (1%)
    pallas_call x1, Pallas kernels, per_device(): pl.pallas_call(functools.partial(first_kernel, scaling=scaling), out_shap...  7.26 us
    ppermute x4, waiting for transfers between devices, per_device(): got = lax.ppermute(inner, axis, full_cycle(pairs, count))  6.76 us
    ppermute x6, starting transfers between devices, send(): lax.ppermute(value, axis, [(i, i ^ pattern << low) for i in range(count)])  6.56 us
    pallas_call x1, Pallas kernels, per_device(): pl.pallas_call(rest_kernel, out_shape=shape(states.shape, F32), in_specs=...  4.84 us
    ppermute x4, starting transfers between devices, per_device(): got = lax.ppermute(inner, axis, full_cycle(pairs, count))  4.04 us
    pallas_call x1, Pallas kernels, per_device(): pl.pallas_call(functools.partial(later_kernel, power=1), out_shape=evolve...  2.85 us
    pallas_call x1, Pallas kernels, per_device(): pl.pallas_call(pack_kernel, out_shape=(shape((half + 8, local), F32), sha...  1.79 us
    ppermute x1, starting transfers between devices, per_device(): got = lax.ppermute(sent, axis, [(i, i + d) for i, d in swaps(0, count)])  1.69 us
  transfers between devices with their start and end apart: 12, of which 5 were waited for; matrix products, arithmetic and copies ran while one was open for 0% of the time, Pallas kernels for 23%

profile of v4, /device:TPU:0, one launch (start us, length us, event | category | flops | bytes accessed | tf_op | source)
XLA Modules:
  0.0 39.5 jit_solution(15387656494299480531)
XLA Ops:
  0.7 1.8 %pack.1 = (f32[208,128]{1,0:T(8,128)S(1)}, f32[208,128]{1,0:T(8,128)S(1)}, f32[240,128]{1,0:T(8,128)S(1)}) custom-call(s32[1]{0:T(128)} %bitcast.first_ref, f32[4,400,128]{2,1,0:T(8,128)} %states_ref.3, f32[2,128]{1,0:T(2,128)} %profile_ref.1), custom_call_target="tpu_custom_call" | custom-call | tf_op jit(solution)/shard_map/pack/pallas_call | solution.py:542
  2.5 3.0 %collective-permute-start = (f32[240,128]{1,0:T(8,128)S(1)}, f32[240,128]{1,0:T(8,128)S(1)}, u32[]{:S(2)}, u32[]{:S(2)}) collective-permute-start(f32[240,128]{1,0:T(8,128)S(1)} %get-tuple-element.23), channel_id=1, source_target_pairs={{0,2},{1,0},{2,3},{3,1},{4,5},{5,4},{6,7},{7,6},{8,9},{9,8},{10,11... | collective-permute-start | bytes 368648 | tf_op jit(solution)/shard_map/ppermute | solution.py:586
  5.5 2.4 %collective-permute-done = f32[240,128]{1,0:T(8,128)S(1)} collective-permute-done((f32[240,128]{1,0:T(8,128)S(1)}, f32[240,128]{1,0:T(8,128)S(1)}, u32[]{:S(2)}, u32[]{:S(2)}) %collective-permute-start) | collective-permute-done | bytes 122912 | tf_op jit(solution)/shard_map/ppermute | solution.py:586
  8.0 1.0 %collective-permute-start.1 = (f32[240,128]{1,0:T(8,128)S(1)}, f32[240,128]{1,0:T(8,128)S(1)}, u32[]{:S(2)}, u32[]{:S(2)}) collective-permute-start(f32[240,128]{1,0:T(8,128)S(1)} %broadcast_select_fusion), channel_id=1, source_target_pairs={{0,12},{1,0},{2,14},{3,2},{4,5},{5,4},{6,7},{7,6},{8,9},{9,8},{10,... | collective-permute-start | bytes 368648 | tf_op jit(solution)/shard_map/ppermute | solution.py:586
  9.0 0.7 %collective-permute-start.4 = (f32[208,128]{1,0:T(8,128)S(1)}, f32[208,128]{1,0:T(8,128)S(1)}, u32[]{:S(2)}, u32[]{:S(2)}) collective-permute-start(f32[208,128]{1,0:T(8,128)S(1)} %get-tuple-element.24), channel_id=1, source_target_pairs={{1,2},{2,1},{3,4},{4,3},{5,6},{6,5},{7,8},{8,7},{9,10},{10,9},{11,... | collective-permute-start | bytes 319496 | tf_op jit(solution)/shard_map/ppermute | solution.py:580
  9.7 0.0 copy-start.3
  9.7 0.0 copy-start.4
  9.7 1.7 %collective-permute-done.1 = f32[240,128]{1,0:T(8,128)S(1)} collective-permute-done((f32[240,128]{1,0:T(8,128)S(1)}, f32[240,128]{1,0:T(8,128)S(1)}, u32[]{:S(2)}, u32[]{:S(2)}) %collective-permute-start.1) | collective-permute-done | bytes 122912 | tf_op jit(solution)/shard_map/ppermute | solution.py:586
  11.4 1.3 %collective-permute-done.2 = f32[240,128]{1,0:T(8,128)S(1)} collective-permute-done((f32[240,128]{1,0:T(8,128)S(1)}, f32[240,128]{1,0:T(8,128)S(1)}, u32[]{:S(2)}, u32[]{:S(2)}) %collective-permute-start.2) | collective-permute-done | bytes 122912 | tf_op jit(solution)/shard_map/ppermute | solution.py:586
  12.7 1.3 %collective-permute-done.3 = f32[240,128]{1,0:T(8,128)S(1)} collective-permute-done((f32[240,128]{1,0:T(8,128)S(1)}, f32[240,128]{1,0:T(8,128)S(1)}, u32[]{:S(2)}, u32[]{:S(2)}) %collective-permute-start.3) | collective-permute-done | bytes 122912 | tf_op jit(solution)/shard_map/ppermute | solution.py:586
  14.1 0.0 collective-permute-done.4.far_ref
  14.1 1.7 %collective-permute-start.5 = (f32[448,128]{1,0:T(8,128)S(1)}, f32[448,128]{1,0:T(8,128)S(1)}, u32[]{:S(2)}, u32[]{:S(2)}) collective-permute-start(f32[448,128]{1,0:T(8,128)S(1)} %constant_dynamic-update-slice_fusion.sent_ref), channel_id=1, source_target_pairs={{0,1},{1,0},{2,3},{3,2},{4,5},{5,4},{6,7},{7,6},{8,9},{9,8},{10,11... | collective-permute-start | bytes 688136 | tf_op jit(solution)/shard_map/ppermute | solution.py:597
  15.8 1.4 %tables.1 = (bf16[400,1200]{1,0:T(8,128)(2,1)S(1)}, f32[2,256,256]{2,1,0:T(8,128)S(1)}, f32[400,256]{1,0:T(8,128)S(1)}, bf16[1200,768]{1,0:T(8,128)(2,1)S(1)}, f...) custom-call(s32[1]{0:T(128)} %bitcast.first_ref, f32[400,400]{1,0:T(8,128)S(1)} %copy-done.1, s32[25,25]{1,0:T(8,128)S(1)} %copy-done.2, ...), custom_call_target="tpu_custom_call" | custom-call | tf_op jit(solution)/shard_map/tables/pallas_call | solution.py:564
  17.3 7.3 %first.1 = (bf16[1200,768]{1,0:T(8,128)(2,1)S(1)}, f32[400,768]{1,0:T(8,128)S(1)}, f32[400,768]{1,0:T(8,128)S(1)}, bf16[2,256,256]{2,1,0:T(8,128)(2,1)S(1)}, f32[8,128]{1,0:T(8,128)S(1)}) custom-call(s32[1]{0:T(128)} %bitcast.first_ref, f32[2]{0:T(128)S(1)} %copy-done.3, ...), custom_call_target="tpu_custom_call", output_to_operand_aliasing={{0}: (11, {}), {1}: (12, {})} | custom-call | tf_op jit(solution)/shard_map/first/pallas_call | solution.py:606
  24.5 0.0 collective-permute-start.6
  24.6 2.5 %collective-permute-start.7 = (f32[8,128]{1,0:T(8,128)S(1)}, f32[8,128]{1,0:T(8,128)S(1)}, u32[]{:S(2)}, u32[]{:S(2)}) collective-permute-start(f32[8,128]{1,0:T(8,128)S(1)} %get-tuple-element.34.after_ref), channel_id=1, source_target_pairs={{0,2},{1,3},{2,0},{3,1},{4,6},{5,7},{6,4},{7,5},{8,10},{9,11},{10,... | collective-permute-start | bytes 12296 | tf_op jit(solution)/shard_map/ppermute | solution.py:629
  27.1 0.1 collective-permute-start.8
  27.2 2.9 %later.1 = (f32[400,768]{1,0:T(8,128)S(1)}, bf16[1200,768]{1,0:T(8,128)(2,1)S(1)}, f32[400,768]{1,0:T(8,128)S(1)}, f32[400,768]{1,0:T(8,128)S(1)}, f32[8,128]{1,0:T(8,128)S(1)}) custom-call(s32[1]{0:T(128)} %bitcast.first_ref, f32[2]{0:T(128)S(1)} %copy-done.3, f32[8,128]{1,0:T(8,128)S(1)} %get-tuple-element.34.after_ref, ...), custom_call_target="tpu_custom_call" | custom-call | tf_op jit(solution)/shard_map/later/pallas_call | solution.py:639
  30.0 0.0 collective-permute-done.6
  30.1 0.1 collective-permute-done.8
  30.1 2.6 %collective-permute-start.10 = (f32[8,128]{1,0:T(8,128)S(1)}, f32[8,128]{1,0:T(8,128)S(1)}, u32[]{:S(2)}, u32[]{:S(2)}) collective-permute-start(f32[8,128]{1,0:T(8,128)S(1)} %add_add_fusion.1.after_ref), channel_id=1, source_target_pairs={{0,8},{1,9},{2,10},{3,11},{4,12},{5,13},{6,14},{7,15},{8,0},{9,1},... | collective-permute-start | bytes 12296 | tf_op jit(solution)/shard_map/ppermute | solution.py:629
  32.8 1.3 %collective-permute-start.11 = (f32[8,128]{1,0:T(8,128)S(1)}, f32[8,128]{1,0:T(8,128)S(1)}, u32[]{:S(2)}, u32[]{:S(2)}) collective-permute-start(f32[8,128]{1,0:T(8,128)S(1)} %add_add_fusion.1.after_ref), channel_id=1, source_target_pairs={{0,12},{1,13},{2,14},{3,15},{4,8},{5,9},{6,10},{7,11},{8,4},{9,5},... | collective-permute-start | bytes 12296 | tf_op jit(solution)/shard_map/ppermute | solution.py:629
  34.1 4.8 %rest.1 = f32[4,400,128]{2,1,0:T(8,128)} custom-call(s32[1]{0:T(128)} %bitcast.first_ref, f32[2]{0:T(128)S(1)} %copy-done.3, f32[8,128]{1,0:T(8,128)S(1)} %add_add_fusion.1.after_ref, bf16[2,256,256]{2,1,0:T(8,128)(2,1)S(1)} %get-tuple-element.35.matrix_ref, bf16[400,1200]{1,0:T(8,128)(2,1)S(1)} %get-tuple-element.28.coupling_ref, ...), custom_call_target="tpu_custom_call" | custom-call | tf_op jit(solution)/shard_map/rest/pallas_call | solution.py:652
  38.9 0.5 %slice_bitcast_fusion = f32[2]{0:T(128)} fusion(f32[8,128]{1,0:T(8,128)S(1)} %add_add_fusion), kind=kLoop, calls=%fused_computation.6 | loop fusion | bytes 16 | tf_op jit(solution)/shard_map/squeeze | solution.py:671
  (26 shorter events, 0.1 us)
Async XLA Ops:
  0.6 15.2 %copy-start = (f32[4,400,128]{2,1,0:T(8,128)S(1)}, f32[4,400,128]{2,1,0:T(8,128)}, u32[]{:S(2)}) copy-start(f32[4,400,128]{2,1,0:T(8,128)} %states_ref.3) | copy-start | bytes 2457604
  0.6 15.1 %copy-start.5 = (s32[400]{0:T(512)S(1)}, s32[400]{0:T(512)}, u32[]{:S(2)}) copy-start(s32[400]{0:T(512)} %param.10) | copy-start | bytes 4804
  0.7 15.1 %copy-start.6 = (f32[400]{0:T(512)S(1)}, f32[400]{0:T(512)}, u32[]{:S(2)}) copy-start(f32[400]{0:T(512)} %param.11) | copy-start | bytes 4804
  0.7 15.1 %copy-start.1 = (f32[400,400]{1,0:T(8,128)S(1)}, f32[400,400]{1,0:T(8,128)}, u32[]{:S(2)}) copy-start(f32[400,400]{1,0:T(8,128)} %dipole_ref.1) | copy-start | bytes 1920004
  0.7 15.1 %copy-start.2 = (s32[25,25]{1,0:T(8,128)S(1)}, s32[25,25]{1,0:T(8,128)}, u32[]{:S(2)}) copy-start(s32[25,25]{1,0:T(8,128)} %pattern_ref.1) | copy-start | bytes 7504
  2.5 5.5 %collective-permute-start = (f32[240,128]{1,0:T(8,128)S(1)}, f32[240,128]{1,0:T(8,128)S(1)}, u32[]{:S(2)}, u32[]{:S(2)}) collective-permute-start(f32[240,128]{1,0:T(8,128)S(1)} %get-tuple-element.23), channel_id=1, source_target_pairs={{0,2},{1,0},{2,3},{3,1},{4,5},{5,4},{6,7},{7,6},{8,9},{9,8},{10,11... | collective-permute-start | bytes 368648 | tf_op jit(solution)/shard_map/ppermute | solution.py:586
  8.0 3.4 %collective-permute-start.1 = (f32[240,128]{1,0:T(8,128)S(1)}, f32[240,128]{1,0:T(8,128)S(1)}, u32[]{:S(2)}, u32[]{:S(2)}) collective-permute-start(f32[240,128]{1,0:T(8,128)S(1)} %broadcast_select_fusion), channel_id=1, source_target_pairs={{0,12},{1,0},{2,14},{3,2},{4,5},{5,4},{6,7},{7,6},{8,9},{9,8},{10,... | collective-permute-start | bytes 368648 | tf_op jit(solution)/shard_map/ppermute | solution.py:586
  9.0 3.7 %collective-permute-start.2 = (f32[240,128]{1,0:T(8,128)S(1)}, f32[240,128]{1,0:T(8,128)S(1)}, u32[]{:S(2)}, u32[]{:S(2)}) collective-permute-start(f32[240,128]{1,0:T(8,128)S(1)} %broadcast_select_fusion), channel_id=1, source_target_pairs={{0,8},{1,0},{2,10},{3,2},{4,5},{5,4},{6,7},{7,6},{8,9},{9,1},{10,1... | collective-permute-start | bytes 368648 | tf_op jit(solution)/shard_map/ppermute | solution.py:586
  9.0 5.0 %collective-permute-start.3 = (f32[240,128]{1,0:T(8,128)S(1)}, f32[240,128]{1,0:T(8,128)S(1)}, u32[]{:S(2)}, u32[]{:S(2)}) collective-permute-start(f32[240,128]{1,0:T(8,128)S(1)} %broadcast_select_fusion), channel_id=1, source_target_pairs={{0,4},{1,0},{2,6},{3,2},{4,5},{5,1},{6,7},{7,3},{8,9},{9,8},{10,11... | collective-permute-start | bytes 368648 | tf_op jit(solution)/shard_map/ppermute | solution.py:586
  9.0 5.1 %collective-permute-start.4 = (f32[208,128]{1,0:T(8,128)S(1)}, f32[208,128]{1,0:T(8,128)S(1)}, u32[]{:S(2)}, u32[]{:S(2)}) collective-permute-start(f32[208,128]{1,0:T(8,128)S(1)} %get-tuple-element.24), channel_id=1, source_target_pairs={{1,2},{2,1},{3,4},{4,3},{5,6},{6,5},{7,8},{8,7},{9,10},{10,9},{11,... | collective-permute-start | bytes 319496 | tf_op jit(solution)/shard_map/ppermute | solution.py:580
  9.7 7.6 %copy-start.3 = (f32[2]{0:T(128)S(1)}, f32[2]{0:T(128)}, u32[]{:S(2)}) copy-start(f32[2]{0:T(128)} %field_ref.5) | copy-start | bytes 28
  9.7 7.6 %copy-start.4 = (f32[2,128]{1,0:T(2,128)S(1)}, f32[2,128]{1,0:T(2,128)}, u32[]{:S(2)}) copy-start(f32[2,128]{1,0:T(2,128)} %profile_ref.1) | copy-start | bytes 3076
  14.1 3.1 %collective-permute-start.5 = (f32[448,128]{1,0:T(8,128)S(1)}, f32[448,128]{1,0:T(8,128)S(1)}, u32[]{:S(2)}, u32[]{:S(2)}) collective-permute-start(f32[448,128]{1,0:T(8,128)S(1)} %constant_dynamic-update-slice_fusion.sent_ref), channel_id=1, source_target_pairs={{0,1},{1,0},{2,3},{3,2},{4,5},{5,4},{6,7},{7,6},{8,9},{9,8},{10,11... | collective-permute-start | bytes 688136 | tf_op jit(solution)/shard_map/ppermute | solution.py:597
  24.5 5.5 %collective-permute-start.6 = (f32[8,128]{1,0:T(8,128)S(1)}, f32[8,128]{1,0:T(8,128)S(1)}, u32[]{:S(2)}, u32[]{:S(2)}) collective-permute-start(f32[8,128]{1,0:T(8,128)S(1)} %get-tuple-element.34.after_ref), channel_id=1, source_target_pairs={{0,1},{1,0},{2,3},{3,2},{4,5},{5,4},{6,7},{7,6},{8,9},{9,8},{10,11... | collective-permute-start | bytes 12296 | tf_op jit(solution)/shard_map/ppermute | solution.py:629
  24.6 5.5 %collective-permute-start.7 = (f32[8,128]{1,0:T(8,128)S(1)}, f32[8,128]{1,0:T(8,128)S(1)}, u32[]{:S(2)}, u32[]{:S(2)}) collective-permute-start(f32[8,128]{1,0:T(8,128)S(1)} %get-tuple-element.34.after_ref), channel_id=1, source_target_pairs={{0,2},{1,3},{2,0},{3,1},{4,6},{5,7},{6,4},{7,5},{8,10},{9,11},{10,... | collective-permute-start | bytes 12296 | tf_op jit(solution)/shard_map/ppermute | solution.py:629
  27.1 3.0 %collective-permute-start.8 = (f32[8,128]{1,0:T(8,128)S(1)}, f32[8,128]{1,0:T(8,128)S(1)}, u32[]{:S(2)}, u32[]{:S(2)}) collective-permute-start(f32[8,128]{1,0:T(8,128)S(1)} %get-tuple-element.34.after_ref), channel_id=1, source_target_pairs={{0,3},{1,2},{2,1},{3,0},{4,7},{5,6},{6,5},{7,4},{8,11},{9,10},{10,... | collective-permute-start | bytes 12296 | tf_op jit(solution)/shard_map/ppermute | solution.py:629
  30.1 8.8 %collective-permute-start.10 = (f32[8,128]{1,0:T(8,128)S(1)}, f32[8,128]{1,0:T(8,128)S(1)}, u32[]{:S(2)}, u32[]{:S(2)}) collective-permute-start(f32[8,128]{1,0:T(8,128)S(1)} %add_add_fusion.1.after_ref), channel_id=1, source_target_pairs={{0,8},{1,9},{2,10},{3,11},{4,12},{5,13},{6,14},{7,15},{8,0},{9,1},... | collective-permute-start | bytes 12296 | tf_op jit(solution)/shard_map/ppermute | solution.py:629
  32.8 6.1 %collective-permute-start.11 = (f32[8,128]{1,0:T(8,128)S(1)}, f32[8,128]{1,0:T(8,128)S(1)}, u32[]{:S(2)}, u32[]{:S(2)}) collective-permute-start(f32[8,128]{1,0:T(8,128)S(1)} %add_add_fusion.1.after_ref), channel_id=1, source_target_pairs={{0,12},{1,13},{2,14},{3,15},{4,8},{5,9},{6,10},{7,11},{8,4},{9,5},... | collective-permute-start | bytes 12296 | tf_op jit(solution)/shard_map/ppermute | solution.py:629
  34.1 4.9 %collective-permute-start.9 = (f32[8,128]{1,0:T(8,128)S(1)}, f32[8,128]{1,0:T(8,128)S(1)}, u32[]{:S(2)}, u32[]{:S(2)}) collective-permute-start(f32[8,128]{1,0:T(8,128)S(1)} %add_add_fusion.1.after_ref), channel_id=1, source_target_pairs={{0,4},{1,5},{2,6},{3,7},{4,0},{5,1},{6,2},{7,3},{8,12},{9,13},{10,... | collective-permute-start | bytes 12296 | tf_op jit(solution)/shard_map/ppermute | solution.py:629

commit v5 on v4

--- a/solution.py
+++ b/solution.py
@@ -199,12 +199,12 @@
     for part in parts:
         own, extra = OWN[part], EXTRA[part]
         weights = matrix_ref[0 if part in "ab" else 1]
-        total = None
-        for rows in (slice(0, channels), slice(channels, 2 * channels)):
-            left = jnp.concatenate([stack_ref[rows, own : own + 128], stack_ref[rows, extra : extra + 128]], axis=1)
-            got = jnp.dot(left, weights, preferred_element_type=F32)
-            total = got if total is None else total + got
-        moved_ref[PARTS.index(part)] = total
+        left = [
+            stack_ref[rows, at : at + 128]
+            for rows in (slice(0, channels), slice(channels, 2 * channels))
+            for at in (own, extra)
+        ]
+        moved_ref[PARTS.index(part)] = jnp.dot(jnp.concatenate(left, axis=1), weights, preferred_element_type=F32)
 
 
 def advance(targets, old, keep, mixed_ref, moved_ref, pot_ref, drive, scale, chunk=80):
@@ -344,7 +344,8 @@
             work_ref[which, at : at + 1, :] = high
             at = local + 64 * which + 32 + INNER + i
             work_ref[which, at : at + 1, :] = row - high
-    matrix_ref[...] = work_ref[...].astype(BF16)
+    matrix_ref[:, : 2 * local, :] = work_ref[...].astype(BF16)
+    matrix_ref[:, 2 * local :, :] = work_ref[...].astype(BF16)
     radii = lane_radii(first, local)
     drive = field_ref[0] * radii
     own_at = {OWN[part]: k for k, part in enumerate(PARTS)}
@@ -375,8 +376,9 @@
             stencil(stack, matrix_ref, moved_ref, pair)
             advance(pair, old, keep, mixed_ref, moved_ref, pot_ref, drive, scale)
         mix(coupling_ref, stack, mixed_ref, (1,))
+        if power == ORDER:
+            mix(coupling_ref, stack_ref, mixed_ref, (0,))
         advance(("ac", "bd"), old, keep, mixed_ref, moved_ref, pot_ref, drive, scale)
-    mix(coupling_ref, stack_ref, mixed_ref, (0,))
     part_ref[...] = jnp.zeros(part_ref.shape, F32)
     state = [state_ref[:, OWN[part] : OWN[part] + local] for part in "cd"]
     for n, value in ((0, part_in_ref[0:1, :]), (1, intersect(state[0], state[1], mixed_ref, radii))):
@@ -539,17 +541,17 @@
     width = 6 * local
     scaling = 1.0 / (math.sqrt(channels * grid_points) * (inner_radius + grid_points * spacing))
 
-    near, far, inner = pl.pallas_call(
+    near, far, inner, own = pl.pallas_call(
         pack_kernel,
         out_shape=(
             shape((half + 8, local), F32),
             shape((half + 8, local), F32),
             shape((half + 40, local), F32),
+            shape(states.shape, F32),
         ),
         in_specs=smem(1) + [pl.BlockSpec(memory_space=pltpu.HBM)] * 2,
-        out_specs=tuple(vmem(3)),
+        out_specs=tuple(vmem(4)),
         scratch_shapes=[
-            pltpu.VMEM(states.shape, F32),
             pltpu.VMEM(surface_profile.shape, F32),
             pltpu.SemaphoreType.DMA((5,)),
         ],
@@ -575,7 +577,7 @@
         out_specs=tuple(vmem(6)),
         compiler_params=params(),
         name="tables",
-    )(first, dipole, pattern, angular.reshape(1, channels), thresholds.reshape(1, channels), states)
+    )(first, dipole, pattern, angular.reshape(1, channels), thresholds.reshape(1, channels), own)
 
     far = lax.ppermute(far, axis, [(i, i + d) for i, d in swaps(1, count - 2)])
     have, far_waits = [0], True
@@ -605,7 +607,7 @@
     )
     stack, mixed, total, matrix, part = pl.pallas_call(
         functools.partial(first_kernel, scaling=scaling),
-        out_shape=evolved[1:] + (shape((2, 2 * local, 2 * local), BF16), shape((8, local), F32)),
+        out_shape=evolved[1:] + (shape((2, 4 * local, 2 * local), BF16), shape((8, local), F32)),
         in_specs=smem(2) + vmem(11),
         out_specs=tuple(vmem(5)),
         scratch_shapes=[
@@ -618,7 +620,7 @@
         input_output_aliases={11: 0, 12: 1},
         compiler_params=params(),
         name="first",
-    )(first, pulse_field, far, got, sent, surface_profile, states, coupling, kinetic, pot, part, stack, mixed)
+    )(first, pulse_field, far, got, sent, surface_profile, own, coupling, kinetic, pot, part, stack, mixed)
 
     bits = (count - 1).bit_length()
     groups = [range(low, min(low + 2, bits)) for low in range(0, bits, 2)]

time: 39.6 us -> 39.6 us (level)
  no operation moved by 1% of the time
where the time goes in v5:
time: 39.6 us; the launch traced here: 39.4 us
  Pallas kernels  18.1 us (46%)
  starting transfers between devices  12.9 us (33%)
  waiting for transfers between devices  6.91 us (17%)
  between operations  0.84 us (2%)
  local copies, waits for them, and re-layouts  0.56 us (1%)
    pallas_call x1, Pallas kernels, per_device(): pl.pallas_call(functools.partial(first_kernel, scaling=scaling), out_shap...  7.26 us
    ppermute x4, waiting for transfers between devices, per_device(): got = lax.ppermute(inner, axis, full_cycle(pairs, count))  6.76 us
    ppermute x6, starting transfers between devices, send(): lax.ppermute(value, axis, [(i, i ^ pattern << low) for i in range(count)])  6.56 us
    pallas_call x1, Pallas kernels, per_device(): pl.pallas_call(rest_kernel, out_shape=shape(states.shape, F32), in_specs=...  4.85 us
    ppermute x4, starting transfers between devices, per_device(): got = lax.ppermute(inner, axis, full_cycle(pairs, count))  4.04 us
    pallas_call x1, Pallas kernels, per_device(): pl.pallas_call(functools.partial(later_kernel, power=1), out_shape=evolve...  2.8 us
    pallas_call x1, Pallas kernels, per_device(): pl.pallas_call(pack_kernel, out_shape=(shape((half + 8, local), F32), sha...  1.75 us
    ppermute x1, starting transfers between devices, per_device(): got = lax.ppermute(sent, axis, [(i, i + d) for i, d in swaps(0, count)])  1.69 us
  transfers between devices with their start and end apart: 12, of which 5 were waited for; matrix products, arithmetic and copies ran while one was open for 0% of the time, Pallas kernels for 23%

profile of v5, /device:TPU:0, one launch (start us, length us, event | category | flops | bytes accessed | tf_op | source)
XLA Modules:
  0.0 39.4 jit_solution(14583890951393780553)
XLA Ops:
  0.7 1.8 %pack.1 = (f32[208,128]{1,0:T(8,128)S(1)}, f32[208,128]{1,0:T(8,128)S(1)}, f32[240,128]{1,0:T(8,128)S(1)}, f32[4,400,128]{2,1,0:T(8,128)S(1)}) custom-call(s32[1]{0:T(128)} %bitcast.first_ref, f32[4,400,128]{2,1,0:T(8,128)} %states_any.1, f32[2,128]{1,0:T(2,128)} %profile_ref.1), custom_call_target="tpu_custom_call" | custom-call | tf_op jit(solution)/shard_map/pack/pallas_call | solution.py:544
  2.4 3.0 %collective-permute-start = (f32[240,128]{1,0:T(8,128)S(1)}, f32[240,128]{1,0:T(8,128)S(1)}, u32[]{:S(2)}, u32[]{:S(2)}) collective-permute-start(f32[240,128]{1,0:T(8,128)S(1)} %get-tuple-element.24), channel_id=1, source_target_pairs={{0,2},{1,0},{2,3},{3,1},{4,5},{5,4},{6,7},{7,6},{8,9},{9,8},{10,11... | collective-permute-start | bytes 368648 | tf_op jit(solution)/shard_map/ppermute | solution.py:588
  5.5 2.4 %collective-permute-done = f32[240,128]{1,0:T(8,128)S(1)} collective-permute-done((f32[240,128]{1,0:T(8,128)S(1)}, f32[240,128]{1,0:T(8,128)S(1)}, u32[]{:S(2)}, u32[]{:S(2)}) %collective-permute-start) | collective-permute-done | bytes 122912 | tf_op jit(solution)/shard_map/ppermute | solution.py:588
  7.9 1.0 %collective-permute-start.1 = (f32[240,128]{1,0:T(8,128)S(1)}, f32[240,128]{1,0:T(8,128)S(1)}, u32[]{:S(2)}, u32[]{:S(2)}) collective-permute-start(f32[240,128]{1,0:T(8,128)S(1)} %broadcast_select_fusion), channel_id=1, source_target_pairs={{0,12},{1,0},{2,14},{3,2},{4,5},{5,4},{6,7},{7,6},{8,9},{9,8},{10,... | collective-permute-start | bytes 368648 | tf_op jit(solution)/shard_map/ppermute | solution.py:588
  8.9 0.7 %collective-permute-start.4 = (f32[208,128]{1,0:T(8,128)S(1)}, f32[208,128]{1,0:T(8,128)S(1)}, u32[]{:S(2)}, u32[]{:S(2)}) collective-permute-start(f32[208,128]{1,0:T(8,128)S(1)} %get-tuple-element.25), channel_id=1, source_target_pairs={{1,2},{2,1},{3,4},{4,3},{5,6},{6,5},{7,8},{8,7},{9,10},{10,9},{11,... | collective-permute-start | bytes 319496 | tf_op jit(solution)/shard_map/ppermute | solution.py:582
  9.6 0.0 copy-start.2
  9.6 0.0 copy-start.3
  9.6 1.7 %collective-permute-done.1 = f32[240,128]{1,0:T(8,128)S(1)} collective-permute-done((f32[240,128]{1,0:T(8,128)S(1)}, f32[240,128]{1,0:T(8,128)S(1)}, u32[]{:S(2)}, u32[]{:S(2)}) %collective-permute-start.1) | collective-permute-done | bytes 122912 | tf_op jit(solution)/shard_map/ppermute | solution.py:588
  11.4 1.3 %collective-permute-done.2 = f32[240,128]{1,0:T(8,128)S(1)} collective-permute-done((f32[240,128]{1,0:T(8,128)S(1)}, f32[240,128]{1,0:T(8,128)S(1)}, u32[]{:S(2)}, u32[]{:S(2)}) %collective-permute-start.2) | collective-permute-done | bytes 122912 | tf_op jit(solution)/shard_map/ppermute | solution.py:588
  12.7 1.3 %collective-permute-done.3 = f32[240,128]{1,0:T(8,128)S(1)} collective-permute-done((f32[240,128]{1,0:T(8,128)S(1)}, f32[240,128]{1,0:T(8,128)S(1)}, u32[]{:S(2)}, u32[]{:S(2)}) %collective-permute-start.3) | collective-permute-done | bytes 122912 | tf_op jit(solution)/shard_map/ppermute | solution.py:588
  14.0 1.7 %collective-permute-start.5 = (f32[448,128]{1,0:T(8,128)S(1)}, f32[448,128]{1,0:T(8,128)S(1)}, u32[]{:S(2)}, u32[]{:S(2)}) collective-permute-start(f32[448,128]{1,0:T(8,128)S(1)} %constant_dynamic-update-slice_fusion.sent_ref), channel_id=1, source_target_pairs={{0,1},{1,0},{2,3},{3,2},{4,5},{5,4},{6,7},{7,6},{8,9},{9,8},{10,11... | collective-permute-start | bytes 688136 | tf_op jit(solution)/shard_map/ppermute | solution.py:599
  15.8 1.4 %tables.1 = (bf16[400,1200]{1,0:T(8,128)(2,1)S(1)}, f32[2,256,256]{2,1,0:T(8,128)S(1)}, f32[400,256]{1,0:T(8,128)S(1)}, bf16[1200,768]{1,0:T(8,128)(2,1)S(1)}, f...) custom-call(s32[1]{0:T(128)} %bitcast.first_ref, f32[400,400]{1,0:T(8,128)S(1)} %copy-done, s32[25,25]{1,0:T(8,128)S(1)} %copy-done.1, ...), custom_call_target="tpu_custom_call" | custom-call | tf_op jit(solution)/shard_map/tables/pallas_call | solution.py:566
  17.2 7.3 %first.1 = (bf16[1200,768]{1,0:T(8,128)(2,1)S(1)}, f32[400,768]{1,0:T(8,128)S(1)}, f32[400,768]{1,0:T(8,128)S(1)}, bf16[2,512,256]{2,1,0:T(8,128)(2,1)S(1)}, f32[8,128]{1,0:T(8,128)S(1)}) custom-call(s32[1]{0:T(128)} %bitcast.first_ref, f32[2]{0:T(128)S(1)} %copy-done.2, ...), custom_call_target="tpu_custom_call", output_to_operand_aliasing={{0}: (11, {}), {1}: (12, {})} | custom-call | tf_op jit(solution)/shard_map/first/pallas_call | solution.py:608
  24.5 0.0 collective-permute-start.6
  24.5 2.5 %collective-permute-start.7 = (f32[8,128]{1,0:T(8,128)S(1)}, f32[8,128]{1,0:T(8,128)S(1)}, u32[]{:S(2)}, u32[]{:S(2)}) collective-permute-start(f32[8,128]{1,0:T(8,128)S(1)} %get-tuple-element.36.after_ref), channel_id=1, source_target_pairs={{0,2},{1,3},{2,0},{3,1},{4,6},{5,7},{6,4},{7,5},{8,10},{9,11},{10,... | collective-permute-start | bytes 12296 | tf_op jit(solution)/shard_map/ppermute | solution.py:631
  27.0 0.1 collective-permute-start.8
  27.1 2.8 %later.1 = (f32[400,768]{1,0:T(8,128)S(1)}, bf16[1200,768]{1,0:T(8,128)(2,1)S(1)}, f32[400,768]{1,0:T(8,128)S(1)}, f32[400,768]{1,0:T(8,128)S(1)}, f32[8,128]{1,0:T(8,128)S(1)}) custom-call(s32[1]{0:T(128)} %bitcast.first_ref, f32[2]{0:T(128)S(1)} %copy-done.2, f32[8,128]{1,0:T(8,128)S(1)} %get-tuple-element.36.after_ref, ...), custom_call_target="tpu_custom_call" | custom-call | tf_op jit(solution)/shard_map/later/pallas_call | solution.py:641
  29.9 0.0 collective-permute-done.6
  29.9 0.0 collective-permute-done.7
  29.9 0.1 collective-permute-done.8
  30.1 2.6 %collective-permute-start.10 = (f32[8,128]{1,0:T(8,128)S(1)}, f32[8,128]{1,0:T(8,128)S(1)}, u32[]{:S(2)}, u32[]{:S(2)}) collective-permute-start(f32[8,128]{1,0:T(8,128)S(1)} %add_add_fusion.1.after_ref), channel_id=1, source_target_pairs={{0,8},{1,9},{2,10},{3,11},{4,12},{5,13},{6,14},{7,15},{8,0},{9,1},... | collective-permute-start | bytes 12296 | tf_op jit(solution)/shard_map/ppermute | solution.py:631
  32.7 1.3 %collective-permute-start.11 = (f32[8,128]{1,0:T(8,128)S(1)}, f32[8,128]{1,0:T(8,128)S(1)}, u32[]{:S(2)}, u32[]{:S(2)}) collective-permute-start(f32[8,128]{1,0:T(8,128)S(1)} %add_add_fusion.1.after_ref), channel_id=1, source_target_pairs={{0,12},{1,13},{2,14},{3,15},{4,8},{5,9},{6,10},{7,11},{8,4},{9,5},... | collective-permute-start | bytes 12296 | tf_op jit(solution)/shard_map/ppermute | solution.py:631
  34.0 4.8 %rest.1 = f32[4,400,128]{2,1,0:T(8,128)} custom-call(s32[1]{0:T(128)} %bitcast.first_ref, f32[2]{0:T(128)S(1)} %copy-done.2, f32[8,128]{1,0:T(8,128)S(1)} %add_add_fusion.1.after_ref, bf16[2,512,256]{2,1,0:T(8,128)(2,1)S(1)} %get-tuple-element.37.matrix_ref, bf16[400,1200]{1,0:T(8,128)(2,1)S(1)} %get-tuple-element.30.coupling_ref, ...), custom_call_target="tpu_custom_call" | custom-call | tf_op jit(solution)/shard_map/rest/pallas_call | solution.py:654
  38.9 0.5 %slice_bitcast_fusion = f32[2]{0:T(128)} fusion(f32[8,128]{1,0:T(8,128)S(1)} %add_add_fusion), kind=kLoop, calls=%fused_computation.6 | loop fusion | bytes 16 | tf_op jit(solution)/shard_map/squeeze | solution.py:673
  (24 shorter events, 0.1 us)
Async XLA Ops:
  0.6 15.1 %copy-start.4 = (s32[400]{0:T(512)S(1)}, s32[400]{0:T(512)}, u32[]{:S(2)}) copy-start(s32[400]{0:T(512)} %param.10) | copy-start | bytes 4804
  0.6 15.1 %copy-start.5 = (f32[400]{0:T(512)S(1)}, f32[400]{0:T(512)}, u32[]{:S(2)}) copy-start(f32[400]{0:T(512)} %param.11) | copy-start | bytes 4804
  0.7 15.1 %copy-start = (f32[400,400]{1,0:T(8,128)S(1)}, f32[400,400]{1,0:T(8,128)}, u32[]{:S(2)}) copy-start(f32[400,400]{1,0:T(8,128)} %dipole_ref.1) | copy-start | bytes 1920004
  0.7 15.1 %copy-start.1 = (s32[25,25]{1,0:T(8,128)S(1)}, s32[25,25]{1,0:T(8,128)}, u32[]{:S(2)}) copy-start(s32[25,25]{1,0:T(8,128)} %pattern_ref.1) | copy-start | bytes 7504
  2.4 5.5 %collective-permute-start = (f32[240,128]{1,0:T(8,128)S(1)}, f32[240,128]{1,0:T(8,128)S(1)}, u32[]{:S(2)}, u32[]{:S(2)}) collective-permute-start(f32[240,128]{1,0:T(8,128)S(1)} %get-tuple-element.24), channel_id=1, source_target_pairs={{0,2},{1,0},{2,3},{3,1},{4,5},{5,4},{6,7},{7,6},{8,9},{9,8},{10,11... | collective-permute-start | bytes 368648 | tf_op jit(solution)/shard_map/ppermute | solution.py:588
  7.9 3.4 %collective-permute-start.1 = (f32[240,128]{1,0:T(8,128)S(1)}, f32[240,128]{1,0:T(8,128)S(1)}, u32[]{:S(2)}, u32[]{:S(2)}) collective-permute-start(f32[240,128]{1,0:T(8,128)S(1)} %broadcast_select_fusion), channel_id=1, source_target_pairs={{0,12},{1,0},{2,14},{3,2},{4,5},{5,4},{6,7},{7,6},{8,9},{9,8},{10,... | collective-permute-start | bytes 368648 | tf_op jit(solution)/shard_map/ppermute | solution.py:588
  8.9 3.7 %collective-permute-start.2 = (f32[240,128]{1,0:T(8,128)S(1)}, f32[240,128]{1,0:T(8,128)S(1)}, u32[]{:S(2)}, u32[]{:S(2)}) collective-permute-start(f32[240,128]{1,0:T(8,128)S(1)} %broadcast_select_fusion), channel_id=1, source_target_pairs={{0,8},{1,0},{2,10},{3,2},{4,5},{5,4},{6,7},{7,6},{8,9},{9,1},{10,1... | collective-permute-start | bytes 368648 | tf_op jit(solution)/shard_map/ppermute | solution.py:588
  8.9 5.0 %collective-permute-start.3 = (f32[240,128]{1,0:T(8,128)S(1)}, f32[240,128]{1,0:T(8,128)S(1)}, u32[]{:S(2)}, u32[]{:S(2)}) collective-permute-start(f32[240,128]{1,0:T(8,128)S(1)} %broadcast_select_fusion), channel_id=1, source_target_pairs={{0,4},{1,0},{2,6},{3,2},{4,5},{5,1},{6,7},{7,3},{8,9},{9,8},{10,11... | collective-permute-start | bytes 368648 | tf_op jit(solution)/shard_map/ppermute | solution.py:588
  8.9 5.1 %collective-permute-start.4 = (f32[208,128]{1,0:T(8,128)S(1)}, f32[208,128]{1,0:T(8,128)S(1)}, u32[]{:S(2)}, u32[]{:S(2)}) collective-permute-start(f32[208,128]{1,0:T(8,128)S(1)} %get-tuple-element.25), channel_id=1, source_target_pairs={{1,2},{2,1},{3,4},{4,3},{5,6},{6,5},{7,8},{8,7},{9,10},{10,9},{11,... | collective-permute-start | bytes 319496 | tf_op jit(solution)/shard_map/ppermute | solution.py:582
  9.6 7.6 %copy-start.2 = (f32[2]{0:T(128)S(1)}, f32[2]{0:T(128)}, u32[]{:S(2)}) copy-start(f32[2]{0:T(128)} %field_ref.5) | copy-start | bytes 28
  9.6 7.6 %copy-start.3 = (f32[2,128]{1,0:T(2,128)S(1)}, f32[2,128]{1,0:T(2,128)}, u32[]{:S(2)}) copy-start(f32[2,128]{1,0:T(2,128)} %profile_ref.1) | copy-start | bytes 3076
  14.0 3.1 %collective-permute-start.5 = (f32[448,128]{1,0:T(8,128)S(1)}, f32[448,128]{1,0:T(8,128)S(1)}, u32[]{:S(2)}, u32[]{:S(2)}) collective-permute-start(f32[448,128]{1,0:T(8,128)S(1)} %constant_dynamic-update-slice_fusion.sent_ref), channel_id=1, source_target_pairs={{0,1},{1,0},{2,3},{3,2},{4,5},{5,4},{6,7},{7,6},{8,9},{9,8},{10,11... | collective-permute-start | bytes 688136 | tf_op jit(solution)/shard_map/ppermute | solution.py:599
  24.5 5.5 %collective-permute-start.6 = (f32[8,128]{1,0:T(8,128)S(1)}, f32[8,128]{1,0:T(8,128)S(1)}, u32[]{:S(2)}, u32[]{:S(2)}) collective-permute-start(f32[8,128]{1,0:T(8,128)S(1)} %get-tuple-element.36.after_ref), channel_id=1, source_target_pairs={{0,1},{1,0},{2,3},{3,2},{4,5},{5,4},{6,7},{7,6},{8,9},{9,8},{10,11... | collective-permute-start | bytes 12296 | tf_op jit(solution)/shard_map/ppermute | solution.py:631
  24.5 5.4 %collective-permute-start.7 = (f32[8,128]{1,0:T(8,128)S(1)}, f32[8,128]{1,0:T(8,128)S(1)}, u32[]{:S(2)}, u32[]{:S(2)}) collective-permute-start(f32[8,128]{1,0:T(8,128)S(1)} %get-tuple-element.36.after_ref), channel_id=1, source_target_pairs={{0,2},{1,3},{2,0},{3,1},{4,6},{5,7},{6,4},{7,5},{8,10},{9,11},{10,... | collective-permute-start | bytes 12296 | tf_op jit(solution)/shard_map/ppermute | solution.py:631
  27.0 3.0 %collective-permute-start.8 = (f32[8,128]{1,0:T(8,128)S(1)}, f32[8,128]{1,0:T(8,128)S(1)}, u32[]{:S(2)}, u32[]{:S(2)}) collective-permute-start(f32[8,128]{1,0:T(8,128)S(1)} %get-tuple-element.36.after_ref), channel_id=1, source_target_pairs={{0,3},{1,2},{2,1},{3,0},{4,7},{5,6},{6,5},{7,4},{8,11},{9,10},{10,... | collective-permute-start | bytes 12296 | tf_op jit(solution)/shard_map/ppermute | solution.py:631
  30.1 8.8 %collective-permute-start.10 = (f32[8,128]{1,0:T(8,128)S(1)}, f32[8,128]{1,0:T(8,128)S(1)}, u32[]{:S(2)}, u32[]{:S(2)}) collective-permute-start(f32[8,128]{1,0:T(8,128)S(1)} %add_add_fusion.1.after_ref), channel_id=1, source_target_pairs={{0,8},{1,9},{2,10},{3,11},{4,12},{5,13},{6,14},{7,15},{8,0},{9,1},... | collective-permute-start | bytes 12296 | tf_op jit(solution)/shard_map/ppermute | solution.py:631
  32.7 6.2 %collective-permute-start.11 = (f32[8,128]{1,0:T(8,128)S(1)}, f32[8,128]{1,0:T(8,128)S(1)}, u32[]{:S(2)}, u32[]{:S(2)}) collective-permute-start(f32[8,128]{1,0:T(8,128)S(1)} %add_add_fusion.1.after_ref), channel_id=1, source_target_pairs={{0,12},{1,13},{2,14},{3,15},{4,8},{5,9},{6,10},{7,11},{8,4},{9,5},... | collective-permute-start | bytes 12296 | tf_op jit(solution)/shard_map/ppermute | solution.py:631
  34.0 4.9 %collective-permute-start.9 = (f32[8,128]{1,0:T(8,128)S(1)}, f32[8,128]{1,0:T(8,128)S(1)}, u32[]{:S(2)}, u32[]{:S(2)}) collective-permute-start(f32[8,128]{1,0:T(8,128)S(1)} %add_add_fusion.1.after_ref), channel_id=1, source_target_pairs={{0,4},{1,5},{2,6},{3,7},{4,0},{5,1},{6,2},{7,3},{8,12},{9,13},{10,... | collective-permute-start | bytes 12296 | tf_op jit(solution)/shard_map/ppermute | solution.py:631
